TPU v7x, 256 devices: a whole 4x4x8 slice. The times are simulated.
256 devices in a mesh: lat: 64 (over x, y_lo, z), coh: 4 (over y_hi, core).
Axes of the slice: x: 4, y: 4 (y_hi: 2, y_lo: 2; y = y_hi * 2 + y_lo), z: 8, core: 2. Of those that a mesh axis runs over, the one named last changes fastest.
Arguments:
- density: float32 [128, 2, 512, 1024], P('coh', None, 'lat'), may hold values from 0.1 to 1
- cotangent: float32 [128, 2, 512, 1024], P('coh', None, 'lat'), may hold values from -0.5 to 1.5
- land_mask: int32 [2, 512, 1024], P(None, 'lat'), may hold values 0 or 1
- east_vel: float32 [2, 512, 1024], P(None, 'lat'), may hold values from -0.4 to 0.4
- north_vel: float32 [2, 512, 1024], P(None, 'lat'), may hold values from -0.4 to 0.4
- diffusion: float32 [2, 512, 1024], P(None, 'lat'), may hold values from 0.02 to 0.2
- age_class: int32 [128], P('coh'), may hold values from 0 to 31, as said below
- mort_rate: float32 [32], replicated, may hold values from 0.05 to 0.5
- crowd_coef: float32 [32], replicated, may hold values from 1 to 4
- mass: float32 [32], replicated, may hold values from 0.5 to 2
- speed: float32 [32], replicated, may hold values from 0.25 to 1
Outputs:
- grad_density: float32 [128, 2, 512, 1024], P('coh', None, 'lat')
- grad_east_vel: float32 [2, 512, 1024], P(None, 'lat', 'coh')
- grad_north_vel: float32 [2, 512, 1024], P(None, 'lat', 'coh')
- grad_diffusion: float32 [2, 512, 1024], P(None, 'lat', 'coh')
Inputs may be any that keep to these rules, and one draw needn't show every extreme that they name: `age_class`: each age class is held by exactly 4 cohorts.
All inputs are finite; a program needn't handle non-finite values. No bound on the sum of `land_mask` on one device may be relied on, other than what follows from the above.
Results may differ from a plain program's by a relative error of at most 0.00014.
Values sent between devices are 32-bit elements; how exact they have to be, the bound alone decides.
No kernel may reach another device: no remote copies, remote signals or barrier semaphores. Data moves between devices by JAX's collectives and lax.ppermute only.
A program may use at most 128 MiB of HBM per device.

v0:
```python
import jax
import jax.numpy as jnp
from jax import lax
from jax.sharding import PartitionSpec as P

COH = 128
STEPS = 2


def extended(value, sides, width):
    for axis, dim in sides:
        devices, length = (lax.axis_size(axis), value.shape[dim])
        up = [(i, (i + 1) % devices) for i in range(devices - 1)]
        down = [(j, i) for i, j in up]
        last = lax.slice_in_dim(value, length - width, length, axis=dim)
        first = lax.slice_in_dim(value, 0, width, axis=dim)
        before = lax.ppermute(last, axis, up)
        after = lax.ppermute(first, axis, down)
        value = jnp.concatenate([before, value, after], axis=dim)
    return value


def lookup(age_class, mort_rate, crowd_coef, mass, speed):
    classes = jnp.arange(mort_rate.shape[0], dtype=jnp.int32)
    onehot = (age_class[:, None] == classes[None, :]).astype(jnp.float32)
    tables = jnp.stack([mort_rate, crowd_coef, mass, speed], axis=1)
    picked = jnp.dot(onehot, tables, precision=lax.Precision.HIGHEST)
    return [picked[:, column][:, None, None, None] for column in range(4)]


def local(
    density,
    cotangent,
    land_mask,
    east_vel,
    north_vel,
    diffusion,
    age_class,
    mort_rate,
    crowd_coef,
    mass,
    speed,
):
    ocean = land_mask.astype(jnp.float32)[None]
    mortal, crowding, weight, swim = lookup(age_class, mort_rate, crowd_coef, mass, speed)
    east_coef = swim * east_vel[None]
    north_coef = swim * north_vel[None]
    kappa = diffusion[None]
    state = density
    saved = []
    for section in range(STEPS):
        crowd = lax.psum(jnp.sum(weight * state, axis=0), "coh") / COH
        survival = jnp.exp(-(mortal + crowding * crowd[None]))
        survived = state * survival
        wet = ocean * survived
        padded = extended(wet, (("lat", 2),), 1)
        north_val = padded[:, :, 2:]
        south_val = padded[:, :, :-2]
        east_val = jnp.roll(wet, -1, axis=3)
        west_val = jnp.roll(wet, 1, axis=3)
        laplace = north_val + south_val + east_val + west_val - 4.0 * wet
        east_diff = 0.5 * (east_val - west_val)
        north_diff = 0.5 * (north_val - south_val)
        state = ocean * (wet + kappa * laplace - east_coef * east_diff - north_coef * north_diff)
        saved.append((survival, survived, laplace, east_diff, north_diff))
    adjoint = cotangent
    shares = None
    for section in reversed(range(STEPS)):
        survival, survived, laplace, east_diff, north_diff = saved[section]
        masked = ocean * adjoint
        grad_east = -jnp.sum(masked * swim * east_diff, axis=0)
        grad_north = -jnp.sum(masked * swim * north_diff, axis=0)
        grad_kappa = jnp.sum(masked * laplace, axis=0)
        pieces = (
            lax.psum_scatter(grad_east, "coh", scatter_dimension=2, tiled=True),
            lax.psum_scatter(grad_north, "coh", scatter_dimension=2, tiled=True),
            lax.psum_scatter(grad_kappa, "coh", scatter_dimension=2, tiled=True),
        )
        shares = pieces if shares is None else jax.tree.map(jnp.add, shares, pieces)
        to_north = (kappa - 0.5 * north_coef) * masked
        to_south = (kappa + 0.5 * north_coef) * masked
        to_east = (kappa - 0.5 * east_coef) * masked
        to_west = (kappa + 0.5 * east_coef) * masked
        stacked = extended(jnp.stack([to_north, to_south]), (("lat", 3),), 1)
        from_below = stacked[0][:, :, :-2]
        from_above = stacked[1][:, :, 2:]
        grad_wet = (
            (1.0 - 4.0 * kappa) * masked
            + jnp.roll(to_east, 1, axis=3)
            + jnp.roll(to_west, -1, axis=3)
            + from_below
            + from_above
        )
        grad_surv = ocean * grad_wet
        pressure = lax.psum(jnp.sum(-crowding * grad_surv * survived, axis=0), "coh")
        adjoint = grad_surv * survival + weight / COH * pressure[None]
    return (adjoint, shares[0], shares[1], shares[2])


def solution(mesh):
    in_specs = (
        P("coh", None, "lat", None),
        P("coh", None, "lat", None),
        P(None, "lat", None),
        P(None, "lat", None),
        P(None, "lat", None),
        P(None, "lat", None),
        P("coh"),
        P(),
        P(),
        P(),
        P(),
    )
    out_specs = (
        P("coh", None, "lat", None),
        P(None, "lat", "coh"),
        P(None, "lat", "coh"),
        P(None, "lat", "coh"),
    )
    return jax.shard_map(local, mesh=mesh, in_specs=in_specs, out_specs=out_specs, check_vma=False)
```

profile of v0, /device:TPU:6, one launch (start us, length us, event | category | flops | bytes accessed | tf_op | source)
XLA Modules:
  0.0 387.9 jit_solution(14787665174152883794)
XLA Ops:
  7.2 0.9 fusion.27
  8.1 3.5 multiply_reduce_fusion.9
  11.7 48.0 %all-reduce.5.cloned.1.call-done = f32[2,8,1024]{2,1,0:T(8,128)} async-done(((f32[2,8,1024]{2,1,0:T(8,128)}), f32[2,8,1024]{2,1,0:T(8,128)}) %all-reduce.5.cloned.1.call-update) | async-done | bytes 65552 | tf_op jit(solution)/shard_map/psum | solution.py:52
  59.8 0.8 broadcast_multiply_fusion.1
  60.6 3.0 fusion.26
  63.6 3.5 collective-permute-start.3
  67.1 5.5 %collective-permute-start.2 = (f32[32,2,1,1024]{3,0,2,1:T(8,128)S(1)}, f32[32,2,1,1024]{3,0,2,1:T(8,128)S(1)}, u32[]{:S(2)}, u32[]{:S(2)}) collective-permute-start(f32[32,2,1,1024]{3,0,2,1:T(8,128)S(1)} %get-tuple-element.48), channel_id=1, source_target_pairs={{4,0},{8,4},{12,8},{16,12},{20,16},{24,20},{28,24},{32,28},{36,32}... | collective-permute-start | bytes 786440 | tf_op jit(solution)/shard_map/ppermute | solution.py:18
  72.7 0.7 fusion.45
  73.6 3.5 collective-permute-done.3
  77.1 1.3 collective-permute-done.2
  78.5 5.9 %fusion.9 = (f32[32,2,8,1024]{3,0,2,1:T(8,128)}, f32[32,2,8,1024]{3,0,2,1:T(8,128)}, f32[1,32,2,8,1024]{4,1,3,2,0:T(8,128)S(1)}, f32[1,32,2,8,1024]{4,1,3,2,0:T(...) fusion(f32[2,8,1024]{2,1,0:T(8,128)S(1)} %copy-done.22, f32[32]{0:T(128)S(1)} %get-tuple-element.58, ...), kind=kLoop, calls=%fused_computation.15 | loop fusion | flops 18333696 | bytes 19726592 | tf_op jit(solution)/shard_map/mul | solution.py:82
  84.4 1.2 pad_maximum_fusion.13
  86.1 0.7 copy-done.4
  86.8 7.4 %collective-permute-start.1 = (f32[2,32,2,1,1024]{4,1,3,2,0:T(8,128)}, f32[2,32,2,1,1024]{4,1,3,2,0:T(8,128)}, u32[]{:S(2)}, u32[]{:S(2)}) collective-permute-start(f32[2,32,2,1,1024]{4,1,3,2,0:T(8,128)} %get-tuple-element.28), channel_id=1, source_target_pairs={{4,0},{8,4},{12,8},{16,12},{20,16},{24,20},{28,24},{32,28},{36,32}... | collective-permute-start | bytes 1572872 | tf_op jit(solution)/shard_map/ppermute | solution.py:18
  94.2 1.9 collective-permute-start
  97.4 1.0 slice.171
  98.3 3.5 slice.170
  101.9 1.8 slice.168
  103.7 36.2 %all-reduce.7.cloned.1.call-done = f32[2,8,1024]{2,1,0:T(8,128)} async-done(((f32[2,8,1024]{2,1,0:T(8,128)}), f32[2,8,1024]{2,1,0:T(8,128)}) %all-reduce.7.cloned.1.call-update) | async-done | bytes 65552 | tf_op jit(solution)/shard_map/psum | solution.py:52
  139.8 0.8 broadcast_multiply_fusion
  140.7 3.1 pad_maximum_fusion
  143.9 0.8 slice_bitcast_fusion.3
  144.7 0.7 copy-done.8
  147.3 4.5 %multiply_reduce_fusion.7 = (f32[2,8,1024]{2,1,0:T(8,128)}, f32[32,2,8,1024]{3,0,2,1:T(8,128)}, f32[32,2,8,1024]{3,0,2,1:T(8,128)S(1)}) fusion(f32[32,2,8,1024]{3,0,2,1:T(8,128)S(1)} %copy-done.13, f32[32]{0:T(128)S(1)} %get-tuple-element.57, f32[2,8,1024]{2,1,0:T(8,128)S(1)} %broadcast_multiply_fusion, f32[32]{0:T(128)S(1)} %get-tuple-element.60, ...), kind=kLoop, calls=%fused_computation.57 | loop fusion | flops 8896512 | bytes 17039744 | tf_op jit(solution)/shard_map/reduce_sum | solution.py:95
  151.8 2.9 fusion.42
  154.7 0.9 fusion.43
  155.7 1.9 fusion.41
  157.5 5.5 %collective-permute-start.6 = (f32[32,2,1,1024]{3,0,2,1:T(8,128)}, f32[32,2,1,1024]{3,0,2,1:T(8,128)}, u32[]{:S(2)}, u32[]{:S(2)}) collective-permute-start(f32[32,2,1,1024]{3,0,2,1:T(8,128)} %get-tuple-element.43), channel_id=1, source_target_pairs={{4,0},{8,4},{12,8},{16,12},{20,16},{24,20},{28,24},{32,28},{36,32}... | collective-permute-start | bytes 786440 | tf_op jit(solution)/shard_map/ppermute | solution.py:18
  163.1 2.1 collective-permute-start.7
  165.2 35.1 %all-reduce.9.cloned.1.call-done = f32[2,8,1024]{2,1,0:T(8,128)} async-done(((f32[2,8,1024]{2,1,0:T(8,128)}), f32[2,8,1024]{2,1,0:T(8,128)}) %all-reduce.9.cloned.1.call-update) | async-done | bytes 65552 | tf_op jit(solution)/shard_map/psum | solution.py:95
  200.3 5.3 %multiply_reduce_fusion = (f32[2,8,1024]{2,1,0:T(8,128)}, f32[2,8,1024]{2,1,0:T(8,128)}, f32[2,8,1024]{2,1,0:T(8,128)}, f32[32,2,8,1024]{3,0,2,1:T(8,128)S(1)}) fusion(f32[32,2,8,1024]{3,0,2,1:T(8,128)S(1)} %fusion.26, f32[32,2,8,1023]{3,0,2,1:T(8,128)} %copy-done.6, f32[32,2,8,1]{3,0,2,1:T(8,128)S(1)} %get-tuple-element.53, ...), kind=kLoop, calls=%fused_computation.48 | loop fusion | flops 14106624 | bytes 11403776 | tf_op jit(solution)/shard_map/reduce_sum | solution.py:73
  205.6 1.2 fusion.8
  207.6 5.8 %collective-permute-start.5 = (f32[2,32,2,1,1024]{4,1,3,2,0:T(8,128)S(1)}, f32[2,32,2,1,1024]{4,1,3,2,0:T(8,128)S(1)}, u32[]{:S(2)}, u32[]{:S(2)}) collective-permute-start(f32[2,32,2,1,1024]{4,1,3,2,0:T(8,128)S(1)} %get-tuple-element.26), channel_id=1, source_target_pairs={{4,0},{8,4},{12,8},{16,12},{20,16},{24,20},{28,24},{32,28},{36,32}... | collective-permute-start | bytes 1572872 | tf_op jit(solution)/shard_map/ppermute | solution.py:18
  213.4 1.9 collective-permute-start.4
  215.5 4.7 %multiply_reduce_fusion.1 = (f32[2,8,1024]{2,1,0:T(8,128)}, f32[2,8,1024]{2,1,0:T(8,128)}, f32[2,8,1024]{2,1,0:T(8,128)}) fusion(f32[32,2,8,1024]{3,0,2,1:T(8,128)S(1)} %copy-done.1, f32[32,2,8,1023]{3,0,2,1:T(8,128)S(1)} %copy-done.12, f32[32,2,8,1]{3,0,2,1:T(8,128)S(1)} %copy-done.16, f32[32,2,8,1]{3,0,2,1:T(8,128)S(1)} %get-tuple-element.46, ...), kind=kLoop, calls=%fused_computation.49 | loop fusion | flops 10960896 | bytes 9175168 | tf_op jit(solution)/shard_map/reduce_sum | solution.py:73
  220.2 4.8 %collective-permute-done.5 = f32[2,32,2,1,1024]{4,1,3,2,0:T(8,128)S(1)} collective-permute-done((f32[2,32,2,1,1024]{4,1,3,2,0:T(8,128)S(1)}, f32[2,32,2,1,1024]{4,1,3,2,0:T(8,128)S(1)}, u32[]{:S(2)}, u32[]{:S(2)}) %collective-permute-start.5) | collective-permute-done | bytes 524320 | tf_op jit(solution)/shard_map/ppermute | solution.py:18
  225.1 7.1 %collective-permute-done.4 = f32[2,32,2,1,1024]{4,1,3,2,0:T(8,128)S(1)} collective-permute-done((f32[2,32,2,1,1024]{4,1,3,2,0:T(8,128)S(1)}, f32[2,32,2,1,1024]{4,1,3,2,0:T(8,128)S(1)}, u32[]{:S(2)}, u32[]{:S(2)}) %collective-permute-start.4) | collective-permute-done | bytes 524320 | tf_op jit(solution)/shard_map/ppermute | solution.py:17
  232.2 0.8 pad_maximum_fusion.1
  233.0 0.8 slice_bitcast_fusion.1
  233.9 0.7 copy-done.2
  234.7 3.6 multiply_reduce_fusion.6
  239.0 0.6 negate_add_fusion
  240.5 37.8 %all-reduce.11.cloned.1.call-done = f32[2,8,1024]{2,1,0:T(8,128)} async-done(((f32[2,8,1024]{2,1,0:T(8,128)}), f32[2,8,1024]{2,1,0:T(8,128)}) %all-reduce.11.cloned.1.call-update) | async-done | bytes 65552 | tf_op jit(solution)/shard_map/psum | solution.py:95
  278.3 1.4 multiply_add_fusion
  279.7 2.5 copy.18
  282.2 30.3 %reduce-scatter.4.cloned.1.call-done = f32[2,8,256]{2,1,0:T(8,128)} async-done(((f32[2,8,1024]{2,1,0:T(8,128)}), f32[2,8,256]{2,1,0:T(8,128)}) %reduce-scatter.4.cloned.1.call-update) | async-done | bytes 16400 | tf_op jit(solution)/shard_map/reduce_scatter | solution.py:75
  312.5 34.2 %reduce-scatter.6.cloned.1.call-done = f32[2,8,256]{2,1,0:T(8,128)} async-done(((f32[2,8,1024]{2,1,0:T(8,128)}), f32[2,8,256]{2,1,0:T(8,128)}) %reduce-scatter.6.cloned.1.call-update) | async-done | bytes 16400 | tf_op jit(solution)/shard_map/reduce_scatter | solution.py:76
  346.7 34.3 %reduce-scatter.8.cloned.1.call-done = f32[2,8,256]{2,1,0:T(8,128)} async-done(((f32[2,8,1024]{2,1,0:T(8,128)}), f32[2,8,256]{2,1,0:T(8,128)}) %reduce-scatter.8.cloned.1.call-update) | async-done | bytes 16400 | tf_op jit(solution)/shard_map/reduce_scatter | solution.py:77
  (95 shorter events, 6.4 us)
Async XLA Ops:
  7.2 4.5 %copy-start.32 = (s32[2,8,1024]{2,1,0:T(8,128)S(1)}, s32[2,8,1024]{2,1,0:T(8,128)}, u32[]{:S(2)}) copy-start(s32[2,8,1024]{2,1,0:T(8,128)} %param.13) | copy-start | bytes 196612
  7.2 52.6 %all-reduce.5.cloned.1.call-start = ((), (), s32[]{:S(2)}) async-start(), calls=%async_computation.3 | async-start | bytes 131072 | tf_op jit(solution)/shard_map/psum | solution.py:52
  11.6 128.2 %all-reduce.7.cloned.1.call-start = ((), (), s32[]{:S(2)}) async-start(), calls=%async_computation.4 | async-start | bytes 131072 | tf_op jit(solution)/shard_map/psum | solution.py:52
  63.6 13.5 %collective-permute-start.3 = (f32[32,2,1,1024]{3,0,2,1:T(8,128)S(1)}, f32[32,2,1,1024]{3,0,2,1:T(8,128)S(1)}, u32[]{:S(2)}, u32[]{:S(2)}) collective-permute-start(f32[32,2,1,1024]{3,0,2,1:T(8,128)S(1)} %get-tuple-element.49), channel_id=1, source_target_pairs={{0,4},{4,8},{8,12},{12,16},{16,20},{20,24},{24,28},{28,32},{32,36}... | collective-permute-start | bytes 786440 | tf_op jit(solution)/shard_map/ppermute | solution.py:17
  67.1 11.4 %copy-start.17 = (f32[2,8,1024]{2,1,0:T(8,128)S(1)}, f32[2,8,1024]{2,1,0:T(8,128)}, u32[]{:S(2)}) copy-start(f32[2,8,1024]{2,1,0:T(8,128)} %param.16) | copy-start | bytes 196612
  67.1 11.4 %copy-start.22 = (f32[2,8,1024]{2,1,0:T(8,128)S(1)}, f32[2,8,1024]{2,1,0:T(8,128)}, u32[]{:S(2)}) copy-start(f32[2,8,1024]{2,1,0:T(8,128)} %param.14) | copy-start | bytes 196612
  67.1 11.4 %copy-start.24 = (f32[2,8,1024]{2,1,0:T(8,128)S(1)}, f32[2,8,1024]{2,1,0:T(8,128)}, u32[]{:S(2)}) copy-start(f32[2,8,1024]{2,1,0:T(8,128)} %param.15) | copy-start | bytes 196612
  67.1 11.3 %collective-permute-start.2 = (f32[32,2,1,1024]{3,0,2,1:T(8,128)S(1)}, f32[32,2,1,1024]{3,0,2,1:T(8,128)S(1)}, u32[]{:S(2)}, u32[]{:S(2)}) collective-permute-start(f32[32,2,1,1024]{3,0,2,1:T(8,128)S(1)} %get-tuple-element.48), channel_id=1, source_target_pairs={{4,0},{8,4},{12,8},{16,12},{20,16},{24,20},{28,24},{32,28},{36,32}... | collective-permute-start | bytes 786440 | tf_op jit(solution)/shard_map/ppermute | solution.py:18
  72.6 5.8 %copy-start.7 = (f32[32,2,8,1024]{3,2,1,0:T(8,128)S(1)}, f32[32,2,8,1024]{3,2,1,0:T(8,128)}, u32[]{:S(2)}) copy-start(f32[32,2,8,1024]{3,2,1,0:T(8,128)} %param.12) | copy-start | bytes 6291460
  73.4 11.0 %copy-start.5 = (f32[32,2,8,1023]{3,0,2,1:T(8,128)}, f32[32,2,8,1023]{3,0,2,1:T(8,128)S(1)}, u32[]{:S(2)}) copy-start(f32[32,2,8,1023]{3,0,2,1:T(8,128)S(1)} %get-tuple-element.50) | copy-start | bytes 6285316
  73.4 11.0 %copy-start.6 = (f32[32,2,8,1023]{3,0,2,1:T(8,128)}, f32[32,2,8,1023]{3,0,2,1:T(8,128)S(1)}, u32[]{:S(2)}) copy-start(f32[32,2,8,1023]{3,0,2,1:T(8,128)S(1)} %get-tuple-element.51) | copy-start | bytes 6285316
  84.4 1.7 copy-start.3
  84.4 2.4 copy-start.4
  86.8 53.9 %collective-permute-start.1 = (f32[2,32,2,1,1024]{4,1,3,2,0:T(8,128)}, f32[2,32,2,1,1024]{4,1,3,2,0:T(8,128)}, u32[]{:S(2)}, u32[]{:S(2)}) collective-permute-start(f32[2,32,2,1,1024]{4,1,3,2,0:T(8,128)} %get-tuple-element.28), channel_id=1, source_target_pairs={{4,0},{8,4},{12,8},{16,12},{20,16},{24,20},{28,24},{32,28},{36,32}... | collective-permute-start | bytes 1572872 | tf_op jit(solution)/shard_map/ppermute | solution.py:18
  94.2 46.5 %collective-permute-start = (f32[2,32,2,1,1024]{4,1,3,2,0:T(8,128)}, f32[2,32,2,1,1024]{4,1,3,2,0:T(8,128)}, u32[]{:S(2)}, u32[]{:S(2)}) collective-permute-start(f32[2,32,2,1,1024]{4,1,3,2,0:T(8,128)} %get-tuple-element.27), channel_id=1, source_target_pairs={{0,4},{4,8},{8,12},{12,16},{16,20},{20,24},{24,28},{28,32},{32,36}... | collective-permute-start | bytes 1572872 | tf_op jit(solution)/shard_map/ppermute | solution.py:17
  96.8 103.5 %all-reduce.9.cloned.1.call-start = ((), (), s32[]{:S(2)}) async-start(), calls=%async_computation.5 | async-start | bytes 131072 | tf_op jit(solution)/shard_map/psum | solution.py:95
  140.7 4.1 %copy-start.21 = (f32[2,8,1024]{2,1,0:T(8,128)}, f32[2,8,1024]{2,1,0:T(8,128)S(1)}, u32[]{:S(2)}) copy-start(f32[2,8,1024]{2,1,0:T(8,128)S(1)} %broadcast_multiply_fusion) | copy-start | bytes 196612
  143.8 1.6 copy-start.8
  143.8 2.2 copy-start.10
  143.8 2.8 copy-start.13
  143.8 3.4 copy-start.14
  143.9 3.4 copy-start.15
  143.9 3.4 copy-start.19
  151.8 2.9 copy-start
  155.6 122.7 %all-reduce.11.cloned.1.call-start = ((), (), s32[]{:S(2)}) async-start(), calls=%async_computation.6 | async-start | bytes 131072 | tf_op jit(solution)/shard_map/psum | solution.py:95
  157.5 57.9 %collective-permute-start.6 = (f32[32,2,1,1024]{3,0,2,1:T(8,128)}, f32[32,2,1,1024]{3,0,2,1:T(8,128)}, u32[]{:S(2)}, u32[]{:S(2)}) collective-permute-start(f32[32,2,1,1024]{3,0,2,1:T(8,128)} %get-tuple-element.43), channel_id=1, source_target_pairs={{4,0},{8,4},{12,8},{16,12},{20,16},{24,20},{28,24},{32,28},{36,32}... | collective-permute-start | bytes 786440 | tf_op jit(solution)/shard_map/ppermute | solution.py:18
  163.1 52.4 %collective-permute-start.7 = (f32[32,2,1,1024]{3,0,2,1:T(8,128)}, f32[32,2,1,1024]{3,0,2,1:T(8,128)}, u32[]{:S(2)}, u32[]{:S(2)}) collective-permute-start(f32[32,2,1,1024]{3,0,2,1:T(8,128)} %get-tuple-element.42), channel_id=1, source_target_pairs={{0,4},{4,8},{8,12},{12,16},{16,20},{20,24},{24,28},{28,32},{32,36}... | collective-permute-start | bytes 786440 | tf_op jit(solution)/shard_map/ppermute | solution.py:17
  200.3 5.3 %copy-start.18 = (f32[2,8,1024]{2,1,0:T(8,128)S(1)}, f32[2,8,1024]{2,1,0:T(8,128)}, u32[]{:S(2)}) copy-start(f32[2,8,1024]{2,1,0:T(8,128)} %param.16) | copy-start | bytes 196612
  200.3 5.3 %copy-start.23 = (f32[2,8,1024]{2,1,0:T(8,128)S(1)}, f32[2,8,1024]{2,1,0:T(8,128)}, u32[]{:S(2)}) copy-start(f32[2,8,1024]{2,1,0:T(8,128)} %param.14) | copy-start | bytes 196612
  200.3 5.3 %copy-start.25 = (f32[2,8,1024]{2,1,0:T(8,128)S(1)}, f32[2,8,1024]{2,1,0:T(8,128)}, u32[]{:S(2)}) copy-start(f32[2,8,1024]{2,1,0:T(8,128)} %param.15) | copy-start | bytes 196612
  206.8 8.6 %copy-start.11 = (f32[32,2,8,1023]{3,0,2,1:T(8,128)S(1)}, f32[32,2,8,1023]{3,0,2,1:T(8,128)}, u32[]{:S(2)}) copy-start(f32[32,2,8,1023]{3,0,2,1:T(8,128)} %get-tuple-element.44) | copy-start | bytes 6285316
  206.8 8.6 %copy-start.12 = (f32[32,2,8,1023]{3,0,2,1:T(8,128)S(1)}, f32[32,2,8,1023]{3,0,2,1:T(8,128)}, u32[]{:S(2)}) copy-start(f32[32,2,8,1023]{3,0,2,1:T(8,128)} %get-tuple-element.45) | copy-start | bytes 6285316
  207.4 8.0 %copy-start.1 = (f32[32,2,8,1024]{3,0,2,1:T(8,128)S(1)}, f32[32,2,8,1024]{3,0,2,1:T(8,128)}, u32[]{:S(2)}) copy-start(f32[32,2,8,1024]{3,0,2,1:T(8,128)} %copy-done) | copy-start | bytes 6291460
  207.4 8.0 %copy-start.9 = (f32[32,2,8,1024]{3,2,1,0:T(8,128)S(1)}, f32[32,2,8,1024]{3,2,1,0:T(8,128)}, u32[]{:S(2)}) copy-start(f32[32,2,8,1024]{3,2,1,0:T(8,128)} %param.12) | copy-start | bytes 6291460
  207.5 8.0 %copy-start.16 = (f32[32,2,8,1]{3,0,2,1:T(8,128)S(1)}, f32[32,2,8,1]{3,0,2,1:T(8,128)}, u32[]{:S(2)}) copy-start(f32[32,2,8,1]{3,0,2,1:T(8,128)} %get-tuple-element.47) | copy-start | bytes 6148
  207.6 17.5 %collective-permute-start.5 = (f32[2,32,2,1,1024]{4,1,3,2,0:T(8,128)S(1)}, f32[2,32,2,1,1024]{4,1,3,2,0:T(8,128)S(1)}, u32[]{:S(2)}, u32[]{:S(2)}) collective-permute-start(f32[2,32,2,1,1024]{4,1,3,2,0:T(8,128)S(1)} %get-tuple-element.26), channel_id=1, source_target_pairs={{4,0},{8,4},{12,8},{16,12},{20,16},{24,20},{28,24},{32,28},{36,32}... | collective-permute-start | bytes 1572872 | tf_op jit(solution)/shard_map/ppermute | solution.py:18
  213.4 18.8 %collective-permute-start.4 = (f32[2,32,2,1,1024]{4,1,3,2,0:T(8,128)S(1)}, f32[2,32,2,1,1024]{4,1,3,2,0:T(8,128)S(1)}, u32[]{:S(2)}, u32[]{:S(2)}) collective-permute-start(f32[2,32,2,1,1024]{4,1,3,2,0:T(8,128)S(1)} %get-tuple-element.25), channel_id=1, source_target_pairs={{0,4},{4,8},{8,12},{12,16},{16,20},{20,24},{24,28},{28,32},{32,36}... | collective-permute-start | bytes 1572872 | tf_op jit(solution)/shard_map/ppermute | solution.py:17
  233.0 1.6 copy-start.2
  234.6 3.7 copy-start.28
  234.6 3.7 copy-start.31
  234.6 4.4 %copy-start.27 = (f32[2,8,1024]{2,1,0:T(8,128)S(1)}, f32[2,8,1024]{2,1,0:T(8,128)}, u32[]{:S(2)}) copy-start(f32[2,8,1024]{2,1,0:T(8,128)} %get-tuple-element.12) | copy-start | bytes 196612
  234.6 4.4 %copy-start.30 = (f32[2,8,1024]{2,1,0:T(8,128)S(1)}, f32[2,8,1024]{2,1,0:T(8,128)}, u32[]{:S(2)}) copy-start(f32[2,8,1024]{2,1,0:T(8,128)} %get-tuple-element.24) | copy-start | bytes 196612
  234.6 5.1 %copy-start.26 = (f32[2,8,1024]{2,1,0:T(8,128)S(1)}, f32[2,8,1024]{2,1,0:T(8,128)}, u32[]{:S(2)}) copy-start(f32[2,8,1024]{2,1,0:T(8,128)} %get-tuple-element.10) | copy-start | bytes 196612
  234.6 5.1 %copy-start.29 = (f32[2,8,1024]{2,1,0:T(8,128)S(1)}, f32[2,8,1024]{2,1,0:T(8,128)}, u32[]{:S(2)}) copy-start(f32[2,8,1024]{2,1,0:T(8,128)} %get-tuple-element.8) | copy-start | bytes 196612
  234.6 43.7 %copy-start.33 = (f32[32]{0:T(128)S(1)}, f32[32]{0:T(128)}, u32[]{:S(2)}) copy-start(f32[32]{0:T(128)} %get-tuple-element.56) | copy-start | bytes 388
  238.2 74.3 %reduce-scatter.4.cloned.1.call-start = ((), (), s32[]{:S(2)}) async-start(), calls=%async_computation.7 | async-start | bytes 81920 | tf_op jit(solution)/shard_map/reduce_scatter | solution.py:75
  239.0 107.7 %reduce-scatter.6.cloned.1.call-start = ((), (), s32[]{:S(2)}) async-start(), calls=%async_computation.8 | async-start | bytes 81920 | tf_op jit(solution)/shard_map/reduce_scatter | solution.py:76
  239.7 141.3 %reduce-scatter.8.cloned.1.call-start = ((), (), s32[]{:S(2)}) async-start(), calls=%async_computation.9 | async-start | bytes 81920 | tf_op jit(solution)/shard_map/reduce_scatter | solution.py:77
  (1 other events, 1.6 us)
Sparse Core Ops, SparseCore 0:
  11.8 47.9 all-reduce.4
  96.9 42.8 all-reduce.6
  155.7 44.5 all-reduce.8
  238.4 39.8 all-reduce.10
  281.4 31.0 reduce-scatter.3
  315.6 31.0 reduce-scatter.5
  349.9 31.0 reduce-scatter.7
where the time goes:
time: 389 us; the launch traced here: 388 us
  waiting for transfers between devices  273 us (70%)
  other arithmetic  43 us (11%)
  starting transfers between devices  33.9 us (9%)
  local copies, waits for them, and re-layouts  22.4 us (6%)
  between operations  14.7 us (4%)
    psum x2, waiting for transfers between devices, local(): crowd = lax.psum(jnp.sum(weight * state, axis=0), 'coh') / COH  84.2 us
    psum x2, waiting for transfers between devices, local(): lax.psum(jnp.sum(-crowding * grad_surv * survived, axis=0), 'coh')  72.9 us
    reduce_scatter x1, waiting for transfers between devices, local(): lax.psum_scatter(grad_kappa, 'coh', scatter_dimension=2, tiled=True)  34.3 us
    reduce_scatter x1, waiting for transfers between devices, local(): lax.psum_scatter(grad_north, 'coh', scatter_dimension=2, tiled=True)  34.2 us
    reduce_scatter x1, waiting for transfers between devices, local(): lax.psum_scatter(grad_east, 'coh', scatter_dimension=2, tiled=True)  30.3 us
    ppermute x4, starting transfers between devices, extended(): after = lax.ppermute(first, axis, down)  24.2 us
    ppermute x4, waiting for transfers between devices, extended(): before = lax.ppermute(last, axis, up)  10.7 us
    reduce_sum x2, other arithmetic, local(): grad_kappa = jnp.sum(masked * laplace, axis=0)  9.98 us
  transfers between devices with their start and end apart: 15, of which 11 were waited for; matrix products, arithmetic and copies ran while one was open for 7% of the time, Pallas kernels for 0%

commit v1 on v0

--- a/solution.py
+++ b/solution.py
@@ -18,6 +18,35 @@
         after = lax.ppermute(first, axis, down)
         value = jnp.concatenate([before, value, after], axis=dim)
     return value
+
+
+def swap(value, flip):
+    return lax.ppermute(value, "coh", [(i, i ^ flip) for i in range(4)])
+
+
+def total(value):
+    value = value + swap(value, 1)
+    return value + swap(value, 2)
+
+
+def scatter(value):
+    high, low = lax.axis_index("coh") // 2, lax.axis_index("coh") % 2
+    split = value.reshape(value.shape[:-1] + (2, 2, value.shape[-1] // 4))
+
+    def halves(array, dim, side):
+        first, second = (lax.index_in_dim(array, k, dim, keepdims=False) for k in range(2))
+        return jnp.where(side == 0, first, second), jnp.where(side == 0, second, first)
+
+    keep, send = halves(split, split.ndim - 2, low)
+    keep, send = halves(keep + swap(send, 1), keep.ndim - 2, high)
+    return keep + swap(send, 2)
+
+
+def rows(value, up):
+    devices, length = (lax.axis_size("lat"), value.shape[2])
+    edge = lax.slice_in_dim(value, length - 1, length, axis=2) if up else lax.slice_in_dim(value, 0, 1, axis=2)
+    pairs = [(i, i + 1) if up else (i + 1, i) for i in range(devices - 1)]
+    return lax.ppermute(edge, "lat", pairs)
 
 
 def lookup(age_class, mort_rate, crowd_coef, mass, speed):
@@ -49,7 +78,7 @@
     state = density
     saved = []
     for section in range(STEPS):
-        crowd = lax.psum(jnp.sum(weight * state, axis=0), "coh") / COH
+        crowd = total(jnp.sum(weight * state, axis=0)) / COH
         survival = jnp.exp(-(mortal + crowding * crowd[None]))
         survived = state * survival
         wet = ocean * survived
@@ -71,19 +100,14 @@
         grad_east = -jnp.sum(masked * swim * east_diff, axis=0)
         grad_north = -jnp.sum(masked * swim * north_diff, axis=0)
         grad_kappa = jnp.sum(masked * laplace, axis=0)
-        pieces = (
-            lax.psum_scatter(grad_east, "coh", scatter_dimension=2, tiled=True),
-            lax.psum_scatter(grad_north, "coh", scatter_dimension=2, tiled=True),
-            lax.psum_scatter(grad_kappa, "coh", scatter_dimension=2, tiled=True),
-        )
-        shares = pieces if shares is None else jax.tree.map(jnp.add, shares, pieces)
+        pieces = jnp.stack([grad_east, grad_north, grad_kappa])
+        shares = pieces if shares is None else shares + pieces
         to_north = (kappa - 0.5 * north_coef) * masked
         to_south = (kappa + 0.5 * north_coef) * masked
         to_east = (kappa - 0.5 * east_coef) * masked
         to_west = (kappa + 0.5 * east_coef) * masked
-        stacked = extended(jnp.stack([to_north, to_south]), (("lat", 3),), 1)
-        from_below = stacked[0][:, :, :-2]
-        from_above = stacked[1][:, :, 2:]
+        from_below = jnp.concatenate([rows(to_north, True), to_north[:, :, :-1]], axis=2)
+        from_above = jnp.concatenate([to_south[:, :, 1:], rows(to_south, False)], axis=2)
         grad_wet = (
             (1.0 - 4.0 * kappa) * masked
             + jnp.roll(to_east, 1, axis=3)
@@ -92,8 +116,9 @@
             + from_above
         )
         grad_surv = ocean * grad_wet
-        pressure = lax.psum(jnp.sum(-crowding * grad_surv * survived, axis=0), "coh")
+        pressure = total(jnp.sum(-crowding * grad_surv * survived, axis=0))
         adjoint = grad_surv * survival + weight / COH * pressure[None]
+    shares = scatter(shares)
     return (adjoint, shares[0], shares[1], shares[2])
 
 

time: 389 us -> 129 us (0.33)
  waiting for transfers between devices: 273 us -> 26.1 us
  starting transfers between devices: 33.9 us -> 48.7 us
  between operations: 14.7 us -> 1.36 us
  other arithmetic: 43 us -> 33 us
  local copies, waits for them, and re-layouts: 22.4 us -> 18.3 us
    psum x4 -> x0, waiting for transfers between devices: 157 us -> none  [the longest x2 84.2 us: local(): crowd = lax.psum(jnp.sum(weight * state, axis=0), 'coh') / COH]
    reduce_scatter x3 -> x0, waiting for transfers between devices: 98.8 us -> none  [the longest x1 34.3 us: local(): lax.psum_scatter(grad_kappa, 'coh', scatter_dimension=2, tiled=True)]
    ppermute x0 -> x14, starting transfers between devices: none -> 28.8 us  [the longest x4 17.5 us: rows(): return lax.ppermute(edge, 'lat', pairs)]
    ppermute x0 -> x14, waiting for transfers between devices: none -> 22.3 us  [the longest x10 12 us: swap(): return lax.ppermute(value, 'coh', [(i, i ^ flip) for i in range(4)])]
    ppermute x4 -> x2, starting transfers between devices: 24.2 us -> 14.2 us  [extended(): after = lax.ppermute(first, axis, down)]
    ppermute x4 -> x2, waiting for transfers between devices: 10.7 us -> 2.44 us  [extended(): before = lax.ppermute(last, axis, up)]
    ppermute x4 -> x2, waiting for transfers between devices: 6.19 us -> 1.35 us  [extended(): after = lax.ppermute(first, axis, down)]
    concatenate x2 -> x0, other arithmetic: 3.93 us -> none  [extended(): value = jnp.concatenate([before, value, after], axis=dim)]
  transfers between devices with their start and end apart: 15 -> 18, of which waited for: 11 -> 9; matrix products, arithmetic and copies ran while one was open for 7% -> 18% of each run, Pallas kernels for 0% -> 0%
where the time goes in v1:
time: 129 us
  starting transfers between devices  48.7 us (38%)
  other arithmetic  33 us (26%)
  waiting for transfers between devices  26.1 us (20%)
  local copies, waits for them, and re-layouts  18.3 us (14%)
  between operations  1.36 us (1%)
    ppermute x4, starting transfers between devices, rows(): return lax.ppermute(edge, 'lat', pairs)  17.5 us
    ppermute x2, starting transfers between devices, extended(): after = lax.ppermute(first, axis, down)  14.2 us
    reduce_sum x2, other arithmetic, local(): grad_east = -jnp.sum(masked * swim * east_diff, axis=0)  12 us
    ppermute x10, waiting for transfers between devices, swap(): return lax.ppermute(value, 'coh', [(i, i ^ flip) for i in range(4)])  12 us
    ppermute x10, starting transfers between devices, swap(): return lax.ppermute(value, 'coh', [(i, i ^ flip) for i in range(4)])  11.3 us
    ppermute x4, waiting for transfers between devices, rows(): return lax.ppermute(edge, 'lat', pairs)  10.3 us
    reduce_sum x2, other arithmetic, local(): pressure = total(jnp.sum(-crowding * grad_surv * survived, axis=0))  6.72 us
    mul x2, other arithmetic, local(): to_east = (kappa - 0.5 * east_coef) * masked  6.66 us
  transfers between devices with their start and end apart: 18, of which 9 were waited for; matrix products, arithmetic and copies ran while one was open for 18% of the time, Pallas kernels for 0%

profile of v1, /device:TPU:6, one launch (start us, length us, event | category | flops | bytes accessed | tf_op | source)
XLA Modules:
  0.0 128.5 jit_solution(6337365810225075857)
XLA Ops:
  0.7 1.1 fusion.31
  1.7 2.8 %multiply_reduce_fusion.9 = f32[2,8,1024]{2,1,0:T(8,128)S(1)} fusion(f32[32,2,8,1024]{3,2,1,0:T(8,128)} %param.11, f32[32]{0:T(128)S(1)} %get-tuple-element.60), kind=kLoop, calls=%fused_computation.56 | loop fusion | flops 1032192 | bytes 2162816 | tf_op jit(solution)/shard_map/reduce_sum | solution.py:81
  4.7 1.2 collective-permute-done.2
  5.9 3.3 %collective-permute-start.3 = (f32[2,8,1024]{2,1,0:T(8,128)S(1)}, f32[2,8,1024]{2,1,0:T(8,128)S(1)}, u32[]{:S(2)}, u32[]{:S(2)}) collective-permute-start(f32[2,8,1024]{2,1,0:T(8,128)S(1)} %add.134), channel_id=1, source_target_pairs={{0,2},{1,3},{2,0},{3,1},{4,6},{5,7},{6,4},{7,5},{8,10},{9,11},{10,... | collective-permute-start | bytes 196616 | tf_op jit(solution)/shard_map/ppermute | solution.py:24
  9.2 2.6 %collective-permute-done.3 = f32[2,8,1024]{2,1,0:T(8,128)S(1)} collective-permute-done((f32[2,8,1024]{2,1,0:T(8,128)S(1)}, f32[2,8,1024]{2,1,0:T(8,128)S(1)}, u32[]{:S(2)}, u32[]{:S(2)}) %collective-permute-start.3) | collective-permute-done | bytes 65568 | tf_op jit(solution)/shard_map/ppermute | solution.py:24
  11.8 1.4 %fusion.26 = f32[32,2,8,1024]{3,0,2,1:T(8,128)S(1)} fusion(f32[32,2,8,1024]{3,2,1,0:T(8,128)S(1)} %copy-done.1, f32[2,8,1024]{2,1,0:T(8,128)S(1)} %add_multiply_fusion.2, f32[32]{0:T(128)S(1)} %get-tuple-element.61, f32[32]{0:T(128)S(1)} %get-tuple-element.62, f32[2,8,1024]{2,1,0:T(8,128)S(1)} %convert_element_type.4), kind=kLoop, calls=%fused_computation.58 | loop fusion | flops 2621440 | bytes 4325632 | tf_op jit(solution)/shard_map/mul | solution.py:84
  13.3 3.8 %collective-permute-start.5 = (f32[32,2,1,1024]{3,0,2,1:T(8,128)S(1)}, f32[32,2,1,1024]{3,0,2,1:T(8,128)S(1)}, u32[]{:S(2)}, u32[]{:S(2)}) collective-permute-start(f32[32,2,1,1024]{3,0,2,1:T(8,128)S(1)} %get-tuple-element.41), channel_id=1, source_target_pairs={{0,4},{4,8},{8,12},{12,16},{16,20},{20,24},{24,28},{28,32},{32,36}... | collective-permute-start | bytes 786440 | tf_op jit(solution)/shard_map/ppermute | solution.py:17
  17.1 7.3 %collective-permute-start.4 = (f32[32,2,1,1024]{3,0,2,1:T(8,128)S(1)}, f32[32,2,1,1024]{3,0,2,1:T(8,128)S(1)}, u32[]{:S(2)}, u32[]{:S(2)}) collective-permute-start(f32[32,2,1,1024]{3,0,2,1:T(8,128)S(1)} %get-tuple-element.40), channel_id=1, source_target_pairs={{4,0},{8,4},{12,8},{16,12},{20,16},{24,20},{28,24},{32,28},{36,32}... | collective-permute-start | bytes 786440 | tf_op jit(solution)/shard_map/ppermute | solution.py:18
  24.4 0.7 fusion.49
  25.3 2.4 %collective-permute-done.5 = f32[32,2,1,1024]{3,0,2,1:T(8,128)S(1)} collective-permute-done((f32[32,2,1,1024]{3,0,2,1:T(8,128)S(1)}, f32[32,2,1,1024]{3,0,2,1:T(8,128)S(1)}, u32[]{:S(2)}, u32[]{:S(2)}) %collective-permute-start.5) | collective-permute-done | bytes 262176 | tf_op jit(solution)/shard_map/ppermute | solution.py:17
  27.8 1.3 %collective-permute-done.4 = f32[32,2,1,1024]{3,0,2,1:T(8,128)S(1)} collective-permute-done((f32[32,2,1,1024]{3,0,2,1:T(8,128)S(1)}, f32[32,2,1,1024]{3,0,2,1:T(8,128)S(1)}, u32[]{:S(2)}, u32[]{:S(2)}) %collective-permute-start.4) | collective-permute-done | bytes 262176 | tf_op jit(solution)/shard_map/ppermute | solution.py:18
  29.1 5.3 %fusion.9 = (f32[32,2,8,1024]{3,0,2,1:T(8,128)}, f32[32,2,8,1024]{3,0,2,1:T(8,128)}, f32[32,2,8,1024]{3,0,2,1:T(8,128)S(1)}, f32[32,2,8,1024]{3,0,2,1:T(8,128)S(...) fusion(f32[2,8,1024]{2,1,0:T(8,128)S(1)} %copy-done.20, f32[32]{0:T(128)S(1)} %get-tuple-element.59, ...), kind=kLoop, calls=%fused_computation.13 | loop fusion | flops 18333696 | bytes 19726592 | tf_op jit(solution)/shard_map/mul | solution.py:107
  34.6 0.9 slice.187
  35.5 7.4 %collective-permute-start.1 = (f32[32,2,1,1024]{3,0,2,1:T(8,128)}, f32[32,2,1,1024]{3,0,2,1:T(8,128)}, u32[]{:S(2)}, u32[]{:S(2)}) collective-permute-start(f32[32,2,1,1024]{3,0,2,1:T(8,128)} %slice.187), channel_id=1, source_target_pairs={{4,0},{8,4},{12,8},{16,12},{20,16},{24,20},{28,24},{32,28},{36,32}... | collective-permute-start | bytes 786440 | tf_op jit(solution)/shard_map/ppermute | solution.py:49
  42.9 0.7 slice.184
  43.6 1.9 %collective-permute-start = (f32[32,2,1,1024]{3,0,2,1:T(8,128)}, f32[32,2,1,1024]{3,0,2,1:T(8,128)}, u32[]{:S(2)}, u32[]{:S(2)}) collective-permute-start(f32[32,2,1,1024]{3,0,2,1:T(8,128)} %slice.184), channel_id=1, source_target_pairs={{0,4},{4,8},{8,12},{12,16},{16,20},{20,24},{24,28},{28,32},{32,36}... | collective-permute-start | bytes 786440 | tf_op jit(solution)/shard_map/ppermute | solution.py:49
  45.6 3.0 %collective-permute-start.7 = (f32[2,8,1024]{2,1,0:T(8,128)S(1)}, f32[2,8,1024]{2,1,0:T(8,128)S(1)}, u32[]{:S(2)}, u32[]{:S(2)}) collective-permute-start(f32[2,8,1024]{2,1,0:T(8,128)S(1)} %add.141), channel_id=1, source_target_pairs={{0,2},{1,3},{2,0},{3,1},{4,6},{5,7},{6,4},{7,5},{8,10},{9,11},{10,... | collective-permute-start | bytes 196616 | tf_op jit(solution)/shard_map/ppermute | solution.py:24
  49.1 1.8 %slice.186 = f32[32,2,7,1024]{3,0,2,1:T(8,128)S(1)} slice(f32[32,2,8,1024]{3,0,2,1:T(8,128)} %copy-done.14), slice={[0:32], [0:2], [1:8], [0:1024]} | slice | bytes 3670016 | tf_op jit(solution)/shard_map/slice | solution.py:110
  51.4 1.4 %copy-done.10 = f32[32,2,8,1024]{3,0,2,1:T(8,128)S(1)} copy-done((f32[32,2,8,1024]{3,0,2,1:T(8,128)S(1)}, f32[32,2,8,1024]{3,0,2,1:T(8,128)}, u32[]{:S(2)}) %copy-start.10) | copy-done | bytes 2097176
  52.9 0.6 slice.182
  53.5 1.0 copy-done.11
  54.6 2.5 %collective-permute-done.7 = f32[2,8,1024]{2,1,0:T(8,128)S(1)} collective-permute-done((f32[2,8,1024]{2,1,0:T(8,128)S(1)}, f32[2,8,1024]{2,1,0:T(8,128)S(1)}, u32[]{:S(2)}, u32[]{:S(2)}) %collective-permute-start.7) | collective-permute-done | bytes 65568 | tf_op jit(solution)/shard_map/ppermute | solution.py:24
  57.1 3.9 %multiply_reduce_fusion.7 = (f32[2,8,1024]{2,1,0:T(8,128)S(1)}, f32[32,2,8,1024]{3,0,2,1:T(8,128)S(1)}, f32[32,2,8,1024]{3,0,2,1:T(8,128)S(1)}) fusion(f32[32,2,8,1024]{3,0,2,1:T(8,128)S(1)} %copy-done.15, f32[32]{0:T(128)S(1)} %get-tuple-element.58, f32[2,8,1024]{2,1,0:T(8,128)S(1)} %add_multiply_fusion.1, f32[32]{0:T(128)S(1)} %get-tuple-element.61, ...), kind=kLoop, calls=%fused_computation.47 | loop fusion | flops 9945088 | bytes 17039744 | tf_op jit(solution)/shard_map/reduce_sum | solution.py:119
  61.4 2.8 %fusion.46 = (f32[32,2,8,1023]{3,0,2,1:T(8,128)}, f32[32,2,8,1023]{3,0,2,1:T(8,128)}) fusion(f32[32,2,8,1024]{3,0,2,1:T(8,128)S(1)} %get-tuple-element.25), kind=kLoop, calls=%fused_computation.94 | loop fusion | bytes 8380416 | tf_op jit(solution)/shard_map/jit(_roll_static)/slice | solution.py:88
  64.2 0.9 fusion.47
  65.1 3.0 %collective-permute-start.9 = (f32[2,8,1024]{2,1,0:T(8,128)S(1)}, f32[2,8,1024]{2,1,0:T(8,128)S(1)}, u32[]{:S(2)}, u32[]{:S(2)}) collective-permute-start(f32[2,8,1024]{2,1,0:T(8,128)S(1)} %add.144), channel_id=1, source_target_pairs={{0,2},{1,3},{2,0},{3,1},{4,6},{5,7},{6,4},{7,5},{8,10},{9,11},{10,... | collective-permute-start | bytes 196616 | tf_op jit(solution)/shard_map/ppermute | solution.py:24
  68.0 0.8 fusion.45
  68.9 1.9 %collective-permute-start.15 = (f32[32,2,1,1024]{3,0,2,1:T(8,128)}, f32[32,2,1,1024]{3,0,2,1:T(8,128)}, u32[]{:S(2)}, u32[]{:S(2)}) collective-permute-start(f32[32,2,1,1024]{3,0,2,1:T(8,128)} %get-tuple-element.35), channel_id=1, source_target_pairs={{0,4},{4,8},{8,12},{12,16},{16,20},{20,24},{24,28},{28,32},{32,36}... | collective-permute-start | bytes 786440 | tf_op jit(solution)/shard_map/ppermute | solution.py:17
  70.8 6.9 %collective-permute-start.14 = (f32[32,2,1,1024]{3,0,2,1:T(8,128)}, f32[32,2,1,1024]{3,0,2,1:T(8,128)}, u32[]{:S(2)}, u32[]{:S(2)}) collective-permute-start(f32[32,2,1,1024]{3,0,2,1:T(8,128)} %get-tuple-element.34), channel_id=1, source_target_pairs={{4,0},{8,4},{12,8},{16,12},{20,16},{24,20},{28,24},{32,28},{36,32}... | collective-permute-start | bytes 786440 | tf_op jit(solution)/shard_map/ppermute | solution.py:18
  77.8 4.3 %multiply_reduce_fusion.2 = (f32[2,8,1024]{2,1,0:T(8,128)}, f32[2,8,1024]{2,1,0:T(8,128)}, f32[2,8,1024]{2,1,0:T(8,128)}, f32[32,2,8,1024]{3,0,2,1:T(8,128)}) fusion(f32[32]{0:T(128)S(1)} %get-tuple-element.59, f32[32,2,8,1023]{3,0,2,1:T(8,128)S(1)} %copy-done.6, f32[32,2,8,1]{3,0,2,1:T(8,128)S(1)} %get-tuple-element.45, ...), kind=kLoop, calls=%fused_computation.40 | loop fusion | flops 14106624 | bytes 11403776 | tf_op jit(solution)/shard_map/reduce_sum | solution.py:100
  82.1 0.9 stack.38
  83.0 0.8 neg.80
  84.0 0.8 neg.78
  84.9 7.7 %multiply_reduce_fusion.5 = (f32[2,8,1024]{2,1,0:T(8,128)S(1)}, f32[2,8,1024]{2,1,0:T(8,128)S(1)}, f32[2,8,1024]{2,1,0:T(8,128)S(1)}) fusion(f32[32,2,8,1023]{3,0,2,1:T(8,128)} %get-tuple-element.37, f32[32,2,8,1]{3,0,2,1:T(8,128)} %get-tuple-element.39, f32[32,2,8,1]{3,0,2,1:T(8,128)S(1)} %get-tuple-element.38, f32[32,2,8,1023]{3,0,2,1:T(8,128)} %get-tuple-element.36, ...), kind=kLoop, calls=%fused_computation.43 | loop fusion | flops 10960896 | bytes 9175168 | tf_op jit(solution)/shard_map/reduce_sum | solution.py:100
  93.4 1.3 %fusion.8 = (f32[32,2,8,1024]{3,0,2,1:T(8,128)S(1)}, f32[32,2,8,1024]{3,0,2,1:T(8,128)S(1)}, f32[32,2,8,1024]{3,0,2,1:T(8,128)S(1)}, f32[32,2,8,1024]{3,0,2,1:T(8,128)S(1)}) fusion(f32[32,2,8,1024]{3,0,2,1:T(8,128)S(1)} %copy-done.7, f32[2,8,1024]{2,1,0:T(8,128)S(1)} %copy-done.21, f32[32]{0:T(128)S(1)} %get-tuple-element.59, ...), kind=kLoop, calls=%fused_computation.12 | loop fusion | flops 6291456 | bytes 10682496 | tf_op jit(solution)/shard_map/mul | solution.py:107
  95.3 0.6 slice.196
  95.9 6.2 %collective-permute-start.11 = (f32[32,2,1,1024]{3,0,2,1:T(8,128)S(1)}, f32[32,2,1,1024]{3,0,2,1:T(8,128)S(1)}, u32[]{:S(2)}, u32[]{:S(2)}) collective-permute-start(f32[32,2,1,1024]{3,0,2,1:T(8,128)S(1)} %slice.201), channel_id=1, source_target_pairs={{4,0},{8,4},{12,8},{16,12},{20,16},{24,20},{28,24},{32,28},{36,32}... | collective-permute-start | bytes 786440 | tf_op jit(solution)/shard_map/ppermute | solution.py:49
  102.1 1.9 %collective-permute-start.10 = (f32[32,2,1,1024]{3,0,2,1:T(8,128)S(1)}, f32[32,2,1,1024]{3,0,2,1:T(8,128)S(1)}, u32[]{:S(2)}, u32[]{:S(2)}) collective-permute-start(f32[32,2,1,1024]{3,0,2,1:T(8,128)S(1)} %slice.198), channel_id=1, source_target_pairs={{0,4},{4,8},{8,12},{12,16},{16,20},{20,24},{24,28},{28,32},{32,36}... | collective-permute-start | bytes 786440 | tf_op jit(solution)/shard_map/ppermute | solution.py:49
  104.4 0.7 collective-permute-start.17
  105.1 3.2 %collective-permute-done.11 = f32[32,2,1,1024]{3,0,2,1:T(8,128)S(1)} collective-permute-done((f32[32,2,1,1024]{3,0,2,1:T(8,128)S(1)}, f32[32,2,1,1024]{3,0,2,1:T(8,128)S(1)}, u32[]{:S(2)}, u32[]{:S(2)}) %collective-permute-start.11) | collective-permute-done | bytes 262176 | tf_op jit(solution)/shard_map/ppermute | solution.py:49
  108.3 7.1 %collective-permute-done.10 = f32[32,2,1,1024]{3,0,2,1:T(8,128)S(1)} collective-permute-done((f32[32,2,1,1024]{3,0,2,1:T(8,128)S(1)}, f32[32,2,1,1024]{3,0,2,1:T(8,128)S(1)}, u32[]{:S(2)}, u32[]{:S(2)}) %collective-permute-start.10) | collective-permute-done | bytes 262176 | tf_op jit(solution)/shard_map/ppermute | solution.py:49
  115.4 2.8 %multiply_reduce_fusion.6 = (f32[2,8,1024]{2,1,0:T(8,128)S(1)}, f32[32,2,8,1024]{3,0,2,1:T(8,128)S(1)}) fusion(f32[32,2,8,1024]{3,2,1,0:T(8,128)S(1)} %copy-done.2, f32[32]{0:T(128)S(1)} %get-tuple-element.58, f32[2,8,1024]{2,1,0:T(8,128)S(1)} %add_multiply_fusion.2, f32[32]{0:T(128)S(1)} %get-tuple-element.61, f32[32]{0:T(128)S(1)} %get-tuple-element.62, ...), kind=kLoop, calls=%fused_computation.45 | loop fusion | flops 8896512 | bytes 14942592 | tf_op jit(solution)/shard_map/reduce_sum | solution.py:119
  118.4 1.2 collective-permute-done.12
  119.6 0.7 collective-permute-start.13
  120.3 0.6 slice_bitcast_fusion
  120.9 4.5 %collective-permute-done.13 = f32[2,8,1024]{2,1,0:T(8,128)S(1)} collective-permute-done((f32[2,8,1024]{2,1,0:T(8,128)S(1)}, f32[2,8,1024]{2,1,0:T(8,128)S(1)}, u32[]{:S(2)}, u32[]{:S(2)}) %collective-permute-start.13) | collective-permute-done | bytes 65568 | tf_op jit(solution)/shard_map/ppermute | solution.py:24
  125.5 0.5 multiply_add_fusion
  126.0 2.5 %copy.34 = f32[32,2,8,1024]{3,2,1,0:T(8,128)} copy(f32[32,2,8,1024]{3,0,2,1:T(8,128)S(1)} %multiply_add_fusion) | data formatting | bytes 4194304
  (103 shorter events, 3.9 us)
Async XLA Ops:
  0.6 11.2 %copy-start.1 = (f32[32,2,8,1024]{3,2,1,0:T(8,128)S(1)}, f32[32,2,8,1024]{3,2,1,0:T(8,128)}, u32[]{:S(2)}) copy-start(f32[32,2,8,1024]{3,2,1,0:T(8,128)} %param.11) | copy-start | bytes 6291460
  0.6 8.6 %copy-start.24 = (s32[2,8,1024]{2,1,0:T(8,128)S(1)}, s32[2,8,1024]{2,1,0:T(8,128)}, u32[]{:S(2)}) copy-start(s32[2,8,1024]{2,1,0:T(8,128)} %param.13) | copy-start | bytes 196612
  4.6 1.3 %collective-permute-start.2 = (f32[2,8,1024]{2,1,0:T(8,128)S(1)}, f32[2,8,1024]{2,1,0:T(8,128)S(1)}, u32[]{:S(2)}, u32[]{:S(2)}) collective-permute-start(f32[2,8,1024]{2,1,0:T(8,128)S(1)} %multiply_reduce_fusion.9), channel_id=1, source_target_pairs={{0,1},{1,0},{2,3},{3,2},{4,5},{5,4},{6,7},{7,6},{8,9},{9,8},{10,11... | collective-permute-start | bytes 196616 | tf_op jit(solution)/shard_map/ppermute | solution.py:24
  5.9 5.9 %collective-permute-start.3 = (f32[2,8,1024]{2,1,0:T(8,128)S(1)}, f32[2,8,1024]{2,1,0:T(8,128)S(1)}, u32[]{:S(2)}, u32[]{:S(2)}) collective-permute-start(f32[2,8,1024]{2,1,0:T(8,128)S(1)} %add.134), channel_id=1, source_target_pairs={{0,2},{1,3},{2,0},{3,1},{4,6},{5,7},{6,4},{7,5},{8,10},{9,11},{10,... | collective-permute-start | bytes 196616 | tf_op jit(solution)/shard_map/ppermute | solution.py:24
  13.3 14.5 %collective-permute-start.5 = (f32[32,2,1,1024]{3,0,2,1:T(8,128)S(1)}, f32[32,2,1,1024]{3,0,2,1:T(8,128)S(1)}, u32[]{:S(2)}, u32[]{:S(2)}) collective-permute-start(f32[32,2,1,1024]{3,0,2,1:T(8,128)S(1)} %get-tuple-element.41), channel_id=1, source_target_pairs={{0,4},{4,8},{8,12},{12,16},{16,20},{20,24},{24,28},{28,32},{32,36}... | collective-permute-start | bytes 786440 | tf_op jit(solution)/shard_map/ppermute | solution.py:17
  17.1 12.0 %copy-start.16 = (f32[2,8,1024]{2,1,0:T(8,128)S(1)}, f32[2,8,1024]{2,1,0:T(8,128)}, u32[]{:S(2)}) copy-start(f32[2,8,1024]{2,1,0:T(8,128)} %param.16) | copy-start | bytes 196612
  17.1 12.0 %copy-start.20 = (f32[2,8,1024]{2,1,0:T(8,128)S(1)}, f32[2,8,1024]{2,1,0:T(8,128)}, u32[]{:S(2)}) copy-start(f32[2,8,1024]{2,1,0:T(8,128)} %param.14) | copy-start | bytes 196612
  17.1 12.0 %copy-start.22 = (f32[2,8,1024]{2,1,0:T(8,128)S(1)}, f32[2,8,1024]{2,1,0:T(8,128)}, u32[]{:S(2)}) copy-start(f32[2,8,1024]{2,1,0:T(8,128)} %param.15) | copy-start | bytes 196612
  17.1 12.0 %collective-permute-start.4 = (f32[32,2,1,1024]{3,0,2,1:T(8,128)S(1)}, f32[32,2,1,1024]{3,0,2,1:T(8,128)S(1)}, u32[]{:S(2)}, u32[]{:S(2)}) collective-permute-start(f32[32,2,1,1024]{3,0,2,1:T(8,128)S(1)} %get-tuple-element.40), channel_id=1, source_target_pairs={{4,0},{8,4},{12,8},{16,12},{20,16},{24,20},{28,24},{32,28},{36,32}... | collective-permute-start | bytes 786440 | tf_op jit(solution)/shard_map/ppermute | solution.py:18
  24.4 4.7 %copy-start.8 = (f32[32,2,8,1024]{3,2,1,0:T(8,128)S(1)}, f32[32,2,8,1024]{3,2,1,0:T(8,128)}, u32[]{:S(2)}) copy-start(f32[32,2,8,1024]{3,2,1,0:T(8,128)} %param.12) | copy-start | bytes 6291460
  25.2 9.3 %copy-start.3 = (f32[32,2,8,1023]{3,0,2,1:T(8,128)}, f32[32,2,8,1023]{3,0,2,1:T(8,128)S(1)}, u32[]{:S(2)}) copy-start(f32[32,2,8,1023]{3,0,2,1:T(8,128)S(1)} %get-tuple-element.42) | copy-start | bytes 6285316
  25.2 9.3 %copy-start.5 = (f32[32,2,8,1023]{3,0,2,1:T(8,128)}, f32[32,2,8,1023]{3,0,2,1:T(8,128)S(1)}, u32[]{:S(2)}) copy-start(f32[32,2,8,1023]{3,0,2,1:T(8,128)S(1)} %get-tuple-element.43) | copy-start | bytes 6285316
  34.5 8.4 %copy-start.12 = (f32[32,2,8,1024]{3,0,2,1:T(8,128)}, f32[32,2,8,1024]{3,0,2,1:T(8,128)S(1)}, u32[]{:S(2)}) copy-start(f32[32,2,8,1024]{3,0,2,1:T(8,128)S(1)} %get-tuple-element.31) | copy-start | bytes 6291460
  34.5 9.1 %copy-start.14 = (f32[32,2,8,1024]{3,0,2,1:T(8,128)}, f32[32,2,8,1024]{3,0,2,1:T(8,128)S(1)}, u32[]{:S(2)}) copy-start(f32[32,2,8,1024]{3,0,2,1:T(8,128)S(1)} %get-tuple-element.30) | copy-start | bytes 6291460
  34.5 11.1 %collective-permute-start.6 = (f32[2,8,1024]{2,1,0:T(8,128)S(1)}, f32[2,8,1024]{2,1,0:T(8,128)S(1)}, u32[]{:S(2)}, u32[]{:S(2)}) collective-permute-start(f32[2,8,1024]{2,1,0:T(8,128)S(1)} %get-tuple-element.46), channel_id=1, source_target_pairs={{0,1},{1,0},{2,3},{3,2},{4,5},{5,4},{6,7},{7,6},{8,9},{9,8},{10,11... | collective-permute-start | bytes 196616 | tf_op jit(solution)/shard_map/ppermute | solution.py:24
  34.6 22.5 %copy-start.18 = (f32[2,8,1024]{2,1,0:T(8,128)}, f32[2,8,1024]{2,1,0:T(8,128)S(1)}, u32[]{:S(2)}) copy-start(f32[2,8,1024]{2,1,0:T(8,128)S(1)} %multiply_subtract_fusion.1) | copy-start | bytes 196612
  35.5 21.6 %collective-permute-start.1 = (f32[32,2,1,1024]{3,0,2,1:T(8,128)}, f32[32,2,1,1024]{3,0,2,1:T(8,128)}, u32[]{:S(2)}, u32[]{:S(2)}) collective-permute-start(f32[32,2,1,1024]{3,0,2,1:T(8,128)} %slice.187), channel_id=1, source_target_pairs={{4,0},{8,4},{12,8},{16,12},{20,16},{24,20},{28,24},{32,28},{36,32}... | collective-permute-start | bytes 786440 | tf_op jit(solution)/shard_map/ppermute | solution.py:49
  43.6 13.5 %collective-permute-start = (f32[32,2,1,1024]{3,0,2,1:T(8,128)}, f32[32,2,1,1024]{3,0,2,1:T(8,128)}, u32[]{:S(2)}, u32[]{:S(2)}) collective-permute-start(f32[32,2,1,1024]{3,0,2,1:T(8,128)} %slice.184), channel_id=1, source_target_pairs={{0,4},{4,8},{8,12},{12,16},{16,20},{20,24},{24,28},{28,32},{32,36}... | collective-permute-start | bytes 786440 | tf_op jit(solution)/shard_map/ppermute | solution.py:49
  45.6 11.5 %collective-permute-start.7 = (f32[2,8,1024]{2,1,0:T(8,128)S(1)}, f32[2,8,1024]{2,1,0:T(8,128)S(1)}, u32[]{:S(2)}, u32[]{:S(2)}) collective-permute-start(f32[2,8,1024]{2,1,0:T(8,128)S(1)} %add.141), channel_id=1, source_target_pairs={{0,2},{1,3},{2,0},{3,1},{4,6},{5,7},{6,4},{7,5},{8,10},{9,11},{10,... | collective-permute-start | bytes 196616 | tf_op jit(solution)/shard_map/ppermute | solution.py:24
  49.1 2.1 %copy-start.13 = (f32[32,2,8,1024]{3,0,2,1:T(8,128)S(1)}, f32[32,2,8,1024]{3,0,2,1:T(8,128)}, u32[]{:S(2)}) copy-start(f32[32,2,8,1024]{3,0,2,1:T(8,128)} %copy-done.12) | copy-start | bytes 6291460
  51.2 1.6 %copy-start.10 = (f32[32,2,8,1024]{3,0,2,1:T(8,128)S(1)}, f32[32,2,8,1024]{3,0,2,1:T(8,128)}, u32[]{:S(2)}) copy-start(f32[32,2,8,1024]{3,0,2,1:T(8,128)} %get-tuple-element.22) | copy-start | bytes 6291460
  51.2 5.9 %copy-start.15 = (f32[32,2,8,1024]{3,0,2,1:T(8,128)S(1)}, f32[32,2,8,1024]{3,0,2,1:T(8,128)}, u32[]{:S(2)}) copy-start(f32[32,2,8,1024]{3,0,2,1:T(8,128)} %get-tuple-element.47) | copy-start | bytes 6291460
  52.9 1.6 %copy-start.11 = (f32[32,2,8,1024]{3,0,2,1:T(8,128)S(1)}, f32[32,2,8,1024]{3,0,2,1:T(8,128)}, u32[]{:S(2)}) copy-start(f32[32,2,8,1024]{3,0,2,1:T(8,128)} %get-tuple-element.21) | copy-start | bytes 6291460
  52.9 4.2 %copy-start.9 = (f32[32,2,8,1024]{3,2,1,0:T(8,128)S(1)}, f32[32,2,8,1024]{3,2,1,0:T(8,128)}, u32[]{:S(2)}) copy-start(f32[32,2,8,1024]{3,2,1,0:T(8,128)} %param.12) | copy-start | bytes 6291460
  61.1 7.0 %copy-start = (f32[32,2,8,1024]{3,0,2,1:T(8,128)}, f32[32,2,8,1024]{3,0,2,1:T(8,128)S(1)}, u32[]{:S(2)}) copy-start(f32[32,2,8,1024]{3,0,2,1:T(8,128)S(1)} %get-tuple-element.25) | copy-start | bytes 6291460
  61.1 4.0 %collective-permute-start.8 = (f32[2,8,1024]{2,1,0:T(8,128)S(1)}, f32[2,8,1024]{2,1,0:T(8,128)S(1)}, u32[]{:S(2)}, u32[]{:S(2)}) collective-permute-start(f32[2,8,1024]{2,1,0:T(8,128)S(1)} %get-tuple-element.16), channel_id=1, source_target_pairs={{0,1},{1,0},{2,3},{3,2},{4,5},{5,4},{6,7},{7,6},{8,9},{9,8},{10,11... | collective-permute-start | bytes 196616 | tf_op jit(solution)/shard_map/ppermute | solution.py:24
  61.3 16.4 %copy-start.6 = (f32[32,2,8,1023]{3,0,2,1:T(8,128)S(1)}, f32[32,2,8,1023]{3,0,2,1:T(8,128)}, u32[]{:S(2)}) copy-start(f32[32,2,8,1023]{3,0,2,1:T(8,128)} %copy-done.5) | copy-start | bytes 6285316
  64.2 13.6 %copy-start.4 = (f32[32,2,8,1023]{3,0,2,1:T(8,128)S(1)}, f32[32,2,8,1023]{3,0,2,1:T(8,128)}, u32[]{:S(2)}) copy-start(f32[32,2,8,1023]{3,0,2,1:T(8,128)} %copy-done.3) | copy-start | bytes 6285316
  64.2 13.6 %copy-start.25 = (f32[32]{0:T(128)S(1)}, f32[32]{0:T(128)}, u32[]{:S(2)}) copy-start(f32[32]{0:T(128)} %get-tuple-element.57) | copy-start | bytes 388
  65.1 12.7 %collective-permute-start.9 = (f32[2,8,1024]{2,1,0:T(8,128)S(1)}, f32[2,8,1024]{2,1,0:T(8,128)S(1)}, u32[]{:S(2)}, u32[]{:S(2)}) collective-permute-start(f32[2,8,1024]{2,1,0:T(8,128)S(1)} %add.144), channel_id=1, source_target_pairs={{0,2},{1,3},{2,0},{3,1},{4,6},{5,7},{6,4},{7,5},{8,10},{9,11},{10,... | collective-permute-start | bytes 196616 | tf_op jit(solution)/shard_map/ppermute | solution.py:24
  68.9 16.0 %collective-permute-start.15 = (f32[32,2,1,1024]{3,0,2,1:T(8,128)}, f32[32,2,1,1024]{3,0,2,1:T(8,128)}, u32[]{:S(2)}, u32[]{:S(2)}) collective-permute-start(f32[32,2,1,1024]{3,0,2,1:T(8,128)} %get-tuple-element.35), channel_id=1, source_target_pairs={{0,4},{4,8},{8,12},{12,16},{16,20},{20,24},{24,28},{28,32},{32,36}... | collective-permute-start | bytes 786440 | tf_op jit(solution)/shard_map/ppermute | solution.py:17
  70.8 14.1 %collective-permute-start.14 = (f32[32,2,1,1024]{3,0,2,1:T(8,128)}, f32[32,2,1,1024]{3,0,2,1:T(8,128)}, u32[]{:S(2)}, u32[]{:S(2)}) collective-permute-start(f32[32,2,1,1024]{3,0,2,1:T(8,128)} %get-tuple-element.34), channel_id=1, source_target_pairs={{4,0},{8,4},{12,8},{16,12},{20,16},{24,20},{28,24},{32,28},{36,32}... | collective-permute-start | bytes 786440 | tf_op jit(solution)/shard_map/ppermute | solution.py:18
  84.9 8.5 %copy-start.7 = (f32[32,2,8,1024]{3,0,2,1:T(8,128)S(1)}, f32[32,2,8,1024]{3,0,2,1:T(8,128)}, u32[]{:S(2)}) copy-start(f32[32,2,8,1024]{3,0,2,1:T(8,128)} %get-tuple-element.13) | copy-start | bytes 6291460
  84.9 8.5 %copy-start.17 = (f32[2,8,1024]{2,1,0:T(8,128)S(1)}, f32[2,8,1024]{2,1,0:T(8,128)}, u32[]{:S(2)}) copy-start(f32[2,8,1024]{2,1,0:T(8,128)} %param.16) | copy-start | bytes 196612
  84.9 8.5 %copy-start.21 = (f32[2,8,1024]{2,1,0:T(8,128)S(1)}, f32[2,8,1024]{2,1,0:T(8,128)}, u32[]{:S(2)}) copy-start(f32[2,8,1024]{2,1,0:T(8,128)} %param.14) | copy-start | bytes 196612
  84.9 8.5 %copy-start.23 = (f32[2,8,1024]{2,1,0:T(8,128)S(1)}, f32[2,8,1024]{2,1,0:T(8,128)}, u32[]{:S(2)}) copy-start(f32[2,8,1024]{2,1,0:T(8,128)} %param.15) | copy-start | bytes 196612
  93.2 10.9 %collective-permute-start.16 = (f32[3,2,8,2,256]{4,3,2,1,0:T(2,128)S(1)}, f32[3,2,8,2,256]{4,3,2,1,0:T(2,128)S(1)}, u32[]{:S(2)}, u32[]{:S(2)}) collective-permute-start(f32[3,2,8,2,256]{4,3,2,1,0:T(2,128)S(1)} %bitcast.40), channel_id=1, source_target_pairs={{0,1},{1,0},{2,3},{3,2},{4,5},{5,4},{6,7},{7,6},{8,9},{9,8},{10,11... | collective-permute-start | bytes 294920 | tf_op jit(solution)/shard_map/ppermute | solution.py:24
  95.2 20.2 %copy-start.2 = (f32[32,2,8,1024]{3,2,1,0:T(8,128)S(1)}, f32[32,2,8,1024]{3,2,1,0:T(8,128)}, u32[]{:S(2)}) copy-start(f32[32,2,8,1024]{3,2,1,0:T(8,128)} %param.11) | copy-start | bytes 6291460
  95.3 20.2 %copy-start.19 = (f32[2,8,1024]{2,1,0:T(8,128)S(1)}, f32[2,8,1024]{2,1,0:T(8,128)}, u32[]{:S(2)}) copy-start(f32[2,8,1024]{2,1,0:T(8,128)} %copy-done.18) | copy-start | bytes 196612
  95.9 12.4 %collective-permute-start.11 = (f32[32,2,1,1024]{3,0,2,1:T(8,128)S(1)}, f32[32,2,1,1024]{3,0,2,1:T(8,128)S(1)}, u32[]{:S(2)}, u32[]{:S(2)}) collective-permute-start(f32[32,2,1,1024]{3,0,2,1:T(8,128)S(1)} %slice.201), channel_id=1, source_target_pairs={{4,0},{8,4},{12,8},{16,12},{20,16},{24,20},{28,24},{32,28},{36,32}... | collective-permute-start | bytes 786440 | tf_op jit(solution)/shard_map/ppermute | solution.py:49
  102.1 13.3 %collective-permute-start.10 = (f32[32,2,1,1024]{3,0,2,1:T(8,128)S(1)}, f32[32,2,1,1024]{3,0,2,1:T(8,128)S(1)}, u32[]{:S(2)}, u32[]{:S(2)}) collective-permute-start(f32[32,2,1,1024]{3,0,2,1:T(8,128)S(1)} %slice.198), channel_id=1, source_target_pairs={{0,4},{4,8},{8,12},{12,16},{16,20},{20,24},{24,28},{28,32},{32,36}... | collective-permute-start | bytes 786440 | tf_op jit(solution)/shard_map/ppermute | solution.py:49
  104.4 13.9 %collective-permute-start.17 = (f32[3,2,8,256]{3,2,1,0:T(8,128)S(1)}, f32[3,2,8,256]{3,2,1,0:T(8,128)S(1)}, u32[]{:S(2)}, u32[]{:S(2)}) collective-permute-start(f32[3,2,8,256]{3,2,1,0:T(8,128)S(1)} %bitcast.41), channel_id=1, source_target_pairs={{0,2},{1,3},{2,0},{3,1},{4,6},{5,7},{6,4},{7,5},{8,10},{9,11},{10,... | collective-permute-start | bytes 147464 | tf_op jit(solution)/shard_map/ppermute | solution.py:24
  115.4 10.0 %copy-start.26 = (f32[32]{0:T(128)S(1)}, f32[32]{0:T(128)}, u32[]{:S(2)}) copy-start(f32[32]{0:T(128)} %get-tuple-element.57) | copy-start | bytes 388
  118.2 1.3 %collective-permute-start.12 = (f32[2,8,1024]{2,1,0:T(8,128)S(1)}, f32[2,8,1024]{2,1,0:T(8,128)S(1)}, u32[]{:S(2)}, u32[]{:S(2)}) collective-permute-start(f32[2,8,1024]{2,1,0:T(8,128)S(1)} %get-tuple-element.14), channel_id=1, source_target_pairs={{0,1},{1,0},{2,3},{3,2},{4,5},{5,4},{6,7},{7,6},{8,9},{9,8},{10,11... | collective-permute-start | bytes 196616 | tf_op jit(solution)/shard_map/ppermute | solution.py:24
  119.6 5.9 %collective-permute-start.13 = (f32[2,8,1024]{2,1,0:T(8,128)S(1)}, f32[2,8,1024]{2,1,0:T(8,128)S(1)}, u32[]{:S(2)}, u32[]{:S(2)}) collective-permute-start(f32[2,8,1024]{2,1,0:T(8,128)S(1)} %add.151), channel_id=1, source_target_pairs={{0,2},{1,3},{2,0},{3,1},{4,6},{5,7},{6,4},{7,5},{8,10},{9,11},{10,... | collective-permute-start | bytes 196616 | tf_op jit(solution)/shard_map/ppermute | solution.py:24

commit v2 on v0

v2 whole, which is shorter than its diff:
```python
import functools

import jax
import jax.numpy as jnp
from jax import lax
from jax.experimental import pallas as pl
from jax.experimental.pallas import tpu as pltpu
from jax.sharding import PartitionSpec as P


COH = 128
LOG2E = 1.4426950408889634
STEP = 4
F32 = jnp.float32


def rows_of(shape):
    return lax.broadcasted_iota(jnp.int32, shape, 0)


def turn(tile, shift):
    return pltpu.roll(tile, shift, 0)


def east(tile):
    return pltpu.roll(tile, tile.shape[1] - 1, 1)


def west(tile):
    return pltpu.roll(tile, 1, 1)


def northern(first, second, halo):
    row = rows_of(first.shape)
    return (
        jnp.where(row == 7, turn(halo, 3), turn(first, 7)),
        jnp.where(row == 7, turn(halo, 1), turn(second, 7)),
    )


def southern(first, second, halo):
    row = rows_of(first.shape)
    return (
        jnp.where(row == 0, turn(halo, 7), turn(first, 1)),
        jnp.where(row == 0, turn(halo, 5), turn(second, 1)),
    )


def within(tile, shift):
    return jnp.where(rows_of(tile.shape) == (0 if shift == 1 else 7), 0.0, turn(tile, shift))


def rim(first, second):
    row = rows_of(first.shape)
    last = jnp.where(row == 4, turn(first, 5), turn(second, 7))
    return jnp.where(row == 1, turn(first, 1), jnp.where(row == 3, turn(second, 3), last))


def halo_neighbours(own, north, south):
    row = rows_of(own.shape)
    lower, upper = (row == 1) | (row == 3), (row == 4) | (row == 6)
    return jnp.where(lower, own, turn(north, 7)), jnp.where(upper, own, turn(south, 1))


def combine(inner, added):
    row = rows_of(inner.shape)
    used = (row == 1) | (row == 3) | (row == 4) | (row == 6)
    return jnp.where(used, inner, jnp.where(row < 4, turn(added, 7), turn(added, 1)))


def addends(both):
    row = rows_of(both.shape)
    return (
        jnp.where(row == 0, both, jnp.where(row == 7, turn(both, 2), 0.0)),
        jnp.where(row == 7, both, jnp.where(row == 0, turn(both, 6), 0.0)),
    )


def stay(value):
    return pltpu.with_memory_space_constraint(value, pltpu.HBM)


def decays(mortal, crowded, crowd):
    return jnp.exp2(-LOG2E * mortal - (LOG2E / COH * crowded) * crowd)


def join(before, after, out):
    out[0:4, :] = before
    out[4:8, :] = after


def pack(source, up, down, slot):
    for out, start in ((up, 6), (down, 0)):
        out[slot, 0:2, :] = source(0, start)
        out[slot, 2:4, :] = source(1, start)


def clear(*refs):
    for ref in refs:
        ref[...] = jnp.zeros_like(ref)


def nothing():
    pass


def crowd_kernel(age, mass, state, crowd):
    def begin():
        clear(crowd)

    def each(group):
        for layer in range(2):
            crowd[layer] += sum(mass[age[c]] * state[c, layer] for c in group)

    return begin, each, nothing


def edges_kernel(*refs):
    *raw, state, up, down = refs

    def begin():
        for slot, field in enumerate(raw):
            pack(lambda layer, start: field[layer, start : start + 2, :].astype(F32), up, down, state.shape[0] + slot)
        if raw:
            for out in (up, down):
                out[state.shape[0] + len(raw)] = jnp.zeros(out.shape[1:], F32)

    def each(group):
        for c in group:
            pack(lambda layer, start: state[c, layer, start : start + 2, :], up, down, c)

    return begin, each, nothing


def forward_kernel(age, mort, crowding, mass, speed, ocean, east_vel, north_vel, kappa, crowd, state,
                   state_out, rims, fields, total, sums, coef):
    def begin():
        clear(total, sums)
        for slot, (field, scale) in enumerate(((ocean, None), (east_vel, 0.5), (north_vel, 0.5), (kappa, None))):
            for layer in range(2):
                fields[slot, layer] = field[layer].astype(F32)
            if scale is not None:
                fields[slot] = scale * fields[slot]
        coef[0] = fields[0] * (1.0 - 4.0 * fields[3])
        coef[1] = fields[0] * fields[3]
        coef[2] = fields[0] * fields[1]
        coef[3] = fields[0] * fields[2]

    def each(group):
        for c in group:
            mortal, crowded, weight, swim = [table[age[c]] for table in (mort, crowding, mass, speed)]
            wet = [state[c, k] * (fields[0, k] * decays(mortal, crowded, crowd[k])) for k in range(2)]
            rims[c] = rim(*wet)
            for k in range(2):
                north, south, to_east, to_west = within(wet[k], 7), within(wet[k], 1), east(wet[k]), west(wet[k])
                around = (north + south) + (to_east + to_west)
                drift = coef[2, k] * (to_east - to_west) + coef[3, k] * (north - south)
                moved = coef[0, k] * wet[k] + coef[1, k] * around - swim * drift
                state_out[c, k] = moved
                total[k] += weight * moved
                mine = weight * wet[k]
                swum = swim * mine
                sums[0, k] += mine
                sums[1, k] += swum
                sums[2, k] += crowded * mine
                sums[3, k] += crowded * swum

    return begin, each, nothing


def forward_halo_kernel(age, mort, crowding, mass, speed, fields, total, before, after, rims,
                        both_out, wet_out, halo_fields, total_out, sums, coef, own, crowd, edge, added):
    def begin():
        clear(sums, added)
        cohorts = rims.shape[0]
        for slot, scale in enumerate((None, 0.5, 0.5, None)):
            join(before[cohorts + slot], after[cohorts + slot], edge.at[0])
            halo_fields[slot] = edge[0] if scale is None else scale * edge[0]
        ocean = halo_fields[0]
        coef[0] = ocean * (1.0 - 4.0 * halo_fields[3])
        coef[1] = ocean * halo_fields[3]
        coef[2] = ocean * halo_fields[1]
        coef[3] = ocean * halo_fields[2]
        row = rows_of(ocean.shape)
        ocean = rim(fields[0, 0], fields[0, 1])
        own[0] = ocean * rim(fields[3, 0], fields[3, 1])
        own[1] = jnp.where(row < 4, ocean, -ocean) * rim(fields[2, 0], fields[2, 1])
        join(before[cohorts + 4], after[cohorts + 4], crowd)

    def each(group):
        for slot, c in enumerate(group):
            join(before[c], after[c], edge.at[slot])
        for slot, c in enumerate(group):
            mortal, crowded, weight, swim = [table[age[c]] for table in (mort, crowding, mass, speed)]
            wet = edge[slot] * (halo_fields[0] * decays(mortal, crowded, crowd[...]))
            wet_out[c] = wet
            north, south = halo_neighbours(rims[c], wet, wet)
            to_east, to_west = east(wet), west(wet)
            around = (north + south) + (to_east + to_west)
            drift = coef[2] * (to_east - to_west) + coef[3] * (north - south)
            moved = coef[0] * wet + coef[1] * around - swim * drift
            both = combine(moved, (own[0] + swim * own[1]) * wet)
            both_out[c] = both
            added[...] += weight * both
            mine = weight * wet
            sums[0] += mine
            sums[1] += swim * mine

    def end():
        total_out[2] = added[...]
        for k, more in enumerate(addends(added[...])):
            total_out[k] = total[k] + more

    return begin, each, end


def transport_coef(fields, coef):
    coef[0] = 1.0 - 4.0 * fields[3]
    coef[1] = fields[3]
    coef[2] = fields[1]
    coef[3] = fields[2]


def pull_kernel(age, speed, fields, cotangent, pulled, rims, coef):
    def begin():
        transport_coef(fields, coef)

    def each(group):
        for c in group:
            swim = speed[age[c]]
            masked = [fields[0, k] * cotangent[c, k] for k in range(2)]
            rims[c] = rim(*masked)
            for k in range(2):
                plain = coef[1, k] * masked[k]
                along = swim * (coef[3, k] * masked[k])
                across = swim * (coef[2, k] * masked[k])
                sides = east(plain + across) + west(plain - across)
                ends = within(plain + along, 7) + within(plain - along, 1)
                pulled[c, k] = fields[0, k] * (coef[0, k] * masked[k] + (ends + sides))

    return begin, each, nothing


def pull_halo_kernel(age, speed, fields, halo_fields, before, after, rims, both_out, coef, own, edge):
    def begin():
        transport_coef(halo_fields, coef)
        row = rows_of(own.shape[1:])
        side = rim(fields[2, 0], fields[2, 1])
        own[0] = rim(fields[3, 0], fields[3, 1])
        own[1] = jnp.where(row < 4, side, -side)
        own[2] = rim(fields[0, 0], fields[0, 1])

    def each(group):
        for slot, c in enumerate(group):
            join(before[c], after[c], edge.at[slot])
        for slot, c in enumerate(group):
            swim = speed[age[c]]
            masked = halo_fields[0] * edge[slot]
            plain = coef[1] * masked
            along = swim * (coef[3] * masked)
            across = swim * (coef[2] * masked)
            onward, backward = plain + along, plain - along
            sides = east(plain + across) + west(plain - across)
            north, south = halo_neighbours((own[0] + swim * own[1]) * rims[c], onward, backward)
            grad = coef[0] * masked + ((north + south) + sides)
            more = jnp.where(rows_of(grad.shape) < 4, backward, onward)
            both_out[c] = combine(halo_fields[0] * grad, own[2] * more)

    return begin, each, nothing


def whole_tiles(tiles, both, c):
    more = addends(both[c])
    return [tiles[c, 0] + more[0], tiles[c, 1] + more[1], both[c]]


def backward_kernel(age, mort, crowding, speed, fields, halo_fields, crowd, crowd_two, sums, pulled, pulled_both, state,
                    state_both, start, partial, totals, coef):
    pressure, later = totals.at[0:3], totals.at[3:5]

    def begin():
        for k in range(4):
            totals[5 + k] = sums[2 + k // 2, k % 2]
        for k in range(3):
            field = lambda n: fields[n, k] if k < 2 else halo_fields[n]
            coef[0, k] = 1.0 - 4.0 * field(3)
            coef[1, k] = field(3)
            coef[2, k] = field(1)
            coef[3, k] = field(2)
        clear(pressure, later)

    def each(group):
        for c in group:
            mortal, crowded, swim = [table[age[c]] for table in (mort, crowding, speed)]
            grad, now = whole_tiles(pulled, pulled_both, c), whole_tiles(state, state_both, c)
            value = []
            for k in range(3):
                value.append(grad[k] * decays(mortal, crowded, crowd_two[k]))
                pressure[k] -= crowded * (value[k] * now[k])
            plain = [coef[1, k] * value[k] for k in range(3)]
            along = [swim * (coef[3, k] * value[k]) for k in range(3)]
            north = northern(*[plain[k] + along[k] for k in range(3)])
            south = southern(*[plain[k] - along[k] for k in range(3)])
            for k in range(2):
                across = swim * (coef[2, k] * value[k])
                sides = east(plain[k] + across) + west(plain[k] - across)
                spread = coef[0, k] * value[k] + ((north[k] + south[k]) + sides)
                mine = (fields[0, k] * decays(mortal, crowded, crowd[k])) * spread
                partial[c, k] = mine
                later[k] -= crowded * (start[c, k] * mine)

    return begin, each, nothing


def shares_kernel(age, mort, crowding, speed, fields, crowd, crowd_two, sums, halo_sums, cotangent, pulled, pulled_both, start,
                  wet_halo, state, state_both, shares):
    def begin():
        clear(shares)
        plain, swum = [[sums[n, 0], sums[n, 1], halo_sums[n]] for n in range(2)]
        plain_north, plain_south = northern(*plain), southern(*plain)
        swum_north, swum_south = northern(*swum), southern(*swum)
        for k in range(2):
            ocean = fields[0, k]
            shares[3, k] = (-0.5 * ocean) * (east(swum[k]) - west(swum[k]))
            shares[4, k] = (-0.5 * ocean) * (swum_north[k] - swum_south[k])
            around = plain_north[k] + plain_south[k] + east(plain[k]) + west(plain[k])
            shares[5, k] = ocean * (around - 4.0 * plain[k])

    def each(group):
        for c in group:
            mortal, crowded, swim = [table[age[c]] for table in (mort, crowding, speed)]
            old = [start[c, k] * (fields[0, k] * decays(mortal, crowded, crowd[k])) for k in range(2)] + [wet_halo[c]]
            fade = [decays(mortal, crowded, crowd_two[k]) for k in range(3)]
            new = [tile * fade[k] for k, tile in enumerate(whole_tiles(state, state_both, c))]
            grad = whole_tiles(pulled, pulled_both, c)
            for wet, weigh in ((old, lambda k: grad[k] * fade[k]), (new, lambda k: fields[0, k] * cotangent[c, k])):
                north, south = northern(*wet), southern(*wet)
                for k in range(2):
                    by = weigh(k)
                    to_east, to_west = east(wet[k]), west(wet[k])
                    pace = (-0.5 * swim) * by
                    shares[0, k] += pace * (to_east - to_west)
                    shares[1, k] += pace * (north[k] - south[k])
                    shares[2, k] += by * ((north[k] + south[k]) + (to_east + to_west) - 4.0 * wet[k])

    return begin, each, nothing


def last_kernel(age, mort, crowding, mass, speed, totals, fields, halo_fields, crowd, partial, out, terms):
    pressure = totals.at[0:3]

    def begin():
        field = lambda n, k: fields[n, k] if k < 2 else halo_fields[n]
        value = [field(0, k) * (pressure[k] * (1.0 / COH)) for k in range(3)]
        plain = [field(3, k) * value[k] for k in range(3)]
        along = [field(2, k) * value[k] for k in range(3)]
        north, south = northern(*plain), southern(*plain)
        drift_north, drift_south = northern(*along), southern(*along)
        for k in range(2):
            across = fields[1, k] * value[k]
            still = (1.0 - 4.0 * fields[3, k]) * value[k]
            still += (north[k] + south[k]) + (east(plain[k]) + west(plain[k]))
            moving = (drift_north[k] - drift_south[k]) + (east(across) - west(across))
            terms[0, k] = fields[0, k] * still
            terms[1, k] = fields[0, k] * moving
            terms[2, k] = (totals[3 + k] - totals[5 + k] * still - totals[7 + k] * moving) * (1.0 / COH)

    def each(group):
        for c in group:
            mortal, crowded, weight, swim = [table[age[c]] for table in (mort, crowding, mass, speed)]
            for k in range(2):
                term = decays(mortal, crowded, crowd[k]) * (terms[0, k] + swim * terms[1, k]) + terms[2, k]
                out[c, k] = partial[c, k] + weight * term

    return begin, each, nothing


def driver(kernel, cohorts, sides, n_small, n_in, n_out, n_whole, n_scratch, *refs):
    refs = list(refs)

    def take(count):
        taken, refs[:] = refs[:count], refs[count:]
        return taken

    small, sources, sinks, wholes, scratch = take(n_small), take(n_in), take(n_out), take(n_whole), take(n_scratch)
    inside, outside = take(n_in), take(n_out)
    groups = cohorts // STEP

    def span(group):
        return pl.ds(pl.multiple_of(group * STEP, STEP) if not isinstance(group, int) else group * STEP, STEP)

    def loads(group):
        return [pltpu.make_async_copy(a.at[span(group)], b.at[span(group)], refs[0].at[n, group])
                for n, (a, b) in enumerate(zip(sources, inside))]

    def stores(group):
        return [pltpu.make_async_copy(b.at[span(group)], a.at[span(group)], refs[-1].at[n, group])
                for n, (a, b) in enumerate(zip(sinks, outside))]

    for group in range(groups):
        for copy in loads(group):
            copy.start()

    def run(arrays):
        begin, each, end = kernel(*arrays)
        begin()

        def step(group, _):
            for copy in loads(group):
                copy.wait()
            each([group * STEP + slot for slot in range(STEP)])
            for copy in stores(group):
                copy.start()
            return 0

        lax.fori_loop(0, groups, step, 0)
        end()

    arrays = small + inside + outside + wholes + scratch
    if sides is None:
        run(arrays)
    else:
        even, arrays = arrays[0], arrays[1:]
        turned = list(arrays)
        turned[sides], turned[sides + 1] = arrays[sides + 1], arrays[sides]

        @pl.when(even[0] == 1)
        def _():
            run(turned if sides < n_small else arrays)

        @pl.when(even[0] == 0)
        def _():
            run(arrays if sides < n_small else turned)

    for group in range(groups):
        for copy in stores(group):
            copy.wait()


SMEM = pl.BlockSpec(memory_space=pltpu.SMEM)
VMEM = pl.BlockSpec(memory_space=pltpu.VMEM)
LARGE = pl.BlockSpec(memory_space=pl.ANY)


def call(kernel, tables, small, large, large_outs, outs, scratch, cycles, sides=None):
    cohorts = large[0].shape[0]
    groups = cohorts // STEP
    vmem = lambda shape: pltpu.VMEM(shape, F32)
    sems = [pltpu.SemaphoreType.DMA((len(arrays), groups)) for arrays in (large, large_outs) if arrays]
    outputs = pl.pallas_call(
        functools.partial(driver, kernel, cohorts, sides, len(tables) + len(small), len(large), len(large_outs), len(outs), len(scratch)),
        in_specs=[SMEM] * len(tables) + [VMEM] * len(small) + [LARGE] * len(large),
        out_specs=[LARGE] * len(large_outs) + [VMEM] * len(outs),
        out_shape=[pltpu.HBM(shape, F32) for shape in large_outs] + [jax.ShapeDtypeStruct(shape, F32) for shape in outs],
        scratch_shapes=[vmem(shape) for shape in scratch] + [vmem(x.shape) for x in large]
        + [vmem(shape) for shape in large_outs] + sems,
        compiler_params=pltpu.CompilerParams(vmem_limit_bytes=32 << 20),
        cost_estimate=pl.CostEstimate(flops=cycles, transcendentals=0, bytes_accessed=cycles),
    )(*tables, *small, *[stay(x) for x in large])
    count = len(large_outs)
    return [stay(x) for x in outputs[:count]] + list(outputs[count:])


def swap(value, flip):
    return lax.ppermute(value, "coh", [(i, i ^ flip) for i in range(4)])


def total_of(value):
    value = value + swap(value, 1)
    return value + swap(value, 2)


def halves(value, side):
    middle = value.shape[-1] // 2
    low, high = value[..., :middle], value[..., middle:]
    return jnp.where(side == 0, low, high), jnp.where(side == 0, high, low)


def total_by_halves(value):
    side = lax.axis_index("coh") % 2
    keep, send = halves(value, side)
    keep = keep + swap(send, 1)
    keep = keep + swap(keep, 2)
    other = swap(keep, 1)
    return jnp.where(side == 0, jnp.concatenate([keep, other], -1), jnp.concatenate([other, keep], -1))


def quarter(value):
    side, block = lax.axis_index("coh") % 2, lax.axis_index("coh") // 2
    fourth = value.shape[-1] // 4
    parts = [value[..., k * fourth : (k + 1) * fourth] for k in range(4)]
    keep = [jnp.where(side == 0, parts[2 * k], parts[2 * k + 1]) for k in range(2)]
    send = [jnp.where(side == 0, parts[2 * k + 1], parts[2 * k]) for k in range(2)]
    return keep, send, block


def scatter(value):
    keep, send, block = quarter(value)
    got = swap(jnp.stack(send), 1)
    keep = [keep[0] + got[0], keep[1] + got[1]]
    mine = jnp.where(block == 0, keep[0], keep[1])
    rest = jnp.where(block == 0, keep[1], keep[0])
    return mine + swap(rest, 2)


def near_swap(value, count):
    return lax.ppermute(value, "lat", [(i, i ^ 1) for i in range(count)])


def far_swap(value, count):
    return lax.ppermute(value, "lat", [(i, ((i + 1) ^ 1) - 1) for i in range(1, count - 1)])


def local(density, cotangent, land_mask, east_vel, north_vel, diffusion, age_class, mort_rate, crowd_coef, mass, speed):
    age_class, mort_rate, crowd_coef, mass, speed = [stay(x) for x in (age_class, mort_rate, crowd_coef, mass, speed)]
    raw_fields = [stay(x) for x in (land_mask, east_vel, north_vel, diffusion)]
    count = lax.axis_size("lat")
    odd = lax.axis_index("lat") % 2
    even = (1 - odd).astype(jnp.int32)[None]
    cohorts, _, height, lon = density.shape
    main, halo, edge = (cohorts, 2, height, lon), (cohorts, height, lon), (cohorts, 4, lon)
    tiles, three, fields_shape = (2, height, lon), (3, height, lon), (4, 3, height, lon)

    wide = (cohorts + 5, 4, lon)
    (crowd,) = call(crowd_kernel, [age_class, mass], [], [density], [], [tiles], [], 2000)
    crowd = total_of(crowd)
    near, far = call(edges_kernel, [even], raw_fields, [density], [], [wide, wide], [], 2000, sides=len(raw_fields) + 1)
    late_near, late_far = call(edges_kernel, [even], [], [cotangent], [], [edge, edge], [], 2000, sides=1)

    def edge_rows(value, start):
        return value[:, start : start + 2].reshape(4, lon)

    up, down = edge_rows(crowd, height - 2), edge_rows(crowd, 0)
    far = far.at[cohorts + 4].set(jnp.where(odd == 1, up, down))
    near = near.at[cohorts + 4].set(jnp.where(odd == 1, down, up))
    far = far_swap(far, count)
    near = near_swap(near, count)
    late_far = far_swap(late_far, count)
    late_near = near_swap(late_near, count)

    tables = [age_class, mort_rate, crowd_coef, mass, speed]
    own_fields, halo_fields_shape = (4,) + tiles, (4, height, lon)
    state, rims, fields, crowd_two, sums = call(
        forward_kernel, tables, raw_fields + [crowd], [density],
        [main, halo], [own_fields, tiles, (4,) + tiles], [own_fields], 4000)
    pulled, late_rims = call(
        pull_kernel, [age_class, speed], [fields], [cotangent], [main, halo], [], [own_fields], 4000)
    state_both, wet_halo, halo_fields, crowd_two, halo_sums = call(
        forward_halo_kernel, [even] + tables, [fields, crowd_two, near, far], [rims],
        [halo, halo], [halo_fields_shape, three, (2, height, lon)],
        [halo_fields_shape, (2, height, lon), (height, lon), (STEP, height, lon), (height, lon)], 2500, sides=7)
    crowd_two = total_of(crowd_two)
    (pulled_both,) = call(
        pull_halo_kernel, [even, age_class, speed], [fields, halo_fields, late_near, late_far], [late_rims],
        [halo], [], [halo_fields_shape, (3, height, lon), (STEP, height, lon)], 2500, sides=4)

    tables = [age_class, mort_rate, crowd_coef, speed]
    partial, totals = call(
        backward_kernel, tables, [fields, halo_fields, crowd, crowd_two, sums],
        [pulled, pulled_both, state, state_both, density], [main], [(9, height, lon)], [fields_shape], 5000)
    totals = total_by_halves(totals)

    (shares,) = call(
        shares_kernel, tables, [fields, crowd, crowd_two, sums, halo_sums],
        [cotangent, pulled, pulled_both, density, wet_halo, state, state_both], [], [(6,) + tiles], [], 6000)
    shares = scatter(shares)

    (grad,) = call(
        last_kernel, [age_class, mort_rate, crowd_coef, mass, speed],
        [totals, fields, halo_fields, crowd], [partial], [main], [], [(3,) + tiles], 3000)

    fourth = lon // 4
    mine = lax.dynamic_slice_in_dim(totals[:2], lax.axis_index("coh") * fourth, fourth, axis=2)
    shares = shares[:3] + shares[3:] * (mine * (1.0 / COH))[None]
    return (grad, shares[0], shares[1], shares[2])


def solution(mesh):
    spread_spec = P("coh", None, "lat", None)
    field_spec = P(None, "lat", None)
    in_specs = (spread_spec, spread_spec) + (field_spec,) * 4 + (P("coh"),) + (P(),) * 4
    out_specs = (spread_spec,) + (P(None, "lat", "coh"),) * 3
    return jax.shard_map(local, mesh=mesh, in_specs=in_specs, out_specs=out_specs, check_vma=False)
```

time: 389 us -> 81.2 us (0.21)
  waiting for transfers between devices: 273 us -> 11.2 us
  Pallas kernels: 0 us -> 42.9 us
  other arithmetic: 43 us -> 0.28 us
  local copies, waits for them, and re-layouts: 22.4 us -> 1.28 us
  between operations: 14.7 us -> 0.91 us
  starting transfers between devices: 33.9 us -> 23.8 us
    psum x4 -> x0, waiting for transfers between devices: 157 us -> none  [the longest x2 84.2 us: local(): crowd = lax.psum(jnp.sum(weight * state, axis=0), 'coh') / COH]
    reduce_scatter x3 -> x0, waiting for transfers between devices: 98.8 us -> none  [the longest x1 34.3 us: local(): lax.psum_scatter(grad_kappa, 'coh', scatter_dimension=2, tiled=True)]
    pallas_call x0 -> x10, Pallas kernels: none -> 42.9 us  [call(): pl.pallas_call(functools.partial(driver, kernel, cohorts, sides, len(tabl...]
    reduce_sum x5 -> x0, other arithmetic: 21.6 us -> none  [the longest x2 9.98 us: local(): grad_kappa = jnp.sum(masked * laplace, axis=0)]
    slice x12 -> x1, local copies, waits for them, and re-layouts: 13.6 us -> 0.01 us  [local(): totals[:2]]
    mul x3 -> x1, other arithmetic: 10.1 us -> 0.01 us  [local(): shares = shares[:3] + shares[3:] * (mine * (1.0 / COH))[None]]
    ppermute x8 -> x13, starting transfers between devices: 33.6 us -> 23.8 us  [the longest x2 11.2 us: far_swap(): lax.ppermute(value, 'lat', [(i, (i + 1 ^ 1) - 1) for i in range(1, count...]
    unnamed x69 -> x0, local copies, waits for them, and re-layouts: 7.11 us -> none
  transfers between devices with their start and end apart: 15 -> 13, of which waited for: 11 -> 7; matrix products, arithmetic and copies ran while one was open for 7% -> 0% of each run, Pallas kernels for 0% -> 38%
where the time goes in v2:
time: 81.2 us; the launch traced here: 80.4 us
  Pallas kernels  42.9 us (53%)
  starting transfers between devices  23.8 us (29%)
  waiting for transfers between devices  11.2 us (14%)
  local copies, waits for them, and re-layouts  1.28 us (2%)
  between operations  0.91 us (1%)
    pallas_call x10, Pallas kernels, call(): pl.pallas_call(functools.partial(driver, kernel, cohorts, sides, len(tabl...  42.9 us
    ppermute x2, starting transfers between devices, far_swap(): lax.ppermute(value, 'lat', [(i, (i + 1 ^ 1) - 1) for i in range(1, count...  11.2 us
    ppermute x9, starting transfers between devices, swap(): return lax.ppermute(value, 'coh', [(i, i ^ flip) for i in range(4)])  10.6 us
    ppermute x9, waiting for transfers between devices, swap(): return lax.ppermute(value, 'coh', [(i, i ^ flip) for i in range(4)])  8.74 us
    ppermute x2, waiting for transfers between devices, far_swap(): lax.ppermute(value, 'lat', [(i, (i + 1 ^ 1) - 1) for i in range(1, count...  2.47 us
    ppermute x2, starting transfers between devices, near_swap(): return lax.ppermute(value, 'lat', [(i, i ^ 1) for i in range(count)])  2 us
  transfers between devices with their start and end apart: 13, of which 7 were waited for; matrix products, arithmetic and copies ran while one was open for 0% of the time, Pallas kernels for 38%

profile of v2, /device:TPU:6, one launch (start us, length us, event | category | flops | bytes accessed | tf_op | source)
XLA Modules:
  0.0 80.4 jit_solution(14126325773842346822)
XLA Ops:
  0.6 2.3 %shard_map.138 = f32[2,8,1024]{2,1,0:T(8,128)S(1)} custom-call(s32[32]{0:T(128)} %refs_0_.11, f32[32]{0:T(128)} %refs_3_.12, f32[32,2,8,1024]{3,2,1,0:T(8,128)} %refs_12_.1), custom_call_target="tpu_custom_call" | custom-call | flops 2000 | bytes 2000 | tf_op jit(solution)/shard_map/pallas_call | solution.py:450
  2.9 0.1 collective-permute-start
  3.0 1.2 %collective-permute-done = f32[2,8,1024]{2,1,0:T(8,128)S(1)} collective-permute-done((f32[2,8,1024]{2,1,0:T(8,128)S(1)}, f32[2,8,1024]{2,1,0:T(8,128)S(1)}, u32[]{:S(2)}, u32[]{:S(2)}) %collective-permute-start) | collective-permute-done | bytes 65568 | tf_op jit(solution)/shard_map/ppermute | solution.py:465
  4.3 3.3 %collective-permute-start.1 = (f32[2,8,1024]{2,1,0:T(8,128)S(1)}, f32[2,8,1024]{2,1,0:T(8,128)S(1)}, u32[]{:S(2)}, u32[]{:S(2)}) collective-permute-start(f32[2,8,1024]{2,1,0:T(8,128)S(1)} %add.47), channel_id=1, source_target_pairs={{0,2},{1,3},{2,0},{3,1},{4,6},{5,7},{6,4},{7,5},{8,10},{9,11},{10,... | collective-permute-start | bytes 196616 | tf_op jit(solution)/shard_map/ppermute | solution.py:465
  7.5 3.4 %shard_map.140 = (f32[37,4,1024]{2,1,0:T(4,128)}, f32[37,4,1024]{2,1,0:T(4,128)S(1)}) custom-call(s32[1]{0:T(128)} %bitcast.refs_0_, s32[2,8,1024]{2,1,0:T(8,128)} %refs_1_.12, f32[2,8,1024]{2,1,0:T(8,128)} %refs_2_.10, f32[2,8,1024]{2,1,0:T(8,128)} %refs_3_.8, f32[2,8,1024]{2,1,0:T(8,128)} %refs_4_.5, f32[32,2,8,1024]{3,2,1,0:T(8,128)} %refs_12_.1), custom_call_target="tpu_custom_call" | custom-call | flops 2000 | bytes 2000 | tf_op jit(solution)/shard_map/pallas_call | solution.py:450
  10.9 0.0 collective-permute-done.1
  11.0 0.6 constant_dynamic-update-slice_fusion.1
  11.6 1.9 %collective-permute-start.2 = (f32[37,4,1024]{2,1,0:T(4,128)}, f32[37,4,1024]{2,1,0:T(4,128)S(1)}, u32[]{:S(2)}, u32[]{:S(2)}) collective-permute-start(f32[37,4,1024]{2,1,0:T(4,128)} %constant_dynamic-update-slice_fusion.1), channel_id=1, source_target_pairs={{0,4},{4,0},{8,12},{12,8},{16,20},{20,16},{24,28},{28,24},{32,36},... | collective-permute-start | bytes 1818632 | tf_op jit(solution)/shard_map/ppermute | solution.py:507
  13.6 7.3 %collective-permute-start.3 = (f32[37,4,1024]{2,1,0:T(4,128)S(1)}, f32[37,4,1024]{2,1,0:T(4,128)S(1)}, u32[]{:S(2)}, u32[]{:S(2)}) collective-permute-start(f32[37,4,1024]{2,1,0:T(4,128)S(1)} %constant_dynamic-update-slice_fusion), channel_id=1, source_target_pairs={{4,8},{8,4},{12,16},{16,12},{20,24},{24,20},{28,32},{32,28},{36,40... | collective-permute-start | bytes 1818632 | tf_op jit(solution)/shard_map/ppermute | solution.py:511
  20.9 2.4 %shard_map.143 = (f32[32,4,1024]{2,1,0:T(4,128)}, f32[32,4,1024]{2,1,0:T(4,128)S(1)}) custom-call(s32[1]{0:T(128)} %bitcast.refs_0_, f32[32,2,8,1024]{3,2,1,0:T(8,128)} %refs_9_.1), custom_call_target="tpu_custom_call" | custom-call | flops 2000 | bytes 2000 | tf_op jit(solution)/shard_map/pallas_call | solution.py:450
  23.3 0.1 collective-permute-start.6
  23.4 3.9 %collective-permute-start.7 = (f32[32,4,1024]{2,1,0:T(4,128)S(1)}, f32[32,4,1024]{2,1,0:T(4,128)S(1)}, u32[]{:S(2)}, u32[]{:S(2)}) collective-permute-start(f32[32,4,1024]{2,1,0:T(4,128)S(1)} %get-tuple-element.56), channel_id=1, source_target_pairs={{4,8},{8,4},{12,16},{16,12},{20,24},{24,20},{28,32},{32,28},{36,40... | collective-permute-start | bytes 1572872 | tf_op jit(solution)/shard_map/ppermute | solution.py:511
  27.3 5.6 %shard_map.139 = (f32[32,2,8,1024]{3,2,1,0:T(8,128)}, f32[32,8,1024]{2,1,0:T(8,128)}, f32[4,2,8,1024]{3,2,1,0:T(8,128)S(1)}, f32[2,8,1024]{2,1,0:T(8,128)S(1)}, f32[4,2,8,1024]{3,2,1,0:T(8,128)S(1)}) custom-call(s32[32]{0:T(128)} %refs_0_.11, f32[32]{0:T(128)} %refs_1_.19, f32[32]{0:T(128)} %refs_2_.15, f32[32]{0:T(128)} %refs_3_.12, f32[32]{0:T(128)} %refs_3_.13, ...), custom_call_target="tpu_custom_call" | custom-call | flops 4000 | bytes 4000 | tf_op jit(solution)/shard_map/pallas_call | solution.py:450
  32.9 0.0 collective-permute-done.2.refs_8_
  32.9 2.5 %collective-permute-done.3.refs_9_ = f32[37,4,1024]{2,1,0:T(4,128)S(1)} collective-permute-done((f32[37,4,1024]{2,1,0:T(4,128)S(1)}, f32[37,4,1024]{2,1,0:T(4,128)S(1)}, u32[]{:S(2)}, u32[]{:S(2)}) %collective-permute-start.3) | collective-permute-done | bytes 606240 | tf_op jit(solution)/shard_map/ppermute | solution.py:511
  35.4 4.0 %shard_map.141 = (f32[32,8,1024]{2,1,0:T(8,128)}, f32[32,8,1024]{2,1,0:T(8,128)}, f32[4,8,1024]{2,1,0:T(8,128)S(1)}, f32[3,8,1024]{2,1,0:T(8,128)S(1)}, f32[2,8,1024]{2,1,0:T(8,128)S(1)}) custom-call(s32[1]{0:T(128)} %bitcast.refs_0_, s32[32]{0:T(128)} %refs_0_.11, f32[32]{0:T(128)} %refs_1_.19, f32[32]{0:T(128)} %refs_2_.15, f32[32]{0:T(128)} %refs_3_.12, ...), custom_call_target="tpu_custom_call" | custom-call | flops 2500 | bytes 2500 | tf_op jit(solution)/shard_map/pallas_call | solution.py:450
  39.4 0.1 collective-permute-start.4
  39.5 1.3 %collective-permute-done.4 = f32[3,8,1024]{2,1,0:T(8,128)S(1)} collective-permute-done((f32[3,8,1024]{2,1,0:T(8,128)S(1)}, f32[3,8,1024]{2,1,0:T(8,128)S(1)}, u32[]{:S(2)}, u32[]{:S(2)}) %collective-permute-start.4) | collective-permute-done | bytes 98336 | tf_op jit(solution)/shard_map/ppermute | solution.py:465
  40.8 3.0 %collective-permute-start.5 = (f32[3,8,1024]{2,1,0:T(8,128)S(1)}, f32[3,8,1024]{2,1,0:T(8,128)S(1)}, u32[]{:S(2)}, u32[]{:S(2)}) collective-permute-start(f32[3,8,1024]{2,1,0:T(8,128)S(1)} %add.50), channel_id=1, source_target_pairs={{0,2},{1,3},{2,0},{3,1},{4,6},{5,7},{6,4},{7,5},{8,10},{9,11},{10,... | collective-permute-start | bytes 294920 | tf_op jit(solution)/shard_map/ppermute | solution.py:465
  43.8 4.5 %shard_map.142 = (f32[32,2,8,1024]{3,2,1,0:T(8,128)}, f32[32,8,1024]{2,1,0:T(8,128)}) custom-call(s32[32]{0:T(128)} %refs_0_.11, f32[32]{0:T(128)} %refs_3_.13, f32[4,2,8,1024]{3,2,1,0:T(8,128)S(1)} %get-tuple-element.46.refs_6_.refs_2_.refs_3_.refs_4_, f32[32,2,8,1024]{3,2,1,0:T(8,128)} %refs_9_.1), custom_call_target="tpu_custom_call" | custom-call | flops 4000 | bytes 4000 | tf_op jit(solution)/shard_map/pallas_call | solution.py:450
  48.3 0.0 collective-permute-done.6.refs_5_
  48.3 0.0 collective-permute-done.7.refs_6_
  48.3 3.7 %shard_map.144.refs_10_.refs_11_ = f32[32,8,1024]{2,1,0:T(8,128)} custom-call(s32[1]{0:T(128)} %bitcast.refs_0_, s32[32]{0:T(128)} %refs_0_.11, f32[32]{0:T(128)} %refs_3_.13, f32[4,2,8,1024]{3,2,1,0:T(8,128)S(1)} %get-tuple-element.46.refs_6_.refs_2_.refs_3_.refs_4_, f32[4,8,1024]{2,1,0:T(8,128)S(1)} %get-tuple-element.51.refs_4_.refs_5_.refs_7_, ...), custom_call_target="tpu_custom_call" | custom-call | flops 2500 | bytes 2500 | tf_op jit(solution)/shard_map/pallas_call | solution.py:450
  52.0 0.0 collective-permute-done.5
  52.0 6.7 %shard_map.145 = (f32[32,2,8,1024]{3,2,1,0:T(8,128)}, f32[9,8,1024]{2,1,0:T(8,128)S(1)}) custom-call(s32[32]{0:T(128)} %refs_0_.11, f32[32]{0:T(128)} %refs_1_.19, f32[32]{0:T(128)} %refs_2_.15, f32[32]{0:T(128)} %refs_3_.13, f32[4,2,8,1024]{3,2,1,0:T(8,128)S(1)} %get-tuple-element.46.refs_6_.refs_2_.refs_3_.refs_4_, ...), custom_call_target="tpu_custom_call" | custom-call | flops 5000 | bytes 5000 | tf_op jit(solution)/shard_map/pallas_call | solution.py:450
  58.8 0.1 collective-permute-start.8
  58.9 7.2 %shard_map.147 = f32[6,2,8,1024]{3,2,1,0:T(8,128)S(1)} custom-call(s32[32]{0:T(128)} %refs_0_.11, f32[32]{0:T(128)} %refs_1_.19, f32[32]{0:T(128)} %refs_2_.15, f32[32]{0:T(128)} %refs_3_.13, f32[4,2,8,1024]{3,2,1,0:T(8,128)S(1)} %get-tuple-element.46.refs_6_.refs_2_.refs_3_.refs_4_, f32[2,8,1024]{2,1,0:T(8,128)S(1)} %add.48.refs_9_.refs_6_.refs_8_.refs_5_, ...), custom_call_target="tpu_custom_call" | custom-call | flops 6000 | bytes 6000 | tf_op jit(solution)/shard_map/pallas_call | solution.py:450
  66.1 0.6 collective-permute-start.11
  66.7 0.0 collective-permute-done.8
  66.7 0.7 collective-permute-start.9
  67.4 0.3 collective-permute-done.11
  67.8 2.7 %collective-permute-start.12 = (f32[6,2,8,256]{3,2,1,0:T(8,128)S(1)}, f32[6,2,8,256]{3,2,1,0:T(8,128)S(1)}, u32[]{:S(2)}, u32[]{:S(2)}) collective-permute-start(f32[6,2,8,256]{3,2,1,0:T(8,128)S(1)} %get-tuple-element.64), channel_id=1, source_target_pairs={{0,2},{1,3},{2,0},{3,1},{4,6},{5,7},{6,4},{7,5},{8,10},{9,11},{10,... | collective-permute-start | bytes 294920 | tf_op jit(solution)/shard_map/ppermute | solution.py:465
  70.4 4.6 %collective-permute-done.9 = f32[9,8,512]{2,1,0:T(8,128)S(1)} collective-permute-done((f32[9,8,512]{2,1,0:T(8,128)S(1)}, f32[9,8,512]{2,1,0:T(8,128)S(1)}, u32[]{:S(2)}, u32[]{:S(2)}) %collective-permute-start.9) | collective-permute-done | bytes 147488 | tf_op jit(solution)/shard_map/ppermute | solution.py:465
  75.0 0.1 collective-permute-start.10
  75.1 1.0 %collective-permute-done.12 = f32[6,2,8,256]{3,2,1,0:T(8,128)S(1)} collective-permute-done((f32[6,2,8,256]{3,2,1,0:T(8,128)S(1)}, f32[6,2,8,256]{3,2,1,0:T(8,128)S(1)}, u32[]{:S(2)}, u32[]{:S(2)}) %collective-permute-start.12) | collective-permute-done | bytes 98336 | tf_op jit(solution)/shard_map/ppermute | solution.py:465
  76.2 0.3 collective-permute-done.10
  76.6 0.6 slice_bitcast_fusion.2
  77.2 3.2 %shard_map.146 = f32[32,2,8,1024]{3,2,1,0:T(8,128)} custom-call(s32[32]{0:T(128)} %refs_0_.11, f32[32]{0:T(128)} %refs_1_.19, f32[32]{0:T(128)} %refs_2_.15, f32[32]{0:T(128)} %refs_3_.12, f32[32]{0:T(128)} %refs_3_.13, f32[9,8,1024]{2,1,0:T(8,128)S(1)} %maximum_select_fusion.refs_5_, ...), custom_call_target="tpu_custom_call" | custom-call | flops 3000 | bytes 3000 | tf_op jit(solution)/shard_map/pallas_call | solution.py:450
  (19 shorter events, 0.3 us)
Async XLA Ops:
  2.9 1.3 %collective-permute-start = (f32[2,8,1024]{2,1,0:T(8,128)S(1)}, f32[2,8,1024]{2,1,0:T(8,128)S(1)}, u32[]{:S(2)}, u32[]{:S(2)}) collective-permute-start(f32[2,8,1024]{2,1,0:T(8,128)S(1)} %shard_map.138), channel_id=1, source_target_pairs={{0,1},{1,0},{2,3},{3,2},{4,5},{5,4},{6,7},{7,6},{8,9},{9,8},{10,11... | collective-permute-start | bytes 196616 | tf_op jit(solution)/shard_map/ppermute | solution.py:465
  4.3 6.7 %collective-permute-start.1 = (f32[2,8,1024]{2,1,0:T(8,128)S(1)}, f32[2,8,1024]{2,1,0:T(8,128)S(1)}, u32[]{:S(2)}, u32[]{:S(2)}) collective-permute-start(f32[2,8,1024]{2,1,0:T(8,128)S(1)} %add.47), channel_id=1, source_target_pairs={{0,2},{1,3},{2,0},{3,1},{4,6},{5,7},{6,4},{7,5},{8,10},{9,11},{10,... | collective-permute-start | bytes 196616 | tf_op jit(solution)/shard_map/ppermute | solution.py:465
  11.6 21.3 %collective-permute-start.2 = (f32[37,4,1024]{2,1,0:T(4,128)}, f32[37,4,1024]{2,1,0:T(4,128)S(1)}, u32[]{:S(2)}, u32[]{:S(2)}) collective-permute-start(f32[37,4,1024]{2,1,0:T(4,128)} %constant_dynamic-update-slice_fusion.1), channel_id=1, source_target_pairs={{0,4},{4,0},{8,12},{12,8},{16,20},{20,16},{24,28},{28,24},{32,36},... | collective-permute-start | bytes 1818632 | tf_op jit(solution)/shard_map/ppermute | solution.py:507
  13.6 21.8 %collective-permute-start.3 = (f32[37,4,1024]{2,1,0:T(4,128)S(1)}, f32[37,4,1024]{2,1,0:T(4,128)S(1)}, u32[]{:S(2)}, u32[]{:S(2)}) collective-permute-start(f32[37,4,1024]{2,1,0:T(4,128)S(1)} %constant_dynamic-update-slice_fusion), channel_id=1, source_target_pairs={{4,8},{8,4},{12,16},{16,12},{20,24},{24,20},{28,32},{32,28},{36,40... | collective-permute-start | bytes 1818632 | tf_op jit(solution)/shard_map/ppermute | solution.py:511
  23.3 25.0 %collective-permute-start.6 = (f32[32,4,1024]{2,1,0:T(4,128)}, f32[32,4,1024]{2,1,0:T(4,128)S(1)}, u32[]{:S(2)}, u32[]{:S(2)}) collective-permute-start(f32[32,4,1024]{2,1,0:T(4,128)} %get-tuple-element.55), channel_id=1, source_target_pairs={{0,4},{4,0},{8,12},{12,8},{16,20},{20,16},{24,28},{28,24},{32,36},... | collective-permute-start | bytes 1572872 | tf_op jit(solution)/shard_map/ppermute | solution.py:507
  23.4 24.9 %collective-permute-start.7 = (f32[32,4,1024]{2,1,0:T(4,128)S(1)}, f32[32,4,1024]{2,1,0:T(4,128)S(1)}, u32[]{:S(2)}, u32[]{:S(2)}) collective-permute-start(f32[32,4,1024]{2,1,0:T(4,128)S(1)} %get-tuple-element.56), channel_id=1, source_target_pairs={{4,8},{8,4},{12,16},{16,12},{20,24},{24,20},{28,32},{32,28},{36,40... | collective-permute-start | bytes 1572872 | tf_op jit(solution)/shard_map/ppermute | solution.py:511
  39.4 1.4 %collective-permute-start.4 = (f32[3,8,1024]{2,1,0:T(8,128)S(1)}, f32[3,8,1024]{2,1,0:T(8,128)S(1)}, u32[]{:S(2)}, u32[]{:S(2)}) collective-permute-start(f32[3,8,1024]{2,1,0:T(8,128)S(1)} %get-tuple-element.52), channel_id=1, source_target_pairs={{0,1},{1,0},{2,3},{3,2},{4,5},{5,4},{6,7},{7,6},{8,9},{9,8},{10,11... | collective-permute-start | bytes 294920 | tf_op jit(solution)/shard_map/ppermute | solution.py:465
  40.8 11.2 %collective-permute-start.5 = (f32[3,8,1024]{2,1,0:T(8,128)S(1)}, f32[3,8,1024]{2,1,0:T(8,128)S(1)}, u32[]{:S(2)}, u32[]{:S(2)}) collective-permute-start(f32[3,8,1024]{2,1,0:T(8,128)S(1)} %add.50), channel_id=1, source_target_pairs={{0,2},{1,3},{2,0},{3,1},{4,6},{5,7},{6,4},{7,5},{8,10},{9,11},{10,... | collective-permute-start | bytes 294920 | tf_op jit(solution)/shard_map/ppermute | solution.py:465
  58.8 7.9 %collective-permute-start.8 = (f32[9,8,512]{2,1,0:T(8,128)S(1)}, f32[9,8,512]{2,1,0:T(8,128)S(1)}, u32[]{:S(2)}, u32[]{:S(2)}) collective-permute-start(f32[9,8,512]{2,1,0:T(8,128)S(1)} %slice_select_fusion), channel_id=1, source_target_pairs={{0,1},{1,0},{2,3},{3,2},{4,5},{5,4},{6,7},{7,6},{8,9},{9,8},{10,11... | collective-permute-start | bytes 442376 | tf_op jit(solution)/shard_map/ppermute | solution.py:465
  66.1 1.6 %collective-permute-start.11 = (f32[2,6,2,8,256]{4,3,2,1,0:T(8,128)S(1)}, f32[2,6,2,8,256]{4,3,2,1,0:T(8,128)S(1)}, u32[]{:S(2)}, u32[]{:S(2)}) collective-permute-start(f32[2,6,2,8,256]{4,3,2,1,0:T(8,128)S(1)} %pad_maximum_fusion), channel_id=1, source_target_pairs={{0,1},{1,0},{2,3},{3,2},{4,5},{5,4},{6,7},{7,6},{8,9},{9,8},{10,11... | collective-permute-start | bytes 589832 | tf_op jit(solution)/shard_map/ppermute | solution.py:465
  66.7 8.3 %collective-permute-start.9 = (f32[9,8,512]{2,1,0:T(8,128)S(1)}, f32[9,8,512]{2,1,0:T(8,128)S(1)}, u32[]{:S(2)}, u32[]{:S(2)}) collective-permute-start(f32[9,8,512]{2,1,0:T(8,128)S(1)} %select_add_fusion), channel_id=1, source_target_pairs={{0,2},{1,3},{2,0},{3,1},{4,6},{5,7},{6,4},{7,5},{8,10},{9,11},{10,... | collective-permute-start | bytes 442376 | tf_op jit(solution)/shard_map/ppermute | solution.py:465
  67.8 8.4 %collective-permute-start.12 = (f32[6,2,8,256]{3,2,1,0:T(8,128)S(1)}, f32[6,2,8,256]{3,2,1,0:T(8,128)S(1)}, u32[]{:S(2)}, u32[]{:S(2)}) collective-permute-start(f32[6,2,8,256]{3,2,1,0:T(8,128)S(1)} %get-tuple-element.64), channel_id=1, source_target_pairs={{0,2},{1,3},{2,0},{3,1},{4,6},{5,7},{6,4},{7,5},{8,10},{9,11},{10,... | collective-permute-start | bytes 294920 | tf_op jit(solution)/shard_map/ppermute | solution.py:465
  75.0 1.5 %collective-permute-start.10 = (f32[9,8,512]{2,1,0:T(8,128)S(1)}, f32[9,8,512]{2,1,0:T(8,128)S(1)}, u32[]{:S(2)}, u32[]{:S(2)}) collective-permute-start(f32[9,8,512]{2,1,0:T(8,128)S(1)} %add.53), channel_id=1, source_target_pairs={{0,1},{1,0},{2,3},{3,2},{4,5},{5,4},{6,7},{7,6},{8,9},{9,8},{10,11... | collective-permute-start | bytes 442376 | tf_op jit(solution)/shard_map/ppermute | solution.py:465

commit v3 on v2

--- a/solution.py
+++ b/solution.py
@@ -10,7 +10,8 @@
 
 COH = 128
 LOG2E = 1.4426950408889634
-STEP = 4
+STEP = 8
+LAND = 1e7
 F32 = jnp.float32
 
 
@@ -104,36 +105,35 @@
     pass
 
 
-def crowd_kernel(age, mass, state, crowd):
+def first_kernel(age, mass, ocean, east_vel, north_vel, kappa, state, up, down, crowd):
+    cohorts = state.shape[0]
+
     def begin():
         clear(crowd)
 
     def each(group):
         for layer in range(2):
             crowd[layer] += sum(mass[age[c]] * state[c, layer] for c in group)
-
-    return begin, each, nothing
-
-
-def edges_kernel(*refs):
-    *raw, state, up, down = refs
-
-    def begin():
-        for slot, field in enumerate(raw):
-            pack(lambda layer, start: field[layer, start : start + 2, :].astype(F32), up, down, state.shape[0] + slot)
-        if raw:
-            for out in (up, down):
-                out[state.shape[0] + len(raw)] = jnp.zeros(out.shape[1:], F32)
-
-    def each(group):
         for c in group:
             pack(lambda layer, start: state[c, layer, start : start + 2, :], up, down, c)
 
-    return begin, each, nothing
+    def end():
+        for slot, field in enumerate((ocean, east_vel, north_vel, kappa)):
+            pack(lambda layer, start: field[layer, start : start + 2, :].astype(F32), up, down, cohorts + slot)
+
+    return begin, each, end
+
+
+def edges_kernel(state, up, down):
+    def each(group):
+        for c in group:
+            pack(lambda layer, start: state[c, layer, start : start + 2, :], up, down, c)
+
+    return nothing, each, nothing
 
 
 def forward_kernel(age, mort, crowding, mass, speed, ocean, east_vel, north_vel, kappa, crowd, state,
-                   state_out, rims, fields, total, sums, coef):
+                   state_out, rims, fields, crowd_out, total, sums, coef):
     def begin():
         clear(total, sums)
         for slot, (field, scale) in enumerate(((ocean, None), (east_vel, 0.5), (north_vel, 0.5), (kappa, None))):
@@ -145,11 +145,12 @@
         coef[1] = fields[0] * fields[3]
         coef[2] = fields[0] * fields[1]
         coef[3] = fields[0] * fields[2]
+        crowd_out[...] = jnp.where(fields[0] == 0.0, LAND, crowd[...])
 
     def each(group):
         for c in group:
             mortal, crowded, weight, swim = [table[age[c]] for table in (mort, crowding, mass, speed)]
-            wet = [state[c, k] * (fields[0, k] * decays(mortal, crowded, crowd[k])) for k in range(2)]
+            wet = [state[c, k] * decays(mortal, crowded, crowd_out[k]) for k in range(2)]
             rims[c] = rim(*wet)
             for k in range(2):
                 north, south, to_east, to_west = within(wet[k], 7), within(wet[k], 1), east(wet[k]), west(wet[k])
@@ -168,7 +169,7 @@
     return begin, each, nothing
 
 
-def forward_halo_kernel(age, mort, crowding, mass, speed, fields, total, before, after, rims,
+def forward_halo_kernel(age, mort, crowding, mass, speed, fields, total, before, after, crowd_before, crowd_after, rims,
                         both_out, wet_out, halo_fields, total_out, sums, coef, own, crowd, edge, added):
     def begin():
         clear(sums, added)
@@ -185,14 +186,15 @@
         ocean = rim(fields[0, 0], fields[0, 1])
         own[0] = ocean * rim(fields[3, 0], fields[3, 1])
         own[1] = jnp.where(row < 4, ocean, -ocean) * rim(fields[2, 0], fields[2, 1])
-        join(before[cohorts + 4], after[cohorts + 4], crowd)
+        join(crowd_before[...], crowd_after[...], crowd)
+        crowd[...] = jnp.where(halo_fields[0] == 0.0, LAND, crowd[...])
 
     def each(group):
         for slot, c in enumerate(group):
             join(before[c], after[c], edge.at[slot])
         for slot, c in enumerate(group):
             mortal, crowded, weight, swim = [table[age[c]] for table in (mort, crowding, mass, speed)]
-            wet = edge[slot] * (halo_fields[0] * decays(mortal, crowded, crowd[...]))
+            wet = edge[slot] * decays(mortal, crowded, crowd[...])
             wet_out[c] = wet
             north, south = halo_neighbours(rims[c], wet, wet)
             to_east, to_west = east(wet), west(wet)
@@ -305,15 +307,15 @@
                 across = swim * (coef[2, k] * value[k])
                 sides = east(plain[k] + across) + west(plain[k] - across)
                 spread = coef[0, k] * value[k] + ((north[k] + south[k]) + sides)
-                mine = (fields[0, k] * decays(mortal, crowded, crowd[k])) * spread
+                mine = decays(mortal, crowded, crowd[k]) * spread
                 partial[c, k] = mine
                 later[k] -= crowded * (start[c, k] * mine)
 
     return begin, each, nothing
 
 
-def shares_kernel(age, mort, crowding, speed, fields, crowd, crowd_two, sums, halo_sums, cotangent, pulled, pulled_both, start,
-                  wet_halo, state, state_both, shares):
+def shares_kernel(age, mort, crowding, speed, fields, crowd, crowd_two, sums, halo_sums, pulled, pulled_both, wet_halo, state,
+                  state_both, cotangent, start, shares):
     def begin():
         clear(shares)
         plain, swum = [[sums[n, 0], sums[n, 1], halo_sums[n]] for n in range(2)]
@@ -329,7 +331,7 @@
     def each(group):
         for c in group:
             mortal, crowded, swim = [table[age[c]] for table in (mort, crowding, speed)]
-            old = [start[c, k] * (fields[0, k] * decays(mortal, crowded, crowd[k])) for k in range(2)] + [wet_halo[c]]
+            old = [start[c, k] * decays(mortal, crowded, crowd[k]) for k in range(2)] + [wet_halo[c]]
             fade = [decays(mortal, crowded, crowd_two[k]) for k in range(3)]
             new = [tile * fade[k] for k, tile in enumerate(whole_tiles(state, state_both, c))]
             grad = whole_tiles(pulled, pulled_both, c)
@@ -361,8 +363,8 @@
             still = (1.0 - 4.0 * fields[3, k]) * value[k]
             still += (north[k] + south[k]) + (east(plain[k]) + west(plain[k]))
             moving = (drift_north[k] - drift_south[k]) + (east(across) - west(across))
-            terms[0, k] = fields[0, k] * still
-            terms[1, k] = fields[0, k] * moving
+            terms[0, k] = still
+            terms[1, k] = moving
             terms[2, k] = (totals[3 + k] - totals[5 + k] * still - totals[7 + k] * moving) * (1.0 / COH)
 
     def each(group):
@@ -375,15 +377,20 @@
     return begin, each, nothing
 
 
-def driver(kernel, cohorts, sides, n_small, n_in, n_out, n_whole, n_scratch, *refs):
+def driver(kernel, cohorts, sides, n_tables, n_small, n_in, n_out, n_whole, n_scratch, *refs):
     refs = list(refs)
 
     def take(count):
         taken, refs[:] = refs[:count], refs[count:]
         return taken
 
+    tables = take(n_tables)
     small, sources, sinks, wholes, scratch = take(n_small), take(n_in), take(n_out), take(n_whole), take(n_scratch)
-    inside, outside = take(n_in), take(n_out)
+    inside, outside, held = take(n_in), take(n_out), take(n_tables)
+    table_sem = refs.pop()
+    lookups = [pltpu.make_async_copy(a, b, table_sem.at[n]) for n, (a, b) in enumerate(zip(tables, held))]
+    for copy in lookups:
+        copy.start()
     groups = cohorts // STEP
 
     def span(group):
@@ -400,6 +407,9 @@
     for group in range(groups):
         for copy in loads(group):
             copy.start()
+
+    for copy in lookups:
+        copy.wait()
 
     def run(arrays):
         begin, each, end = kernel(*arrays)
@@ -416,47 +426,50 @@
         lax.fori_loop(0, groups, step, 0)
         end()
 
-    arrays = small + inside + outside + wholes + scratch
+    arrays = held + small + inside + outside + wholes + scratch
+    n_small += n_tables
     if sides is None:
         run(arrays)
     else:
         even, arrays = arrays[0], arrays[1:]
         turned = list(arrays)
-        turned[sides], turned[sides + 1] = arrays[sides + 1], arrays[sides]
+        for side in sides:
+            turned[side], turned[side + 1] = arrays[side + 1], arrays[side]
 
         @pl.when(even[0] == 1)
         def _():
-            run(turned if sides < n_small else arrays)
+            run(turned if sides[0] < n_small else arrays)
 
         @pl.when(even[0] == 0)
         def _():
-            run(arrays if sides < n_small else turned)
+            run(arrays if sides[0] < n_small else turned)
 
     for group in range(groups):
         for copy in stores(group):
             copy.wait()
 
 
-SMEM = pl.BlockSpec(memory_space=pltpu.SMEM)
+VMEM_BYTES = {"first": 8, "late_edges": 6, "forward": 8, "pull": 8, "forward_halo": 8, "pull_halo": 8, "backward": 8,
+              "shares": 10, "last": 8}
 VMEM = pl.BlockSpec(memory_space=pltpu.VMEM)
 LARGE = pl.BlockSpec(memory_space=pl.ANY)
 
 
-def call(kernel, tables, small, large, large_outs, outs, scratch, cycles, sides=None):
-    cohorts = large[0].shape[0]
+def call(name, kernel, cohorts, tables, small, large, large_outs, outs, scratch, cycles, sides=None):
     groups = cohorts // STEP
     vmem = lambda shape: pltpu.VMEM(shape, F32)
     sems = [pltpu.SemaphoreType.DMA((len(arrays), groups)) for arrays in (large, large_outs) if arrays]
     outputs = pl.pallas_call(
-        functools.partial(driver, kernel, cohorts, sides, len(tables) + len(small), len(large), len(large_outs), len(outs), len(scratch)),
-        in_specs=[SMEM] * len(tables) + [VMEM] * len(small) + [LARGE] * len(large),
+        functools.partial(driver, kernel, cohorts, sides, len(tables), len(small), len(large), len(large_outs), len(outs), len(scratch)),
+        in_specs=[LARGE] * len(tables) + [VMEM] * len(small) + [LARGE] * len(large),
         out_specs=[LARGE] * len(large_outs) + [VMEM] * len(outs),
         out_shape=[pltpu.HBM(shape, F32) for shape in large_outs] + [jax.ShapeDtypeStruct(shape, F32) for shape in outs],
         scratch_shapes=[vmem(shape) for shape in scratch] + [vmem(x.shape) for x in large]
-        + [vmem(shape) for shape in large_outs] + sems,
-        compiler_params=pltpu.CompilerParams(vmem_limit_bytes=32 << 20),
+        + [vmem(shape) for shape in large_outs] + [(pltpu.SMEM if x.ndim == 1 else pltpu.VMEM)(x.shape, x.dtype) for x in tables]
+        + sems + [pltpu.SemaphoreType.DMA((len(tables),))],
+        compiler_params=pltpu.CompilerParams(vmem_limit_bytes=VMEM_BYTES[name] << 20),
         cost_estimate=pl.CostEstimate(flops=cycles, transcendentals=0, bytes_accessed=cycles),
-    )(*tables, *small, *[stay(x) for x in large])
+    )(*[stay(x) for x in tables], *small, *[stay(x) for x in large])
     count = len(large_outs)
     return [stay(x) for x in outputs[:count]] + list(outputs[count:])
 
@@ -470,36 +483,24 @@
     return value + swap(value, 2)
 
 
-def halves(value, side):
+def total_by_halves(value, lower):
     middle = value.shape[-1] // 2
     low, high = value[..., :middle], value[..., middle:]
-    return jnp.where(side == 0, low, high), jnp.where(side == 0, high, low)
-
-
-def total_by_halves(value):
-    side = lax.axis_index("coh") % 2
-    keep, send = halves(value, side)
+    keep, send = jnp.where(lower, low, high), jnp.where(lower, high, low)
     keep = keep + swap(send, 1)
     keep = keep + swap(keep, 2)
     other = swap(keep, 1)
-    return jnp.where(side == 0, jnp.concatenate([keep, other], -1), jnp.concatenate([other, keep], -1))
-
-
-def quarter(value):
-    side, block = lax.axis_index("coh") % 2, lax.axis_index("coh") // 2
+    return jnp.where(lower, jnp.concatenate([keep, other], -1), jnp.concatenate([other, keep], -1))
+
+
+def scatter(value, lower, first):
     fourth = value.shape[-1] // 4
     parts = [value[..., k * fourth : (k + 1) * fourth] for k in range(4)]
-    keep = [jnp.where(side == 0, parts[2 * k], parts[2 * k + 1]) for k in range(2)]
-    send = [jnp.where(side == 0, parts[2 * k + 1], parts[2 * k]) for k in range(2)]
-    return keep, send, block
-
-
-def scatter(value):
-    keep, send, block = quarter(value)
+    keep = [jnp.where(lower, parts[2 * k], parts[2 * k + 1]) for k in range(2)]
+    send = [jnp.where(lower, parts[2 * k + 1], parts[2 * k]) for k in range(2)]
     got = swap(jnp.stack(send), 1)
     keep = [keep[0] + got[0], keep[1] + got[1]]
-    mine = jnp.where(block == 0, keep[0], keep[1])
-    rest = jnp.where(block == 0, keep[1], keep[0])
+    mine, rest = jnp.where(first, keep[0], keep[1]), jnp.where(first, keep[1], keep[0])
     return mine + swap(rest, 2)
 
 
@@ -515,24 +516,25 @@
     age_class, mort_rate, crowd_coef, mass, speed = [stay(x) for x in (age_class, mort_rate, crowd_coef, mass, speed)]
     raw_fields = [stay(x) for x in (land_mask, east_vel, north_vel, diffusion)]
     count = lax.axis_size("lat")
-    odd = lax.axis_index("lat") % 2
-    even = (1 - odd).astype(jnp.int32)[None]
+    strip, group = lax.axis_index("lat") & 1, lax.axis_index("coh")
+    choices = (1 - strip).astype(jnp.int32)[None], strip == 1, (group & 1) == 0, (group & 2) == 0
+    density, (even, odd, lower, first) = lax.optimization_barrier((density, choices))
     cohorts, _, height, lon = density.shape
     main, halo, edge = (cohorts, 2, height, lon), (cohorts, height, lon), (cohorts, 4, lon)
     tiles, three, fields_shape = (2, height, lon), (3, height, lon), (4, 3, height, lon)
 
-    wide = (cohorts + 5, 4, lon)
-    (crowd,) = call(crowd_kernel, [age_class, mass], [], [density], [], [tiles], [], 2000)
+    wide = (cohorts + 4, 4, lon)
+    near, far, crowd = call("first", first_kernel, cohorts, [even, age_class, mass] + raw_fields, [], [density], [], [wide, wide, tiles], [],
+                            2000, sides=(len(raw_fields) + 3,))
     crowd = total_of(crowd)
-    near, far = call(edges_kernel, [even], raw_fields, [density], [], [wide, wide], [], 2000, sides=len(raw_fields) + 1)
-    late_near, late_far = call(edges_kernel, [even], [], [cotangent], [], [edge, edge], [], 2000, sides=1)
+    late_near, late_far = call("late_edges", edges_kernel, cohorts, [even], [], [cotangent], [], [edge, edge], [], 2000, sides=(1,))
 
     def edge_rows(value, start):
         return value[:, start : start + 2].reshape(4, lon)
 
     up, down = edge_rows(crowd, height - 2), edge_rows(crowd, 0)
-    far = far.at[cohorts + 4].set(jnp.where(odd == 1, up, down))
-    near = near.at[cohorts + 4].set(jnp.where(odd == 1, down, up))
+    crowd_far = far_swap(jnp.where(odd, up, down), count)
+    crowd_near = near_swap(jnp.where(odd, down, up), count)
     far = far_swap(far, count)
     near = near_swap(near, count)
     late_far = far_swap(late_far, count)
@@ -540,38 +542,28 @@
 
     tables = [age_class, mort_rate, crowd_coef, mass, speed]
     own_fields, halo_fields_shape = (4,) + tiles, (4, height, lon)
-    state, rims, fields, crowd_two, sums = call(
-        forward_kernel, tables, raw_fields + [crowd], [density],
-        [main, halo], [own_fields, tiles, (4,) + tiles], [own_fields], 4000)
-    pulled, late_rims = call(
-        pull_kernel, [age_class, speed], [fields], [cotangent], [main, halo], [], [own_fields], 4000)
-    state_both, wet_halo, halo_fields, crowd_two, halo_sums = call(
-        forward_halo_kernel, [even] + tables, [fields, crowd_two, near, far], [rims],
-        [halo, halo], [halo_fields_shape, three, (2, height, lon)],
-        [halo_fields_shape, (2, height, lon), (height, lon), (STEP, height, lon), (height, lon)], 2500, sides=7)
+    state, rims, fields, crowd, crowd_two, sums = call("forward", forward_kernel, cohorts, tables + raw_fields, [crowd], [density],
+        [], [main, halo, own_fields, tiles, tiles, (4,) + tiles], [own_fields], 4000)
+    pulled, late_rims = call("pull", pull_kernel, cohorts, [age_class, speed], [fields], [cotangent], [], [main, halo], [own_fields], 4000)
+    state_both, wet_halo, halo_fields, crowd_two, halo_sums = call("forward_halo", forward_halo_kernel, cohorts, [even] + tables, [fields, crowd_two, near, far, crowd_near, crowd_far, rims], [],
+        [], [halo, halo, halo_fields_shape, three, (2, height, lon)],
+        [halo_fields_shape, (2, height, lon), (height, lon), (STEP, height, lon), (height, lon)], 2500, sides=(7, 9))
     crowd_two = total_of(crowd_two)
-    (pulled_both,) = call(
-        pull_halo_kernel, [even, age_class, speed], [fields, halo_fields, late_near, late_far], [late_rims],
-        [halo], [], [halo_fields_shape, (3, height, lon), (STEP, height, lon)], 2500, sides=4)
+    (pulled_both,) = call("pull_halo", pull_halo_kernel, cohorts, [even, age_class, speed], [fields, halo_fields, late_near, late_far, late_rims], [],
+        [], [halo], [halo_fields_shape, (3, height, lon), (STEP, height, lon)], 2500, sides=(4,))
 
     tables = [age_class, mort_rate, crowd_coef, speed]
-    partial, totals = call(
-        backward_kernel, tables, [fields, halo_fields, crowd, crowd_two, sums],
-        [pulled, pulled_both, state, state_both, density], [main], [(9, height, lon)], [fields_shape], 5000)
-    totals = total_by_halves(totals)
-
-    (shares,) = call(
-        shares_kernel, tables, [fields, crowd, crowd_two, sums, halo_sums],
-        [cotangent, pulled, pulled_both, density, wet_halo, state, state_both], [], [(6,) + tiles], [], 6000)
-    shares = scatter(shares)
-
-    (grad,) = call(
-        last_kernel, [age_class, mort_rate, crowd_coef, mass, speed],
-        [totals, fields, halo_fields, crowd], [partial], [main], [], [(3,) + tiles], 3000)
-
-    fourth = lon // 4
-    mine = lax.dynamic_slice_in_dim(totals[:2], lax.axis_index("coh") * fourth, fourth, axis=2)
-    shares = shares[:3] + shares[3:] * (mine * (1.0 / COH))[None]
+    partial, totals = call("backward", backward_kernel, cohorts, tables, [fields, halo_fields, crowd, crowd_two, sums, pulled, pulled_both, state, state_both],
+        [density], [], [main, (9, height, lon)], [fields_shape], 5000)
+    totals = total_by_halves(totals, lower)
+
+    (shares,) = call("shares", shares_kernel, cohorts, tables, [fields, crowd, crowd_two, sums, halo_sums, pulled, pulled_both, wet_halo, state, state_both],
+        [cotangent, density], [], [(6,) + tiles], [], 6000)
+    shares = scatter(shares[:3] + shares[3:] * (totals[:2] * (1.0 / COH))[None], lower, first)
+
+    (grad,) = call("last", last_kernel, cohorts, [age_class, mort_rate, crowd_coef, mass, speed],
+        [totals, fields, halo_fields, crowd, partial], [], [main], [], [(3,) + tiles], 3000)
+
     return (grad, shares[0], shares[1], shares[2])
 
 

time: 81.2 us -> 92.6 us (1.14)
  waiting for transfers between devices: 11.2 us -> 31.2 us
  Pallas kernels: 42.9 us -> 29.1 us
  starting transfers between devices: 23.8 us -> 29.5 us
    ppermute x9, waiting for transfers between devices: 8.74 us -> 27.5 us  [swap(): return lax.ppermute(value, 'coh', [(i, i ^ flip) for i in range(4)])]
    pallas_call x10 -> x9, Pallas kernels: 42.9 us -> 29.1 us  [call(): pl.pallas_call(functools.partial(driver, kernel, cohorts, sides, len(tabl...]
    ppermute x2 -> x3, starting transfers between devices: 11.2 us -> 17.4 us  [far_swap(): lax.ppermute(value, 'lat', [(i, (i + 1 ^ 1) - 1) for i in range(1, count...]
    ppermute x2 -> x3, waiting for transfers between devices: 0.01 us -> 3.71 us  [near_swap(): return lax.ppermute(value, 'lat', [(i, i ^ 1) for i in range(count)])]
    ppermute x2 -> x3, waiting for transfers between devices: 2.47 us -> 0.01 us  [far_swap(): lax.ppermute(value, 'lat', [(i, (i + 1 ^ 1) - 1) for i in range(1, count...]
    ppermute x2 -> x3, starting transfers between devices: 2 us -> 2.18 us  [near_swap(): return lax.ppermute(value, 'lat', [(i, i ^ 1) for i in range(count)])]
  transfers between devices with their start and end apart: 13 -> 15, of which waited for: 7 -> 7; matrix products, arithmetic and copies ran while one was open for 0% -> 0% of each run, Pallas kernels for 38% -> 25%
where the time goes in v3:
time: 92.6 us; the launch traced here: 91.7 us
  waiting for transfers between devices  31.2 us (34%)
  starting transfers between devices  29.5 us (32%)
  Pallas kernels  29.1 us (31%)
  between operations  0.95 us (1%)
    pallas_call x9, Pallas kernels, call(): pl.pallas_call(functools.partial(driver, kernel, cohorts, sides, len(tabl...  29.1 us
    ppermute x9, waiting for transfers between devices, swap(): return lax.ppermute(value, 'coh', [(i, i ^ flip) for i in range(4)])  27.5 us
    ppermute x3, starting transfers between devices, far_swap(): lax.ppermute(value, 'lat', [(i, (i + 1 ^ 1) - 1) for i in range(1, count...  17.4 us
    ppermute x9, starting transfers between devices, swap(): return lax.ppermute(value, 'coh', [(i, i ^ flip) for i in range(4)])  9.89 us
    ppermute x3, waiting for transfers between devices, near_swap(): return lax.ppermute(value, 'lat', [(i, i ^ 1) for i in range(count)])  3.71 us
    ppermute x3, starting transfers between devices, near_swap(): return lax.ppermute(value, 'lat', [(i, i ^ 1) for i in range(count)])  2.18 us
  transfers between devices with their start and end apart: 15, of which 7 were waited for; matrix products, arithmetic and copies ran while one was open for 0% of the time, Pallas kernels for 25%

profile of v3, /device:TPU:6, one launch (start us, length us, event | category | flops | bytes accessed | tf_op | source)
XLA Modules:
  0.0 91.7 jit_solution(10515741134925720032)
XLA Ops:
  0.6 2.0 %shard_map.138 = (f32[36,4,1024]{2,1,0:T(4,128)S(1)}, f32[36,4,1024]{2,1,0:T(4,128)S(1)}, f32[2,8,1024]{2,1,0:T(8,128)S(1)}) custom-call(s32[1]{0:T(128)} %bitcast.refs_0_, s32[32]{0:T(128)} %refs_0_.9, f32[32]{0:T(128)} %refs_3_.12, s32[2,8,1024]{2,1,0:T(8,128)} %refs_5_.4, f32[2,8,1024]{2,1,0:T(8,128)} %refs_6_.3, f32[2,8,1024]{2,1,0:T(8,128)} %refs_7_.2, ...), custom_call_target="tpu_custom_call" | custom-call | flops 2000 | bytes 2000 | tf_op jit(solution)/shard_map/pallas_call | solution.py:462
  2.6 2.0 %collective-permute-start.2 = (f32[36,4,1024]{2,1,0:T(4,128)S(1)}, f32[36,4,1024]{2,1,0:T(4,128)S(1)}, u32[]{:S(2)}, u32[]{:S(2)}) collective-permute-start(f32[36,4,1024]{2,1,0:T(4,128)S(1)} %get-tuple-element.35), channel_id=1, source_target_pairs={{0,4},{4,0},{8,12},{12,8},{16,20},{20,16},{24,28},{28,24},{32,36},... | collective-permute-start | bytes 1769480 | tf_op jit(solution)/shard_map/ppermute | solution.py:508
  4.6 8.1 %collective-permute-start.3 = (f32[36,4,1024]{2,1,0:T(4,128)S(1)}, f32[36,4,1024]{2,1,0:T(4,128)S(1)}, u32[]{:S(2)}, u32[]{:S(2)}) collective-permute-start(f32[36,4,1024]{2,1,0:T(4,128)S(1)} %get-tuple-element.36), channel_id=1, source_target_pairs={{4,8},{8,4},{12,16},{16,12},{20,24},{24,20},{28,32},{32,28},{36,40... | collective-permute-start | bytes 1769480 | tf_op jit(solution)/shard_map/ppermute | solution.py:512
  12.8 0.1 collective-permute-start
  12.9 2.6 %shard_map.142 = (f32[32,4,1024]{2,1,0:T(4,128)}, f32[32,4,1024]{2,1,0:T(4,128)}) custom-call(s32[1]{0:T(128)} %bitcast.refs_0_, f32[32,2,8,1024]{3,2,1,0:T(8,128)} %refs_14_.1), custom_call_target="tpu_custom_call" | custom-call | flops 2000 | bytes 2000 | tf_op jit(solution)/shard_map/pallas_call | solution.py:462
  15.5 0.1 collective-permute-start.8
  15.6 3.9 %collective-permute-start.9 = (f32[32,4,1024]{2,1,0:T(4,128)}, f32[32,4,1024]{2,1,0:T(4,128)S(1)}, u32[]{:S(2)}, u32[]{:S(2)}) collective-permute-start(f32[32,4,1024]{2,1,0:T(4,128)} %get-tuple-element.45), channel_id=1, source_target_pairs={{4,8},{8,4},{12,16},{16,12},{20,24},{24,20},{28,32},{32,28},{36,40... | collective-permute-start | bytes 1572872 | tf_op jit(solution)/shard_map/ppermute | solution.py:512
  19.5 0.0 collective-permute-done
  19.5 3.0 %collective-permute-start.1 = (f32[2,8,1024]{2,1,0:T(8,128)S(1)}, f32[2,8,1024]{2,1,0:T(8,128)S(1)}, u32[]{:S(2)}, u32[]{:S(2)}) collective-permute-start(f32[2,8,1024]{2,1,0:T(8,128)S(1)} %add.30), channel_id=1, source_target_pairs={{0,2},{1,3},{2,0},{3,1},{4,6},{5,7},{6,4},{7,5},{8,10},{9,11},{10,... | collective-permute-start | bytes 196616 | tf_op jit(solution)/shard_map/ppermute | solution.py:478
  22.5 17.3 %collective-permute-done.1 = f32[2,8,1024]{2,1,0:T(8,128)S(1)} collective-permute-done((f32[2,8,1024]{2,1,0:T(8,128)S(1)}, f32[2,8,1024]{2,1,0:T(8,128)S(1)}, u32[]{:S(2)}, u32[]{:S(2)}) %collective-permute-start.1) | collective-permute-done | bytes 65568 | tf_op jit(solution)/shard_map/ppermute | solution.py:478
  39.8 0.1 collective-permute-start.4
  40.0 3.7 %collective-permute-done.4.refs_10_ = f32[4,1024]{1,0:T(4,128)S(1)} collective-permute-done((f32[4,1024]{1,0:T(4,128)S(1)}, f32[4,1024]{1,0:T(4,128)S(1)}, u32[]{:S(2)}, u32[]{:S(2)}) %collective-permute-start.4) | collective-permute-done | bytes 16416 | tf_op jit(solution)/shard_map/ppermute | solution.py:508
  43.7 5.4 %collective-permute-start.5 = (f32[4,1024]{1,0:T(4,128)S(1)}, f32[4,1024]{1,0:T(4,128)S(1)}, u32[]{:S(2)}, u32[]{:S(2)}) collective-permute-start(f32[4,1024]{1,0:T(4,128)S(1)} %select_n.74), channel_id=1, source_target_pairs={{4,8},{8,4},{12,16},{16,12},{20,24},{24,20},{28,32},{32,28},{36,40... | collective-permute-start | bytes 49160 | tf_op jit(solution)/shard_map/ppermute | solution.py:512
  49.1 4.3 %shard_map.139 = (f32[32,2,8,1024]{3,2,1,0:T(8,128)S(1)}, f32[32,8,1024]{2,1,0:T(8,128)S(1)}, f32[4,2,8,1024]{3,2,1,0:T(8,128)S(1)}, f32[2,8,1024]{2,1,0:T(8,128...) custom-call(s32[32]{0:T(128)} %refs_0_.9, f32[32]{0:T(128)} %refs_1_.17, f32[32]{0:T(128)} %refs_2_.13, ...), custom_call_target="tpu_custom_call" | custom-call | flops 4000 | bytes 4000 | tf_op jit(solution)/shard_map/pallas_call | solution.py:462
  53.4 0.0 collective-permute-done.5.refs_11_
  53.4 0.0 collective-permute-done.2.refs_8_
  53.4 0.0 collective-permute-done.3.refs_9_
  53.4 2.3 %shard_map.140 = (f32[32,8,1024]{2,1,0:T(8,128)S(1)}, f32[32,8,1024]{2,1,0:T(8,128)S(1)}, f32[4,8,1024]{2,1,0:T(8,128)S(1)}, f32[3,8,1024]{2,1,0:T(8,128)S(1)}, f32[2,8,1024]{2,1,0:T(8,128)S(1)}) custom-call(s32[1]{0:T(128)} %bitcast.refs_0_, s32[32]{0:T(128)} %refs_0_.9, f32[32]{0:T(128)} %refs_1_.17, f32[32]{0:T(128)} %refs_2_.13, f32[32]{0:T(128)} %refs_3_.12, ...), custom_call_target="tpu_custom_call" | custom-call | flops 2500 | bytes 2500 | tf_op jit(solution)/shard_map/pallas_call | solution.py:462
  55.7 0.1 collective-permute-start.6
  55.8 1.3 %collective-permute-done.6 = f32[3,8,1024]{2,1,0:T(8,128)S(1)} collective-permute-done((f32[3,8,1024]{2,1,0:T(8,128)S(1)}, f32[3,8,1024]{2,1,0:T(8,128)S(1)}, u32[]{:S(2)}, u32[]{:S(2)}) %collective-permute-start.6) | collective-permute-done | bytes 98336 | tf_op jit(solution)/shard_map/ppermute | solution.py:478
  57.1 1.6 %collective-permute-start.7 = (f32[3,8,1024]{2,1,0:T(8,128)S(1)}, f32[3,8,1024]{2,1,0:T(8,128)S(1)}, u32[]{:S(2)}, u32[]{:S(2)}) collective-permute-start(f32[3,8,1024]{2,1,0:T(8,128)S(1)} %add.32), channel_id=1, source_target_pairs={{0,2},{1,3},{2,0},{3,1},{4,6},{5,7},{6,4},{7,5},{8,10},{9,11},{10,... | collective-permute-start | bytes 294920 | tf_op jit(solution)/shard_map/ppermute | solution.py:478
  58.8 3.0 %shard_map.141 = (f32[32,2,8,1024]{3,2,1,0:T(8,128)S(1)}, f32[32,8,1024]{2,1,0:T(8,128)S(1)}) custom-call(s32[32]{0:T(128)} %refs_0_.9, f32[32]{0:T(128)} %refs_3_.13, f32[4,2,8,1024]{3,2,1,0:T(8,128)S(1)} %get-tuple-element.33.refs_6_.refs_2_.refs_3_.refs_4_, f32[32,2,8,1024]{3,2,1,0:T(8,128)} %refs_14_.1), custom_call_target="tpu_custom_call" | custom-call | flops 4000 | bytes 4000 | tf_op jit(solution)/shard_map/pallas_call | solution.py:462
  61.7 0.0 collective-permute-done.8.refs_5_
  61.7 0.0 collective-permute-done.9.refs_6_
  61.8 2.1 %shard_map.143.refs_10_ = f32[32,8,1024]{2,1,0:T(8,128)S(1)} custom-call(s32[1]{0:T(128)} %bitcast.refs_0_, s32[32]{0:T(128)} %refs_0_.9, f32[32]{0:T(128)} %refs_3_.13, f32[4,2,8,1024]{3,2,1,0:T(8,128)S(1)} %get-tuple-element.33.refs_6_.refs_2_.refs_3_.refs_4_, f32[4,8,1024]{2,1,0:T(8,128)S(1)} %get-tuple-element.39.refs_4_.refs_5_.refs_7_, ...), custom_call_target="tpu_custom_call" | custom-call | flops 2500 | bytes 2500 | tf_op jit(solution)/shard_map/pallas_call | solution.py:462
  63.8 0.0 collective-permute-done.7
  63.9 4.6 %shard_map.144 = (f32[32,2,8,1024]{3,2,1,0:T(8,128)S(1)}, f32[9,8,1024]{2,1,0:T(8,128)S(1)}) custom-call(s32[32]{0:T(128)} %refs_0_.9, f32[32]{0:T(128)} %refs_1_.17, f32[32]{0:T(128)} %refs_2_.13, f32[32]{0:T(128)} %refs_3_.13, f32[4,2,8,1024]{3,2,1,0:T(8,128)S(1)} %get-tuple-element.33.refs_6_.refs_2_.refs_3_.refs_4_, ...), custom_call_target="tpu_custom_call" | custom-call | flops 5000 | bytes 5000 | tf_op jit(solution)/shard_map/pallas_call | solution.py:462
  68.6 0.1 collective-permute-start.10
  68.7 1.4 %collective-permute-done.10 = f32[9,8,512]{2,1,0:T(8,128)S(1)} collective-permute-done((f32[9,8,512]{2,1,0:T(8,128)S(1)}, f32[9,8,512]{2,1,0:T(8,128)S(1)}, u32[]{:S(2)}, u32[]{:S(2)}) %collective-permute-start.10) | collective-permute-done | bytes 147488 | tf_op jit(solution)/shard_map/ppermute | solution.py:478
  70.1 2.1 %collective-permute-start.11 = (f32[9,8,512]{2,1,0:T(8,128)S(1)}, f32[9,8,512]{2,1,0:T(8,128)S(1)}, u32[]{:S(2)}, u32[]{:S(2)}) collective-permute-start(f32[9,8,512]{2,1,0:T(8,128)S(1)} %select_add_fusion), channel_id=1, source_target_pairs={{0,2},{1,3},{2,0},{3,1},{4,6},{5,7},{6,4},{7,5},{8,10},{9,11},{10,... | collective-permute-start | bytes 442376 | tf_op jit(solution)/shard_map/ppermute | solution.py:478
  72.1 5.4 %collective-permute-done.11 = f32[9,8,512]{2,1,0:T(8,128)S(1)} collective-permute-done((f32[9,8,512]{2,1,0:T(8,128)S(1)}, f32[9,8,512]{2,1,0:T(8,128)S(1)}, u32[]{:S(2)}, u32[]{:S(2)}) %collective-permute-start.11) | collective-permute-done | bytes 147488 | tf_op jit(solution)/shard_map/ppermute | solution.py:478
  77.6 0.3 collective-permute-start.12
  77.9 5.8 %shard_map.146 = f32[6,2,8,1024]{3,2,1,0:T(8,128)S(1)} custom-call(s32[32]{0:T(128)} %refs_0_.9, f32[32]{0:T(128)} %refs_1_.17, f32[32]{0:T(128)} %refs_2_.13, f32[32]{0:T(128)} %refs_3_.13, f32[4,2,8,1024]{3,2,1,0:T(8,128)S(1)} %get-tuple-element.33.refs_6_.refs_2_.refs_3_.refs_4_, f32[2,8,1024]{2,1,0:T(8,128)S(1)} %get-tuple-element.40.refs_6_.refs_8_.refs_5_, ...), custom_call_target="tpu_custom_call" | custom-call | flops 6000 | bytes 6000 | tf_op jit(solution)/shard_map/pallas_call | solution.py:462
  83.7 0.0 collective-permute-done.12
  83.8 0.6 collective-permute-start.13
  84.4 0.9 %collective-permute-done.13 = f32[2,3,2,8,256]{4,3,2,1,0:T(8,128)S(1)} collective-permute-done((f32[2,3,2,8,256]{4,3,2,1,0:T(8,128)S(1)}, f32[2,3,2,8,256]{4,3,2,1,0:T(8,128)S(1)}, u32[]{:S(2)}, u32[]{:S(2)}) %collective-permute-start.13) | collective-permute-done | bytes 98336 | tf_op jit(solution)/shard_map/ppermute | solution.py:478
  85.4 2.1 %collective-permute-start.14 = (f32[3,2,8,256]{3,2,1,0:T(8,128)S(1)}, f32[3,2,8,256]{3,2,1,0:T(8,128)S(1)}, u32[]{:S(2)}, u32[]{:S(2)}) collective-permute-start(f32[3,2,8,256]{3,2,1,0:T(8,128)S(1)} %get-tuple-element.54), channel_id=1, source_target_pairs={{0,2},{1,3},{2,0},{3,1},{4,6},{5,7},{6,4},{7,5},{8,10},{9,11},{10,... | collective-permute-start | bytes 147464 | tf_op jit(solution)/shard_map/ppermute | solution.py:478
  87.4 2.4 %shard_map.145 = f32[32,2,8,1024]{3,2,1,0:T(8,128)} custom-call(s32[32]{0:T(128)} %refs_0_.9, f32[32]{0:T(128)} %refs_1_.17, f32[32]{0:T(128)} %refs_2_.13, f32[32]{0:T(128)} %refs_3_.12, f32[32]{0:T(128)} %refs_3_.13, f32[9,8,1024]{2,1,0:T(8,128)S(1)} %maximum_select_fusion.refs_5_, f32[4,2,8,1024]{3,2,1,0:T(8,128)S(1)} %get-tuple-element.33.refs_6_.refs_2_.refs_3_.refs_4_, ...), custom_call_target="tpu_custom_call" | custom-call | flops 3000 | bytes 3000 | tf_op jit(solution)/shard_map/pallas_call | solution.py:462
  89.8 1.2 %collective-permute-done.14 = f32[3,2,8,256]{3,2,1,0:T(8,128)S(1)} collective-permute-done((f32[3,2,8,256]{3,2,1,0:T(8,128)S(1)}, f32[3,2,8,256]{3,2,1,0:T(8,128)S(1)}, u32[]{:S(2)}, u32[]{:S(2)}) %collective-permute-start.14) | collective-permute-done | bytes 49184 | tf_op jit(solution)/shard_map/ppermute | solution.py:478
  91.1 0.6 slice_bitcast_fusion.2
  (17 shorter events, 0.3 us)
Async XLA Ops:
  2.6 50.8 %collective-permute-start.2 = (f32[36,4,1024]{2,1,0:T(4,128)S(1)}, f32[36,4,1024]{2,1,0:T(4,128)S(1)}, u32[]{:S(2)}, u32[]{:S(2)}) collective-permute-start(f32[36,4,1024]{2,1,0:T(4,128)S(1)} %get-tuple-element.35), channel_id=1, source_target_pairs={{0,4},{4,0},{8,12},{12,8},{16,20},{20,16},{24,28},{28,24},{32,36},... | collective-permute-start | bytes 1769480 | tf_op jit(solution)/shard_map/ppermute | solution.py:508
  4.6 48.8 %collective-permute-start.3 = (f32[36,4,1024]{2,1,0:T(4,128)S(1)}, f32[36,4,1024]{2,1,0:T(4,128)S(1)}, u32[]{:S(2)}, u32[]{:S(2)}) collective-permute-start(f32[36,4,1024]{2,1,0:T(4,128)S(1)} %get-tuple-element.36), channel_id=1, source_target_pairs={{4,8},{8,4},{12,16},{16,12},{20,24},{24,20},{28,32},{32,28},{36,40... | collective-permute-start | bytes 1769480 | tf_op jit(solution)/shard_map/ppermute | solution.py:512
  12.8 6.7 %collective-permute-start = (f32[2,8,1024]{2,1,0:T(8,128)S(1)}, f32[2,8,1024]{2,1,0:T(8,128)S(1)}, u32[]{:S(2)}, u32[]{:S(2)}) collective-permute-start(f32[2,8,1024]{2,1,0:T(8,128)S(1)} %get-tuple-element.32), channel_id=1, source_target_pairs={{0,1},{1,0},{2,3},{3,2},{4,5},{5,4},{6,7},{7,6},{8,9},{9,8},{10,11... | collective-permute-start | bytes 196616 | tf_op jit(solution)/shard_map/ppermute | solution.py:478
  15.5 46.3 %collective-permute-start.8 = (f32[32,4,1024]{2,1,0:T(4,128)}, f32[32,4,1024]{2,1,0:T(4,128)S(1)}, u32[]{:S(2)}, u32[]{:S(2)}) collective-permute-start(f32[32,4,1024]{2,1,0:T(4,128)} %get-tuple-element.44), channel_id=1, source_target_pairs={{0,4},{4,0},{8,12},{12,8},{16,20},{20,16},{24,28},{28,24},{32,36},... | collective-permute-start | bytes 1572872 | tf_op jit(solution)/shard_map/ppermute | solution.py:508
  15.6 46.2 %collective-permute-start.9 = (f32[32,4,1024]{2,1,0:T(4,128)}, f32[32,4,1024]{2,1,0:T(4,128)S(1)}, u32[]{:S(2)}, u32[]{:S(2)}) collective-permute-start(f32[32,4,1024]{2,1,0:T(4,128)} %get-tuple-element.45), channel_id=1, source_target_pairs={{4,8},{8,4},{12,16},{16,12},{20,24},{24,20},{28,32},{32,28},{36,40... | collective-permute-start | bytes 1572872 | tf_op jit(solution)/shard_map/ppermute | solution.py:512
  19.5 20.3 %collective-permute-start.1 = (f32[2,8,1024]{2,1,0:T(8,128)S(1)}, f32[2,8,1024]{2,1,0:T(8,128)S(1)}, u32[]{:S(2)}, u32[]{:S(2)}) collective-permute-start(f32[2,8,1024]{2,1,0:T(8,128)S(1)} %add.30), channel_id=1, source_target_pairs={{0,2},{1,3},{2,0},{3,1},{4,6},{5,7},{6,4},{7,5},{8,10},{9,11},{10,... | collective-permute-start | bytes 196616 | tf_op jit(solution)/shard_map/ppermute | solution.py:478
  39.8 3.8 %collective-permute-start.4 = (f32[4,1024]{1,0:T(4,128)S(1)}, f32[4,1024]{1,0:T(4,128)S(1)}, u32[]{:S(2)}, u32[]{:S(2)}) collective-permute-start(f32[4,1024]{1,0:T(4,128)S(1)} %select_n.72), channel_id=1, source_target_pairs={{0,4},{4,0},{8,12},{12,8},{16,20},{20,16},{24,28},{28,24},{32,36},... | collective-permute-start | bytes 49160 | tf_op jit(solution)/shard_map/ppermute | solution.py:508
  43.7 9.7 %collective-permute-start.5 = (f32[4,1024]{1,0:T(4,128)S(1)}, f32[4,1024]{1,0:T(4,128)S(1)}, u32[]{:S(2)}, u32[]{:S(2)}) collective-permute-start(f32[4,1024]{1,0:T(4,128)S(1)} %select_n.74), channel_id=1, source_target_pairs={{4,8},{8,4},{12,16},{16,12},{20,24},{24,20},{28,32},{32,28},{36,40... | collective-permute-start | bytes 49160 | tf_op jit(solution)/shard_map/ppermute | solution.py:512
  55.7 1.4 %collective-permute-start.6 = (f32[3,8,1024]{2,1,0:T(8,128)S(1)}, f32[3,8,1024]{2,1,0:T(8,128)S(1)}, u32[]{:S(2)}, u32[]{:S(2)}) collective-permute-start(f32[3,8,1024]{2,1,0:T(8,128)S(1)} %get-tuple-element.41), channel_id=1, source_target_pairs={{0,1},{1,0},{2,3},{3,2},{4,5},{5,4},{6,7},{7,6},{8,9},{9,8},{10,11... | collective-permute-start | bytes 294920 | tf_op jit(solution)/shard_map/ppermute | solution.py:478
  57.1 6.7 %collective-permute-start.7 = (f32[3,8,1024]{2,1,0:T(8,128)S(1)}, f32[3,8,1024]{2,1,0:T(8,128)S(1)}, u32[]{:S(2)}, u32[]{:S(2)}) collective-permute-start(f32[3,8,1024]{2,1,0:T(8,128)S(1)} %add.32), channel_id=1, source_target_pairs={{0,2},{1,3},{2,0},{3,1},{4,6},{5,7},{6,4},{7,5},{8,10},{9,11},{10,... | collective-permute-start | bytes 294920 | tf_op jit(solution)/shard_map/ppermute | solution.py:478
  68.6 1.5 %collective-permute-start.10 = (f32[9,8,512]{2,1,0:T(8,128)S(1)}, f32[9,8,512]{2,1,0:T(8,128)S(1)}, u32[]{:S(2)}, u32[]{:S(2)}) collective-permute-start(f32[9,8,512]{2,1,0:T(8,128)S(1)} %slice_select_fusion), channel_id=1, source_target_pairs={{0,1},{1,0},{2,3},{3,2},{4,5},{5,4},{6,7},{7,6},{8,9},{9,8},{10,11... | collective-permute-start | bytes 442376 | tf_op jit(solution)/shard_map/ppermute | solution.py:478
  70.1 7.5 %collective-permute-start.11 = (f32[9,8,512]{2,1,0:T(8,128)S(1)}, f32[9,8,512]{2,1,0:T(8,128)S(1)}, u32[]{:S(2)}, u32[]{:S(2)}) collective-permute-start(f32[9,8,512]{2,1,0:T(8,128)S(1)} %select_add_fusion), channel_id=1, source_target_pairs={{0,2},{1,3},{2,0},{3,1},{4,6},{5,7},{6,4},{7,5},{8,10},{9,11},{10,... | collective-permute-start | bytes 442376 | tf_op jit(solution)/shard_map/ppermute | solution.py:478
  77.6 6.1 %collective-permute-start.12 = (f32[9,8,512]{2,1,0:T(8,128)S(1)}, f32[9,8,512]{2,1,0:T(8,128)S(1)}, u32[]{:S(2)}, u32[]{:S(2)}) collective-permute-start(f32[9,8,512]{2,1,0:T(8,128)S(1)} %add.35), channel_id=1, source_target_pairs={{0,1},{1,0},{2,3},{3,2},{4,5},{5,4},{6,7},{7,6},{8,9},{9,8},{10,11... | collective-permute-start | bytes 442376 | tf_op jit(solution)/shard_map/ppermute | solution.py:478
  83.8 1.5 %collective-permute-start.13 = (f32[2,3,2,8,256]{4,3,2,1,0:T(8,128)S(1)}, f32[2,3,2,8,256]{4,3,2,1,0:T(8,128)S(1)}, u32[]{:S(2)}, u32[]{:S(2)}) collective-permute-start(f32[2,3,2,8,256]{4,3,2,1,0:T(8,128)S(1)} %pad_maximum_fusion), channel_id=1, source_target_pairs={{0,1},{1,0},{2,3},{3,2},{4,5},{5,4},{6,7},{7,6},{8,9},{9,8},{10,11... | collective-permute-start | bytes 294920 | tf_op jit(solution)/shard_map/ppermute | solution.py:478
  85.4 5.7 %collective-permute-start.14 = (f32[3,2,8,256]{3,2,1,0:T(8,128)S(1)}, f32[3,2,8,256]{3,2,1,0:T(8,128)S(1)}, u32[]{:S(2)}, u32[]{:S(2)}) collective-permute-start(f32[3,2,8,256]{3,2,1,0:T(8,128)S(1)} %get-tuple-element.54), channel_id=1, source_target_pairs={{0,2},{1,3},{2,0},{3,1},{4,6},{5,7},{6,4},{7,5},{8,10},{9,11},{10,... | collective-permute-start | bytes 147464 | tf_op jit(solution)/shard_map/ppermute | solution.py:478

commit v4 on v3

--- a/solution.py
+++ b/solution.py
@@ -493,15 +493,12 @@
     return jnp.where(lower, jnp.concatenate([keep, other], -1), jnp.concatenate([other, keep], -1))
 
 
-def scatter(value, lower, first):
+def own_quarters(value, lower):
     fourth = value.shape[-1] // 4
     parts = [value[..., k * fourth : (k + 1) * fourth] for k in range(4)]
-    keep = [jnp.where(lower, parts[2 * k], parts[2 * k + 1]) for k in range(2)]
-    send = [jnp.where(lower, parts[2 * k + 1], parts[2 * k]) for k in range(2)]
-    got = swap(jnp.stack(send), 1)
-    keep = [keep[0] + got[0], keep[1] + got[1]]
-    mine, rest = jnp.where(first, keep[0], keep[1]), jnp.where(first, keep[1], keep[0])
-    return mine + swap(rest, 2)
+    keep = jnp.stack([jnp.where(lower, parts[2 * k], parts[2 * k + 1]) for k in range(2)])
+    send = jnp.stack([jnp.where(lower, parts[2 * k + 1], parts[2 * k]) for k in range(2)])
+    return keep, send
 
 
 def near_swap(value, count):
@@ -559,7 +556,12 @@
 
     (shares,) = call("shares", shares_kernel, cohorts, tables, [fields, crowd, crowd_two, sums, halo_sums, pulled, pulled_both, wet_halo, state, state_both],
         [cotangent, density], [], [(6,) + tiles], [], 6000)
-    shares = scatter(shares[:3] + shares[3:] * (totals[:2] * (1.0 / COH))[None], lower, first)
+    keep, send = own_quarters(shares, lower)
+    keep = keep + swap(send, 1)
+    scale, _ = own_quarters(totals[:2] * (1.0 / COH), lower)
+    keep = keep[:, :3] + keep[:, 3:] * scale[:, None]
+    mine, rest = jnp.where(first, keep[0], keep[1]), jnp.where(first, keep[1], keep[0])
+    shares = mine + swap(rest, 2)
 
     (grad,) = call("last", last_kernel, cohorts, [age_class, mort_rate, crowd_coef, mass, speed],
         [totals, fields, halo_fields, crowd, partial], [], [main], [], [(3,) + tiles], 3000)

time: 92.6 us -> 91.4 us (0.987)
  waiting for transfers between devices: 31.2 us -> 30.1 us
    ppermute x9, waiting for transfers between devices: 27.5 us -> 26.4 us  [swap(): return lax.ppermute(value, 'coh', [(i, i ^ flip) for i in range(4)])]
  transfers between devices with their start and end apart: 15 -> 15, of which waited for: 7 -> 6; matrix products, arithmetic and copies ran while one was open for 0% -> 0% of each run, Pallas kernels for 25% -> 25%
where the time goes in v4:
time: 91.4 us; the launch traced here: 90.5 us
  waiting for transfers between devices  30.1 us (33%)
  starting transfers between devices  29.3 us (32%)
  Pallas kernels  29.1 us (32%)
  between operations  0.97 us (1%)
    pallas_call x9, Pallas kernels, call(): pl.pallas_call(functools.partial(driver, kernel, cohorts, sides, len(tabl...  29.1 us
    ppermute x9, waiting for transfers between devices, swap(): return lax.ppermute(value, 'coh', [(i, i ^ flip) for i in range(4)])  26.4 us
    ppermute x3, starting transfers between devices, far_swap(): lax.ppermute(value, 'lat', [(i, (i + 1 ^ 1) - 1) for i in range(1, count...  17.4 us
    ppermute x9, starting transfers between devices, swap(): return lax.ppermute(value, 'coh', [(i, i ^ flip) for i in range(4)])  9.7 us
    ppermute x3, waiting for transfers between devices, near_swap(): return lax.ppermute(value, 'lat', [(i, i ^ 1) for i in range(count)])  3.71 us
    ppermute x3, starting transfers between devices, near_swap(): return lax.ppermute(value, 'lat', [(i, i ^ 1) for i in range(count)])  2.18 us
  transfers between devices with their start and end apart: 15, of which 6 were waited for; matrix products, arithmetic and copies ran while one was open for 0% of the time, Pallas kernels for 25%

profile of v4, /device:TPU:6, one launch (start us, length us, event | category | flops | bytes accessed | tf_op | source)
XLA Modules:
  0.0 90.5 jit_solution(16840680410222820248)
XLA Ops:
  0.6 2.0 %shard_map.138 = (f32[36,4,1024]{2,1,0:T(4,128)S(1)}, f32[36,4,1024]{2,1,0:T(4,128)S(1)}, f32[2,8,1024]{2,1,0:T(8,128)S(1)}) custom-call(s32[1]{0:T(128)} %bitcast.refs_0_, s32[32]{0:T(128)} %refs_0_.9, f32[32]{0:T(128)} %refs_3_.12, s32[2,8,1024]{2,1,0:T(8,128)} %refs_5_.4, f32[2,8,1024]{2,1,0:T(8,128)} %refs_6_.3, f32[2,8,1024]{2,1,0:T(8,128)} %refs_7_.2, ...), custom_call_target="tpu_custom_call" | custom-call | flops 2000 | bytes 2000 | tf_op jit(solution)/shard_map/pallas_call | solution.py:462
  2.6 2.0 %collective-permute-start.2 = (f32[36,4,1024]{2,1,0:T(4,128)S(1)}, f32[36,4,1024]{2,1,0:T(4,128)S(1)}, u32[]{:S(2)}, u32[]{:S(2)}) collective-permute-start(f32[36,4,1024]{2,1,0:T(4,128)S(1)} %get-tuple-element.35), channel_id=1, source_target_pairs={{0,4},{4,0},{8,12},{12,8},{16,20},{20,16},{24,28},{28,24},{32,36},... | collective-permute-start | bytes 1769480 | tf_op jit(solution)/shard_map/ppermute | solution.py:505
  4.6 8.1 %collective-permute-start.3 = (f32[36,4,1024]{2,1,0:T(4,128)S(1)}, f32[36,4,1024]{2,1,0:T(4,128)S(1)}, u32[]{:S(2)}, u32[]{:S(2)}) collective-permute-start(f32[36,4,1024]{2,1,0:T(4,128)S(1)} %get-tuple-element.36), channel_id=1, source_target_pairs={{4,8},{8,4},{12,16},{16,12},{20,24},{24,20},{28,32},{32,28},{36,40... | collective-permute-start | bytes 1769480 | tf_op jit(solution)/shard_map/ppermute | solution.py:509
  12.8 0.1 collective-permute-start
  12.9 2.6 %shard_map.142 = (f32[32,4,1024]{2,1,0:T(4,128)}, f32[32,4,1024]{2,1,0:T(4,128)}) custom-call(s32[1]{0:T(128)} %bitcast.refs_0_, f32[32,2,8,1024]{3,2,1,0:T(8,128)} %refs_14_.1), custom_call_target="tpu_custom_call" | custom-call | flops 2000 | bytes 2000 | tf_op jit(solution)/shard_map/pallas_call | solution.py:462
  15.5 0.1 collective-permute-start.8
  15.6 3.9 %collective-permute-start.9 = (f32[32,4,1024]{2,1,0:T(4,128)}, f32[32,4,1024]{2,1,0:T(4,128)S(1)}, u32[]{:S(2)}, u32[]{:S(2)}) collective-permute-start(f32[32,4,1024]{2,1,0:T(4,128)} %get-tuple-element.45), channel_id=1, source_target_pairs={{4,8},{8,4},{12,16},{16,12},{20,24},{24,20},{28,32},{32,28},{36,40... | collective-permute-start | bytes 1572872 | tf_op jit(solution)/shard_map/ppermute | solution.py:509
  19.5 0.0 collective-permute-done
  19.5 3.0 %collective-permute-start.1 = (f32[2,8,1024]{2,1,0:T(8,128)S(1)}, f32[2,8,1024]{2,1,0:T(8,128)S(1)}, u32[]{:S(2)}, u32[]{:S(2)}) collective-permute-start(f32[2,8,1024]{2,1,0:T(8,128)S(1)} %add.27), channel_id=1, source_target_pairs={{0,2},{1,3},{2,0},{3,1},{4,6},{5,7},{6,4},{7,5},{8,10},{9,11},{10,... | collective-permute-start | bytes 196616 | tf_op jit(solution)/shard_map/ppermute | solution.py:478
  22.5 17.3 %collective-permute-done.1 = f32[2,8,1024]{2,1,0:T(8,128)S(1)} collective-permute-done((f32[2,8,1024]{2,1,0:T(8,128)S(1)}, f32[2,8,1024]{2,1,0:T(8,128)S(1)}, u32[]{:S(2)}, u32[]{:S(2)}) %collective-permute-start.1) | collective-permute-done | bytes 65568 | tf_op jit(solution)/shard_map/ppermute | solution.py:478
  39.8 0.1 collective-permute-start.4
  40.0 3.7 %collective-permute-done.4.refs_10_ = f32[4,1024]{1,0:T(4,128)S(1)} collective-permute-done((f32[4,1024]{1,0:T(4,128)S(1)}, f32[4,1024]{1,0:T(4,128)S(1)}, u32[]{:S(2)}, u32[]{:S(2)}) %collective-permute-start.4) | collective-permute-done | bytes 16416 | tf_op jit(solution)/shard_map/ppermute | solution.py:505
  43.7 5.4 %collective-permute-start.5 = (f32[4,1024]{1,0:T(4,128)S(1)}, f32[4,1024]{1,0:T(4,128)S(1)}, u32[]{:S(2)}, u32[]{:S(2)}) collective-permute-start(f32[4,1024]{1,0:T(4,128)S(1)} %select_n.94), channel_id=1, source_target_pairs={{4,8},{8,4},{12,16},{16,12},{20,24},{24,20},{28,32},{32,28},{36,40... | collective-permute-start | bytes 49160 | tf_op jit(solution)/shard_map/ppermute | solution.py:509
  49.1 4.3 %shard_map.139 = (f32[32,2,8,1024]{3,2,1,0:T(8,128)S(1)}, f32[32,8,1024]{2,1,0:T(8,128)S(1)}, f32[4,2,8,1024]{3,2,1,0:T(8,128)S(1)}, f32[2,8,1024]{2,1,0:T(8,128...) custom-call(s32[32]{0:T(128)} %refs_0_.9, f32[32]{0:T(128)} %refs_1_.17, f32[32]{0:T(128)} %refs_2_.13, ...), custom_call_target="tpu_custom_call" | custom-call | flops 4000 | bytes 4000 | tf_op jit(solution)/shard_map/pallas_call | solution.py:462
  53.4 0.0 collective-permute-done.5.refs_11_
  53.4 0.0 collective-permute-done.2.refs_8_
  53.4 0.0 collective-permute-done.3.refs_9_
  53.4 2.3 %shard_map.140 = (f32[32,8,1024]{2,1,0:T(8,128)S(1)}, f32[32,8,1024]{2,1,0:T(8,128)S(1)}, f32[4,8,1024]{2,1,0:T(8,128)S(1)}, f32[3,8,1024]{2,1,0:T(8,128)S(1)}, f32[2,8,1024]{2,1,0:T(8,128)S(1)}) custom-call(s32[1]{0:T(128)} %bitcast.refs_0_, s32[32]{0:T(128)} %refs_0_.9, f32[32]{0:T(128)} %refs_1_.17, f32[32]{0:T(128)} %refs_2_.13, f32[32]{0:T(128)} %refs_3_.12, ...), custom_call_target="tpu_custom_call" | custom-call | flops 2500 | bytes 2500 | tf_op jit(solution)/shard_map/pallas_call | solution.py:462
  55.7 0.1 collective-permute-start.6
  55.8 1.3 %collective-permute-done.6 = f32[3,8,1024]{2,1,0:T(8,128)S(1)} collective-permute-done((f32[3,8,1024]{2,1,0:T(8,128)S(1)}, f32[3,8,1024]{2,1,0:T(8,128)S(1)}, u32[]{:S(2)}, u32[]{:S(2)}) %collective-permute-start.6) | collective-permute-done | bytes 98336 | tf_op jit(solution)/shard_map/ppermute | solution.py:478
  57.1 1.6 %collective-permute-start.7 = (f32[3,8,1024]{2,1,0:T(8,128)S(1)}, f32[3,8,1024]{2,1,0:T(8,128)S(1)}, u32[]{:S(2)}, u32[]{:S(2)}) collective-permute-start(f32[3,8,1024]{2,1,0:T(8,128)S(1)} %add.29), channel_id=1, source_target_pairs={{0,2},{1,3},{2,0},{3,1},{4,6},{5,7},{6,4},{7,5},{8,10},{9,11},{10,... | collective-permute-start | bytes 294920 | tf_op jit(solution)/shard_map/ppermute | solution.py:478
  58.8 3.0 %shard_map.141 = (f32[32,2,8,1024]{3,2,1,0:T(8,128)S(1)}, f32[32,8,1024]{2,1,0:T(8,128)S(1)}) custom-call(s32[32]{0:T(128)} %refs_0_.9, f32[32]{0:T(128)} %refs_3_.13, f32[4,2,8,1024]{3,2,1,0:T(8,128)S(1)} %get-tuple-element.33.refs_6_.refs_2_.refs_3_.refs_4_, f32[32,2,8,1024]{3,2,1,0:T(8,128)} %refs_14_.1), custom_call_target="tpu_custom_call" | custom-call | flops 4000 | bytes 4000 | tf_op jit(solution)/shard_map/pallas_call | solution.py:462
  61.7 0.0 collective-permute-done.8.refs_5_
  61.7 0.0 collective-permute-done.9.refs_6_
  61.8 2.1 %shard_map.143.refs_10_ = f32[32,8,1024]{2,1,0:T(8,128)S(1)} custom-call(s32[1]{0:T(128)} %bitcast.refs_0_, s32[32]{0:T(128)} %refs_0_.9, f32[32]{0:T(128)} %refs_3_.13, f32[4,2,8,1024]{3,2,1,0:T(8,128)S(1)} %get-tuple-element.33.refs_6_.refs_2_.refs_3_.refs_4_, f32[4,8,1024]{2,1,0:T(8,128)S(1)} %get-tuple-element.39.refs_4_.refs_5_.refs_7_, ...), custom_call_target="tpu_custom_call" | custom-call | flops 2500 | bytes 2500 | tf_op jit(solution)/shard_map/pallas_call | solution.py:462
  63.8 0.0 collective-permute-done.7
  63.9 4.6 %shard_map.144 = (f32[32,2,8,1024]{3,2,1,0:T(8,128)S(1)}, f32[9,8,1024]{2,1,0:T(8,128)S(1)}) custom-call(s32[32]{0:T(128)} %refs_0_.9, f32[32]{0:T(128)} %refs_1_.17, f32[32]{0:T(128)} %refs_2_.13, f32[32]{0:T(128)} %refs_3_.13, f32[4,2,8,1024]{3,2,1,0:T(8,128)S(1)} %get-tuple-element.33.refs_6_.refs_2_.refs_3_.refs_4_, ...), custom_call_target="tpu_custom_call" | custom-call | flops 5000 | bytes 5000 | tf_op jit(solution)/shard_map/pallas_call | solution.py:462
  68.6 0.1 collective-permute-start.10
  68.7 5.8 %shard_map.146 = f32[6,2,8,1024]{3,2,1,0:T(8,128)S(1)} custom-call(s32[32]{0:T(128)} %refs_0_.9, f32[32]{0:T(128)} %refs_1_.17, f32[32]{0:T(128)} %refs_2_.13, f32[32]{0:T(128)} %refs_3_.13, f32[4,2,8,1024]{3,2,1,0:T(8,128)S(1)} %get-tuple-element.33.refs_6_.refs_2_.refs_3_.refs_4_, f32[2,8,1024]{2,1,0:T(8,128)S(1)} %get-tuple-element.40.refs_6_.refs_8_.refs_5_, ...), custom_call_target="tpu_custom_call" | custom-call | flops 6000 | bytes 6000 | tf_op jit(solution)/shard_map/pallas_call | solution.py:462
  74.6 0.6 collective-permute-start.13
  75.1 0.0 collective-permute-done.10
  75.2 2.1 %collective-permute-start.11 = (f32[9,8,512]{2,1,0:T(8,128)S(1)}, f32[9,8,512]{2,1,0:T(8,128)S(1)}, u32[]{:S(2)}, u32[]{:S(2)}) collective-permute-start(f32[9,8,512]{2,1,0:T(8,128)S(1)} %select_add_fusion), channel_id=1, source_target_pairs={{0,2},{1,3},{2,0},{3,1},{4,6},{5,7},{6,4},{7,5},{8,10},{9,11},{10,... | collective-permute-start | bytes 442376 | tf_op jit(solution)/shard_map/ppermute | solution.py:478
  77.3 5.3 %collective-permute-done.11 = f32[9,8,512]{2,1,0:T(8,128)S(1)} collective-permute-done((f32[9,8,512]{2,1,0:T(8,128)S(1)}, f32[9,8,512]{2,1,0:T(8,128)S(1)}, u32[]{:S(2)}, u32[]{:S(2)}) %collective-permute-start.11) | collective-permute-done | bytes 147488 | tf_op jit(solution)/shard_map/ppermute | solution.py:478
  82.6 0.1 collective-permute-start.12
  82.7 0.0 collective-permute-done.13
  82.7 1.3 %collective-permute-done.12 = f32[9,8,512]{2,1,0:T(8,128)S(1)} collective-permute-done((f32[9,8,512]{2,1,0:T(8,128)S(1)}, f32[9,8,512]{2,1,0:T(8,128)S(1)}, u32[]{:S(2)}, u32[]{:S(2)}) %collective-permute-start.12) | collective-permute-done | bytes 147488 | tf_op jit(solution)/shard_map/ppermute | solution.py:478
  84.1 2.1 %collective-permute-start.14 = (f32[3,2,8,256]{3,2,1,0:T(8,128)S(1)}, f32[3,2,8,256]{3,2,1,0:T(8,128)S(1)}, u32[]{:S(2)}, u32[]{:S(2)}) collective-permute-start(f32[3,2,8,256]{3,2,1,0:T(8,128)S(1)} %select_bitcast_fusion.4), channel_id=1, source_target_pairs={{0,2},{1,3},{2,0},{3,1},{4,6},{5,7},{6,4},{7,5},{8,10},{9,11},{10,... | collective-permute-start | bytes 147464 | tf_op jit(solution)/shard_map/ppermute | solution.py:478
  86.2 2.4 %shard_map.145 = f32[32,2,8,1024]{3,2,1,0:T(8,128)} custom-call(s32[32]{0:T(128)} %refs_0_.9, f32[32]{0:T(128)} %refs_1_.17, f32[32]{0:T(128)} %refs_2_.13, f32[32]{0:T(128)} %refs_3_.12, f32[32]{0:T(128)} %refs_3_.13, f32[9,8,1024]{2,1,0:T(8,128)S(1)} %maximum_select_fusion.refs_5_, f32[4,2,8,1024]{3,2,1,0:T(8,128)S(1)} %get-tuple-element.33.refs_6_.refs_2_.refs_3_.refs_4_, ...), custom_call_target="tpu_custom_call" | custom-call | flops 3000 | bytes 3000 | tf_op jit(solution)/shard_map/pallas_call | solution.py:462
  88.6 1.2 %collective-permute-done.14 = f32[3,2,8,256]{3,2,1,0:T(8,128)S(1)} collective-permute-done((f32[3,2,8,256]{3,2,1,0:T(8,128)S(1)}, f32[3,2,8,256]{3,2,1,0:T(8,128)S(1)}, u32[]{:S(2)}, u32[]{:S(2)}) %collective-permute-start.14) | collective-permute-done | bytes 49184 | tf_op jit(solution)/shard_map/ppermute | solution.py:478
  89.8 0.6 slice_bitcast_fusion
  (20 shorter events, 0.3 us)
Async XLA Ops:
  2.6 50.8 %collective-permute-start.2 = (f32[36,4,1024]{2,1,0:T(4,128)S(1)}, f32[36,4,1024]{2,1,0:T(4,128)S(1)}, u32[]{:S(2)}, u32[]{:S(2)}) collective-permute-start(f32[36,4,1024]{2,1,0:T(4,128)S(1)} %get-tuple-element.35), channel_id=1, source_target_pairs={{0,4},{4,0},{8,12},{12,8},{16,20},{20,16},{24,28},{28,24},{32,36},... | collective-permute-start | bytes 1769480 | tf_op jit(solution)/shard_map/ppermute | solution.py:505
  4.6 48.8 %collective-permute-start.3 = (f32[36,4,1024]{2,1,0:T(4,128)S(1)}, f32[36,4,1024]{2,1,0:T(4,128)S(1)}, u32[]{:S(2)}, u32[]{:S(2)}) collective-permute-start(f32[36,4,1024]{2,1,0:T(4,128)S(1)} %get-tuple-element.36), channel_id=1, source_target_pairs={{4,8},{8,4},{12,16},{16,12},{20,24},{24,20},{28,32},{32,28},{36,40... | collective-permute-start | bytes 1769480 | tf_op jit(solution)/shard_map/ppermute | solution.py:509
  12.8 6.7 %collective-permute-start = (f32[2,8,1024]{2,1,0:T(8,128)S(1)}, f32[2,8,1024]{2,1,0:T(8,128)S(1)}, u32[]{:S(2)}, u32[]{:S(2)}) collective-permute-start(f32[2,8,1024]{2,1,0:T(8,128)S(1)} %get-tuple-element.32), channel_id=1, source_target_pairs={{0,1},{1,0},{2,3},{3,2},{4,5},{5,4},{6,7},{7,6},{8,9},{9,8},{10,11... | collective-permute-start | bytes 196616 | tf_op jit(solution)/shard_map/ppermute | solution.py:478
  15.5 46.3 %collective-permute-start.8 = (f32[32,4,1024]{2,1,0:T(4,128)}, f32[32,4,1024]{2,1,0:T(4,128)S(1)}, u32[]{:S(2)}, u32[]{:S(2)}) collective-permute-start(f32[32,4,1024]{2,1,0:T(4,128)} %get-tuple-element.44), channel_id=1, source_target_pairs={{0,4},{4,0},{8,12},{12,8},{16,20},{20,16},{24,28},{28,24},{32,36},... | collective-permute-start | bytes 1572872 | tf_op jit(solution)/shard_map/ppermute | solution.py:505
  15.6 46.2 %collective-permute-start.9 = (f32[32,4,1024]{2,1,0:T(4,128)}, f32[32,4,1024]{2,1,0:T(4,128)S(1)}, u32[]{:S(2)}, u32[]{:S(2)}) collective-permute-start(f32[32,4,1024]{2,1,0:T(4,128)} %get-tuple-element.45), channel_id=1, source_target_pairs={{4,8},{8,4},{12,16},{16,12},{20,24},{24,20},{28,32},{32,28},{36,40... | collective-permute-start | bytes 1572872 | tf_op jit(solution)/shard_map/ppermute | solution.py:509
  19.5 20.3 %collective-permute-start.1 = (f32[2,8,1024]{2,1,0:T(8,128)S(1)}, f32[2,8,1024]{2,1,0:T(8,128)S(1)}, u32[]{:S(2)}, u32[]{:S(2)}) collective-permute-start(f32[2,8,1024]{2,1,0:T(8,128)S(1)} %add.27), channel_id=1, source_target_pairs={{0,2},{1,3},{2,0},{3,1},{4,6},{5,7},{6,4},{7,5},{8,10},{9,11},{10,... | collective-permute-start | bytes 196616 | tf_op jit(solution)/shard_map/ppermute | solution.py:478
  39.8 3.8 %collective-permute-start.4 = (f32[4,1024]{1,0:T(4,128)S(1)}, f32[4,1024]{1,0:T(4,128)S(1)}, u32[]{:S(2)}, u32[]{:S(2)}) collective-permute-start(f32[4,1024]{1,0:T(4,128)S(1)} %select_n.92), channel_id=1, source_target_pairs={{0,4},{4,0},{8,12},{12,8},{16,20},{20,16},{24,28},{28,24},{32,36},... | collective-permute-start | bytes 49160 | tf_op jit(solution)/shard_map/ppermute | solution.py:505
  43.7 9.7 %collective-permute-start.5 = (f32[4,1024]{1,0:T(4,128)S(1)}, f32[4,1024]{1,0:T(4,128)S(1)}, u32[]{:S(2)}, u32[]{:S(2)}) collective-permute-start(f32[4,1024]{1,0:T(4,128)S(1)} %select_n.94), channel_id=1, source_target_pairs={{4,8},{8,4},{12,16},{16,12},{20,24},{24,20},{28,32},{32,28},{36,40... | collective-permute-start | bytes 49160 | tf_op jit(solution)/shard_map/ppermute | solution.py:509
  55.7 1.4 %collective-permute-start.6 = (f32[3,8,1024]{2,1,0:T(8,128)S(1)}, f32[3,8,1024]{2,1,0:T(8,128)S(1)}, u32[]{:S(2)}, u32[]{:S(2)}) collective-permute-start(f32[3,8,1024]{2,1,0:T(8,128)S(1)} %get-tuple-element.41), channel_id=1, source_target_pairs={{0,1},{1,0},{2,3},{3,2},{4,5},{5,4},{6,7},{7,6},{8,9},{9,8},{10,11... | collective-permute-start | bytes 294920 | tf_op jit(solution)/shard_map/ppermute | solution.py:478
  57.1 6.7 %collective-permute-start.7 = (f32[3,8,1024]{2,1,0:T(8,128)S(1)}, f32[3,8,1024]{2,1,0:T(8,128)S(1)}, u32[]{:S(2)}, u32[]{:S(2)}) collective-permute-start(f32[3,8,1024]{2,1,0:T(8,128)S(1)} %add.29), channel_id=1, source_target_pairs={{0,2},{1,3},{2,0},{3,1},{4,6},{5,7},{6,4},{7,5},{8,10},{9,11},{10,... | collective-permute-start | bytes 294920 | tf_op jit(solution)/shard_map/ppermute | solution.py:478
  68.6 6.6 %collective-permute-start.10 = (f32[9,8,512]{2,1,0:T(8,128)S(1)}, f32[9,8,512]{2,1,0:T(8,128)S(1)}, u32[]{:S(2)}, u32[]{:S(2)}) collective-permute-start(f32[9,8,512]{2,1,0:T(8,128)S(1)} %slice_select_fusion), channel_id=1, source_target_pairs={{0,1},{1,0},{2,3},{3,2},{4,5},{5,4},{6,7},{7,6},{8,9},{9,8},{10,11... | collective-permute-start | bytes 442376 | tf_op jit(solution)/shard_map/ppermute | solution.py:478
  74.6 8.1 %collective-permute-start.13 = (f32[2,6,2,8,256]{4,3,2,1,0:T(8,128)S(1)}, f32[2,6,2,8,256]{4,3,2,1,0:T(8,128)S(1)}, u32[]{:S(2)}, u32[]{:S(2)}) collective-permute-start(f32[2,6,2,8,256]{4,3,2,1,0:T(8,128)S(1)} %pad_maximum_fusion), channel_id=1, source_target_pairs={{0,1},{1,0},{2,3},{3,2},{4,5},{5,4},{6,7},{7,6},{8,9},{9,8},{10,11... | collective-permute-start | bytes 589832 | tf_op jit(solution)/shard_map/ppermute | solution.py:478
  75.2 7.4 %collective-permute-start.11 = (f32[9,8,512]{2,1,0:T(8,128)S(1)}, f32[9,8,512]{2,1,0:T(8,128)S(1)}, u32[]{:S(2)}, u32[]{:S(2)}) collective-permute-start(f32[9,8,512]{2,1,0:T(8,128)S(1)} %select_add_fusion), channel_id=1, source_target_pairs={{0,2},{1,3},{2,0},{3,1},{4,6},{5,7},{6,4},{7,5},{8,10},{9,11},{10,... | collective-permute-start | bytes 442376 | tf_op jit(solution)/shard_map/ppermute | solution.py:478
  82.6 1.5 %collective-permute-start.12 = (f32[9,8,512]{2,1,0:T(8,128)S(1)}, f32[9,8,512]{2,1,0:T(8,128)S(1)}, u32[]{:S(2)}, u32[]{:S(2)}) collective-permute-start(f32[9,8,512]{2,1,0:T(8,128)S(1)} %add.32), channel_id=1, source_target_pairs={{0,1},{1,0},{2,3},{3,2},{4,5},{5,4},{6,7},{7,6},{8,9},{9,8},{10,11... | collective-permute-start | bytes 442376 | tf_op jit(solution)/shard_map/ppermute | solution.py:478
  84.1 5.7 %collective-permute-start.14 = (f32[3,2,8,256]{3,2,1,0:T(8,128)S(1)}, f32[3,2,8,256]{3,2,1,0:T(8,128)S(1)}, u32[]{:S(2)}, u32[]{:S(2)}) collective-permute-start(f32[3,2,8,256]{3,2,1,0:T(8,128)S(1)} %select_bitcast_fusion.4), channel_id=1, source_target_pairs={{0,2},{1,3},{2,0},{3,1},{4,6},{5,7},{6,4},{7,5},{8,10},{9,11},{10,... | collective-permute-start | bytes 147464 | tf_op jit(solution)/shard_map/ppermute | solution.py:478

commit v5 on v4

--- a/solution.py
+++ b/solution.py
@@ -277,7 +277,7 @@
 
 
 def backward_kernel(age, mort, crowding, speed, fields, halo_fields, crowd, crowd_two, sums, pulled, pulled_both, state,
-                    state_both, start, partial, totals, coef):
+                    state_both, start, partial, totals, value_out, faded_out, faded_halo, coef):
     pressure, later = totals.at[0:3], totals.at[3:5]
 
     def begin():
@@ -297,7 +297,13 @@
             grad, now = whole_tiles(pulled, pulled_both, c), whole_tiles(state, state_both, c)
             value = []
             for k in range(3):
-                value.append(grad[k] * decays(mortal, crowded, crowd_two[k]))
+                fade = decays(mortal, crowded, crowd_two[k])
+                value.append(grad[k] * fade)
+                if k < 2:
+                    value_out[c, k] = value[k]
+                    faded_out[c, k] = now[k] * fade
+                else:
+                    faded_halo[c] = now[k] * fade
                 pressure[k] -= crowded * (value[k] * now[k])
             plain = [coef[1, k] * value[k] for k in range(3)]
             along = [swim * (coef[3, k] * value[k]) for k in range(3)]
@@ -314,8 +320,8 @@
     return begin, each, nothing
 
 
-def shares_kernel(age, mort, crowding, speed, fields, crowd, crowd_two, sums, halo_sums, pulled, pulled_both, wet_halo, state,
-                  state_both, cotangent, start, shares):
+def shares_kernel(age, mort, crowding, speed, fields, crowd, sums, halo_sums, value, faded, faded_halo, wet_halo,
+                  cotangent, start, shares):
     def begin():
         clear(shares)
         plain, swum = [[sums[n, 0], sums[n, 1], halo_sums[n]] for n in range(2)]
@@ -332,10 +338,8 @@
         for c in group:
             mortal, crowded, swim = [table[age[c]] for table in (mort, crowding, speed)]
             old = [start[c, k] * decays(mortal, crowded, crowd[k]) for k in range(2)] + [wet_halo[c]]
-            fade = [decays(mortal, crowded, crowd_two[k]) for k in range(3)]
-            new = [tile * fade[k] for k, tile in enumerate(whole_tiles(state, state_both, c))]
-            grad = whole_tiles(pulled, pulled_both, c)
-            for wet, weigh in ((old, lambda k: grad[k] * fade[k]), (new, lambda k: fields[0, k] * cotangent[c, k])):
+            new = [faded[c, 0], faded[c, 1], faded_halo[c]]
+            for wet, weigh in ((old, lambda k: value[c, k]), (new, lambda k: fields[0, k] * cotangent[c, k])):
                 north, south = northern(*wet), southern(*wet)
                 for k in range(2):
                     by = weigh(k)
@@ -550,11 +554,11 @@
         [], [halo], [halo_fields_shape, (3, height, lon), (STEP, height, lon)], 2500, sides=(4,))
 
     tables = [age_class, mort_rate, crowd_coef, speed]
-    partial, totals = call("backward", backward_kernel, cohorts, tables, [fields, halo_fields, crowd, crowd_two, sums, pulled, pulled_both, state, state_both],
-        [density], [], [main, (9, height, lon)], [fields_shape], 5000)
+    partial, totals, value, faded, faded_halo = call("backward", backward_kernel, cohorts, tables, [fields, halo_fields, crowd, crowd_two, sums, pulled, pulled_both, state, state_both],
+        [density], [], [main, (9, height, lon), main, main, halo], [fields_shape], 5000)
     totals = total_by_halves(totals, lower)
 
-    (shares,) = call("shares", shares_kernel, cohorts, tables, [fields, crowd, crowd_two, sums, halo_sums, pulled, pulled_both, wet_halo, state, state_both],
+    (shares,) = call("shares", shares_kernel, cohorts, tables, [fields, crowd, sums, halo_sums, value, faded, faded_halo, wet_halo],
         [cotangent, density], [], [(6,) + tiles], [], 6000)
     keep, send = own_quarters(shares, lower)
     keep = keep + swap(send, 1)

time: 91.4 us -> 90.4 us (0.989)
  Pallas kernels: 29.1 us -> 28.1 us
    pallas_call x9, Pallas kernels: 29.1 us -> 28.1 us  [call(): pl.pallas_call(functools.partial(driver, kernel, cohorts, sides, len(tabl...]
  transfers between devices with their start and end apart: 15 -> 15, of which waited for: 6 -> 6; matrix products, arithmetic and copies ran while one was open for 0% -> 0% of each run, Pallas kernels for 25% -> 24%
where the time goes in v5:
time: 90.4 us; the launch traced here: 89.5 us
  waiting for transfers between devices  30.1 us (33%)
  starting transfers between devices  29.3 us (32%)
  Pallas kernels  28.1 us (31%)
  between operations  0.98 us (1%)
    pallas_call x9, Pallas kernels, call(): pl.pallas_call(functools.partial(driver, kernel, cohorts, sides, len(tabl...  28.1 us
    ppermute x9, waiting for transfers between devices, swap(): return lax.ppermute(value, 'coh', [(i, i ^ flip) for i in range(4)])  26.4 us
    ppermute x3, starting transfers between devices, far_swap(): lax.ppermute(value, 'lat', [(i, (i + 1 ^ 1) - 1) for i in range(1, count...  17.4 us
    ppermute x9, starting transfers between devices, swap(): return lax.ppermute(value, 'coh', [(i, i ^ flip) for i in range(4)])  9.71 us
    ppermute x3, waiting for transfers between devices, near_swap(): return lax.ppermute(value, 'lat', [(i, i ^ 1) for i in range(count)])  3.71 us
    ppermute x3, starting transfers between devices, near_swap(): return lax.ppermute(value, 'lat', [(i, i ^ 1) for i in range(count)])  2.18 us
  transfers between devices with their start and end apart: 15, of which 6 were waited for; matrix products, arithmetic and copies ran while one was open for 0% of the time, Pallas kernels for 24%

profile of v5, /device:TPU:6, one launch (start us, length us, event | category | flops | bytes accessed | tf_op | source)
XLA Modules:
  0.0 89.5 jit_solution(10875092488802277974)
XLA Ops:
  0.6 2.0 %shard_map.138 = (f32[36,4,1024]{2,1,0:T(4,128)S(1)}, f32[36,4,1024]{2,1,0:T(4,128)S(1)}, f32[2,8,1024]{2,1,0:T(8,128)S(1)}) custom-call(s32[1]{0:T(128)} %bitcast.refs_0_, s32[32]{0:T(128)} %refs_0_.9, f32[32]{0:T(128)} %refs_3_.12, s32[2,8,1024]{2,1,0:T(8,128)} %refs_5_.4, f32[2,8,1024]{2,1,0:T(8,128)} %refs_6_.3, f32[2,8,1024]{2,1,0:T(8,128)} %refs_7_.2, ...), custom_call_target="tpu_custom_call" | custom-call | flops 2000 | bytes 2000 | tf_op jit(solution)/shard_map/pallas_call | solution.py:466
  2.6 2.0 %collective-permute-start.2 = (f32[36,4,1024]{2,1,0:T(4,128)S(1)}, f32[36,4,1024]{2,1,0:T(4,128)S(1)}, u32[]{:S(2)}, u32[]{:S(2)}) collective-permute-start(f32[36,4,1024]{2,1,0:T(4,128)S(1)} %get-tuple-element.38), channel_id=1, source_target_pairs={{0,4},{4,0},{8,12},{12,8},{16,20},{20,16},{24,28},{28,24},{32,36},... | collective-permute-start | bytes 1769480 | tf_op jit(solution)/shard_map/ppermute | solution.py:509
  4.6 8.1 %collective-permute-start.3 = (f32[36,4,1024]{2,1,0:T(4,128)S(1)}, f32[36,4,1024]{2,1,0:T(4,128)S(1)}, u32[]{:S(2)}, u32[]{:S(2)}) collective-permute-start(f32[36,4,1024]{2,1,0:T(4,128)S(1)} %get-tuple-element.39), channel_id=1, source_target_pairs={{4,8},{8,4},{12,16},{16,12},{20,24},{24,20},{28,32},{32,28},{36,40... | collective-permute-start | bytes 1769480 | tf_op jit(solution)/shard_map/ppermute | solution.py:513
  12.8 0.1 collective-permute-start
  12.9 2.6 %shard_map.142 = (f32[32,4,1024]{2,1,0:T(4,128)}, f32[32,4,1024]{2,1,0:T(4,128)}) custom-call(s32[1]{0:T(128)} %bitcast.refs_0_, f32[32,2,8,1024]{3,2,1,0:T(8,128)} %refs_12_.1), custom_call_target="tpu_custom_call" | custom-call | flops 2000 | bytes 2000 | tf_op jit(solution)/shard_map/pallas_call | solution.py:466
  15.5 0.1 collective-permute-start.8
  15.6 3.9 %collective-permute-start.9 = (f32[32,4,1024]{2,1,0:T(4,128)}, f32[32,4,1024]{2,1,0:T(4,128)S(1)}, u32[]{:S(2)}, u32[]{:S(2)}) collective-permute-start(f32[32,4,1024]{2,1,0:T(4,128)} %get-tuple-element.48), channel_id=1, source_target_pairs={{4,8},{8,4},{12,16},{16,12},{20,24},{24,20},{28,32},{32,28},{36,40... | collective-permute-start | bytes 1572872 | tf_op jit(solution)/shard_map/ppermute | solution.py:513
  19.5 0.0 collective-permute-done
  19.5 3.0 %collective-permute-start.1 = (f32[2,8,1024]{2,1,0:T(8,128)S(1)}, f32[2,8,1024]{2,1,0:T(8,128)S(1)}, u32[]{:S(2)}, u32[]{:S(2)}) collective-permute-start(f32[2,8,1024]{2,1,0:T(8,128)S(1)} %add.27), channel_id=1, source_target_pairs={{0,2},{1,3},{2,0},{3,1},{4,6},{5,7},{6,4},{7,5},{8,10},{9,11},{10,... | collective-permute-start | bytes 196616 | tf_op jit(solution)/shard_map/ppermute | solution.py:482
  22.5 17.3 %collective-permute-done.1 = f32[2,8,1024]{2,1,0:T(8,128)S(1)} collective-permute-done((f32[2,8,1024]{2,1,0:T(8,128)S(1)}, f32[2,8,1024]{2,1,0:T(8,128)S(1)}, u32[]{:S(2)}, u32[]{:S(2)}) %collective-permute-start.1) | collective-permute-done | bytes 65568 | tf_op jit(solution)/shard_map/ppermute | solution.py:482
  39.8 0.1 collective-permute-start.4
  40.0 3.7 %collective-permute-done.4.refs_10_ = f32[4,1024]{1,0:T(4,128)S(1)} collective-permute-done((f32[4,1024]{1,0:T(4,128)S(1)}, f32[4,1024]{1,0:T(4,128)S(1)}, u32[]{:S(2)}, u32[]{:S(2)}) %collective-permute-start.4) | collective-permute-done | bytes 16416 | tf_op jit(solution)/shard_map/ppermute | solution.py:509
  43.7 5.4 %collective-permute-start.5 = (f32[4,1024]{1,0:T(4,128)S(1)}, f32[4,1024]{1,0:T(4,128)S(1)}, u32[]{:S(2)}, u32[]{:S(2)}) collective-permute-start(f32[4,1024]{1,0:T(4,128)S(1)} %select_n.94), channel_id=1, source_target_pairs={{4,8},{8,4},{12,16},{16,12},{20,24},{24,20},{28,32},{32,28},{36,40... | collective-permute-start | bytes 49160 | tf_op jit(solution)/shard_map/ppermute | solution.py:513
  49.1 4.2 %shard_map.139 = (f32[32,2,8,1024]{3,2,1,0:T(8,128)S(1)}, f32[32,8,1024]{2,1,0:T(8,128)S(1)}, f32[4,2,8,1024]{3,2,1,0:T(8,128)S(1)}, f32[2,8,1024]{2,1,0:T(8,128...) custom-call(s32[32]{0:T(128)} %refs_0_.9, f32[32]{0:T(128)} %refs_1_.17, f32[32]{0:T(128)} %refs_2_.13, ...), custom_call_target="tpu_custom_call" | custom-call | flops 4000 | bytes 4000 | tf_op jit(solution)/shard_map/pallas_call | solution.py:466
  53.3 0.0 collective-permute-done.5.refs_11_
  53.3 0.0 collective-permute-done.2.refs_8_
  53.3 0.0 collective-permute-done.3.refs_9_
  53.3 2.3 %shard_map.140 = (f32[32,8,1024]{2,1,0:T(8,128)S(1)}, f32[32,8,1024]{2,1,0:T(8,128)S(1)}, f32[4,8,1024]{2,1,0:T(8,128)S(1)}, f32[3,8,1024]{2,1,0:T(8,128)S(1)}, f32[2,8,1024]{2,1,0:T(8,128)S(1)}) custom-call(s32[1]{0:T(128)} %bitcast.refs_0_, s32[32]{0:T(128)} %refs_0_.9, f32[32]{0:T(128)} %refs_1_.17, f32[32]{0:T(128)} %refs_2_.13, f32[32]{0:T(128)} %refs_3_.12, ...), custom_call_target="tpu_custom_call" | custom-call | flops 2500 | bytes 2500 | tf_op jit(solution)/shard_map/pallas_call | solution.py:466
  55.6 0.1 collective-permute-start.6
  55.7 1.3 %collective-permute-done.6 = f32[3,8,1024]{2,1,0:T(8,128)S(1)} collective-permute-done((f32[3,8,1024]{2,1,0:T(8,128)S(1)}, f32[3,8,1024]{2,1,0:T(8,128)S(1)}, u32[]{:S(2)}, u32[]{:S(2)}) %collective-permute-start.6) | collective-permute-done | bytes 98336 | tf_op jit(solution)/shard_map/ppermute | solution.py:482
  57.0 1.6 %collective-permute-start.7 = (f32[3,8,1024]{2,1,0:T(8,128)S(1)}, f32[3,8,1024]{2,1,0:T(8,128)S(1)}, u32[]{:S(2)}, u32[]{:S(2)}) collective-permute-start(f32[3,8,1024]{2,1,0:T(8,128)S(1)} %add.29), channel_id=1, source_target_pairs={{0,2},{1,3},{2,0},{3,1},{4,6},{5,7},{6,4},{7,5},{8,10},{9,11},{10,... | collective-permute-start | bytes 294920 | tf_op jit(solution)/shard_map/ppermute | solution.py:482
  58.7 3.0 %shard_map.141 = (f32[32,2,8,1024]{3,2,1,0:T(8,128)S(1)}, f32[32,8,1024]{2,1,0:T(8,128)S(1)}) custom-call(s32[32]{0:T(128)} %refs_0_.9, f32[32]{0:T(128)} %refs_3_.13, f32[4,2,8,1024]{3,2,1,0:T(8,128)S(1)} %get-tuple-element.36.refs_6_.refs_2_.refs_3_.refs_4_, f32[32,2,8,1024]{3,2,1,0:T(8,128)} %refs_12_.1), custom_call_target="tpu_custom_call" | custom-call | flops 4000 | bytes 4000 | tf_op jit(solution)/shard_map/pallas_call | solution.py:466
  61.6 0.0 collective-permute-done.8.refs_5_
  61.6 0.0 collective-permute-done.9.refs_6_
  61.7 2.1 %shard_map.143.refs_10_ = f32[32,8,1024]{2,1,0:T(8,128)S(1)} custom-call(s32[1]{0:T(128)} %bitcast.refs_0_, s32[32]{0:T(128)} %refs_0_.9, f32[32]{0:T(128)} %refs_3_.13, f32[4,2,8,1024]{3,2,1,0:T(8,128)S(1)} %get-tuple-element.36.refs_6_.refs_2_.refs_3_.refs_4_, f32[4,8,1024]{2,1,0:T(8,128)S(1)} %get-tuple-element.42.refs_4_.refs_5_.refs_7_, ...), custom_call_target="tpu_custom_call" | custom-call | flops 2500 | bytes 2500 | tf_op jit(solution)/shard_map/pallas_call | solution.py:466
  63.7 0.0 collective-permute-done.7
  63.8 4.8 %shard_map.144 = (f32[32,2,8,1024]{3,2,1,0:T(8,128)S(1)}, f32[9,8,1024]{2,1,0:T(8,128)S(1)}, f32[32,2,8,1024]{3,2,1,0:T(8,128)S(1)}, f32[32,2,8,1024]{3,2,1,0:T(8,128)S(1)}, f32[32,8,1024]{2,1,0:T(8,128)S(1)}) custom-call(s32[32]{0:T(128)} %refs_0_.9, f32[32]{0:T(128)} %refs_1_.17, f32[32]{0:T(128)} %refs_2_.13, f32[32]{0:T(128)} %refs_3_.13, ...), custom_call_target="tpu_custom_call" | custom-call | flops 5000 | bytes 5000 | tf_op jit(solution)/shard_map/pallas_call | solution.py:466
  68.6 0.1 collective-permute-start.10
  68.7 4.8 %shard_map.146 = f32[6,2,8,1024]{3,2,1,0:T(8,128)S(1)} custom-call(s32[32]{0:T(128)} %refs_0_.9, f32[32]{0:T(128)} %refs_1_.17, f32[32]{0:T(128)} %refs_2_.13, f32[32]{0:T(128)} %refs_3_.13, f32[4,2,8,1024]{3,2,1,0:T(8,128)S(1)} %get-tuple-element.36.refs_6_.refs_2_.refs_3_.refs_4_, f32[2,8,1024]{2,1,0:T(8,128)S(1)} %get-tuple-element.43.refs_6_.refs_8_.refs_5_, ...), custom_call_target="tpu_custom_call" | custom-call | flops 6000 | bytes 6000 | tf_op jit(solution)/shard_map/pallas_call | solution.py:466
  73.6 0.6 collective-permute-start.13
  74.1 0.0 collective-permute-done.10
  74.2 2.1 %collective-permute-start.11 = (f32[9,8,512]{2,1,0:T(8,128)S(1)}, f32[9,8,512]{2,1,0:T(8,128)S(1)}, u32[]{:S(2)}, u32[]{:S(2)}) collective-permute-start(f32[9,8,512]{2,1,0:T(8,128)S(1)} %select_add_fusion), channel_id=1, source_target_pairs={{0,2},{1,3},{2,0},{3,1},{4,6},{5,7},{6,4},{7,5},{8,10},{9,11},{10,... | collective-permute-start | bytes 442376 | tf_op jit(solution)/shard_map/ppermute | solution.py:482
  76.2 5.3 %collective-permute-done.11 = f32[9,8,512]{2,1,0:T(8,128)S(1)} collective-permute-done((f32[9,8,512]{2,1,0:T(8,128)S(1)}, f32[9,8,512]{2,1,0:T(8,128)S(1)}, u32[]{:S(2)}, u32[]{:S(2)}) %collective-permute-start.11) | collective-permute-done | bytes 147488 | tf_op jit(solution)/shard_map/ppermute | solution.py:482
  81.6 0.1 collective-permute-start.12
  81.7 0.0 collective-permute-done.13
  81.7 1.3 %collective-permute-done.12 = f32[9,8,512]{2,1,0:T(8,128)S(1)} collective-permute-done((f32[9,8,512]{2,1,0:T(8,128)S(1)}, f32[9,8,512]{2,1,0:T(8,128)S(1)}, u32[]{:S(2)}, u32[]{:S(2)}) %collective-permute-start.12) | collective-permute-done | bytes 147488 | tf_op jit(solution)/shard_map/ppermute | solution.py:482
  83.1 2.1 %collective-permute-start.14 = (f32[3,2,8,256]{3,2,1,0:T(8,128)S(1)}, f32[3,2,8,256]{3,2,1,0:T(8,128)S(1)}, u32[]{:S(2)}, u32[]{:S(2)}) collective-permute-start(f32[3,2,8,256]{3,2,1,0:T(8,128)S(1)} %select_bitcast_fusion.4), channel_id=1, source_target_pairs={{0,2},{1,3},{2,0},{3,1},{4,6},{5,7},{6,4},{7,5},{8,10},{9,11},{10,... | collective-permute-start | bytes 147464 | tf_op jit(solution)/shard_map/ppermute | solution.py:482
  85.2 2.4 %shard_map.145 = f32[32,2,8,1024]{3,2,1,0:T(8,128)} custom-call(s32[32]{0:T(128)} %refs_0_.9, f32[32]{0:T(128)} %refs_1_.17, f32[32]{0:T(128)} %refs_2_.13, f32[32]{0:T(128)} %refs_3_.12, f32[32]{0:T(128)} %refs_3_.13, f32[9,8,1024]{2,1,0:T(8,128)S(1)} %maximum_select_fusion.refs_5_, f32[4,2,8,1024]{3,2,1,0:T(8,128)S(1)} %get-tuple-element.36.refs_6_.refs_2_.refs_3_.refs_4_, ...), custom_call_target="tpu_custom_call" | custom-call | flops 3000 | bytes 3000 | tf_op jit(solution)/shard_map/pallas_call | solution.py:466
  87.6 1.2 %collective-permute-done.14 = f32[3,2,8,256]{3,2,1,0:T(8,128)S(1)} collective-permute-done((f32[3,2,8,256]{3,2,1,0:T(8,128)S(1)}, f32[3,2,8,256]{3,2,1,0:T(8,128)S(1)}, u32[]{:S(2)}, u32[]{:S(2)}) %collective-permute-start.14) | collective-permute-done | bytes 49184 | tf_op jit(solution)/shard_map/ppermute | solution.py:482
  88.8 0.6 slice_bitcast_fusion
  (20 shorter events, 0.3 us)
Async XLA Ops:
  2.6 50.7 %collective-permute-start.2 = (f32[36,4,1024]{2,1,0:T(4,128)S(1)}, f32[36,4,1024]{2,1,0:T(4,128)S(1)}, u32[]{:S(2)}, u32[]{:S(2)}) collective-permute-start(f32[36,4,1024]{2,1,0:T(4,128)S(1)} %get-tuple-element.38), channel_id=1, source_target_pairs={{0,4},{4,0},{8,12},{12,8},{16,20},{20,16},{24,28},{28,24},{32,36},... | collective-permute-start | bytes 1769480 | tf_op jit(solution)/shard_map/ppermute | solution.py:509
  4.6 48.7 %collective-permute-start.3 = (f32[36,4,1024]{2,1,0:T(4,128)S(1)}, f32[36,4,1024]{2,1,0:T(4,128)S(1)}, u32[]{:S(2)}, u32[]{:S(2)}) collective-permute-start(f32[36,4,1024]{2,1,0:T(4,128)S(1)} %get-tuple-element.39), channel_id=1, source_target_pairs={{4,8},{8,4},{12,16},{16,12},{20,24},{24,20},{28,32},{32,28},{36,40... | collective-permute-start | bytes 1769480 | tf_op jit(solution)/shard_map/ppermute | solution.py:513
  12.8 6.7 %collective-permute-start = (f32[2,8,1024]{2,1,0:T(8,128)S(1)}, f32[2,8,1024]{2,1,0:T(8,128)S(1)}, u32[]{:S(2)}, u32[]{:S(2)}) collective-permute-start(f32[2,8,1024]{2,1,0:T(8,128)S(1)} %get-tuple-element.35), channel_id=1, source_target_pairs={{0,1},{1,0},{2,3},{3,2},{4,5},{5,4},{6,7},{7,6},{8,9},{9,8},{10,11... | collective-permute-start | bytes 196616 | tf_op jit(solution)/shard_map/ppermute | solution.py:482
  15.5 46.1 %collective-permute-start.8 = (f32[32,4,1024]{2,1,0:T(4,128)}, f32[32,4,1024]{2,1,0:T(4,128)S(1)}, u32[]{:S(2)}, u32[]{:S(2)}) collective-permute-start(f32[32,4,1024]{2,1,0:T(4,128)} %get-tuple-element.47), channel_id=1, source_target_pairs={{0,4},{4,0},{8,12},{12,8},{16,20},{20,16},{24,28},{28,24},{32,36},... | collective-permute-start | bytes 1572872 | tf_op jit(solution)/shard_map/ppermute | solution.py:509
  15.6 46.1 %collective-permute-start.9 = (f32[32,4,1024]{2,1,0:T(4,128)}, f32[32,4,1024]{2,1,0:T(4,128)S(1)}, u32[]{:S(2)}, u32[]{:S(2)}) collective-permute-start(f32[32,4,1024]{2,1,0:T(4,128)} %get-tuple-element.48), channel_id=1, source_target_pairs={{4,8},{8,4},{12,16},{16,12},{20,24},{24,20},{28,32},{32,28},{36,40... | collective-permute-start | bytes 1572872 | tf_op jit(solution)/shard_map/ppermute | solution.py:513
  19.5 20.3 %collective-permute-start.1 = (f32[2,8,1024]{2,1,0:T(8,128)S(1)}, f32[2,8,1024]{2,1,0:T(8,128)S(1)}, u32[]{:S(2)}, u32[]{:S(2)}) collective-permute-start(f32[2,8,1024]{2,1,0:T(8,128)S(1)} %add.27), channel_id=1, source_target_pairs={{0,2},{1,3},{2,0},{3,1},{4,6},{5,7},{6,4},{7,5},{8,10},{9,11},{10,... | collective-permute-start | bytes 196616 | tf_op jit(solution)/shard_map/ppermute | solution.py:482
  39.8 3.8 %collective-permute-start.4 = (f32[4,1024]{1,0:T(4,128)S(1)}, f32[4,1024]{1,0:T(4,128)S(1)}, u32[]{:S(2)}, u32[]{:S(2)}) collective-permute-start(f32[4,1024]{1,0:T(4,128)S(1)} %select_n.92), channel_id=1, source_target_pairs={{0,4},{4,0},{8,12},{12,8},{16,20},{20,16},{24,28},{28,24},{32,36},... | collective-permute-start | bytes 49160 | tf_op jit(solution)/shard_map/ppermute | solution.py:509
  43.7 9.6 %collective-permute-start.5 = (f32[4,1024]{1,0:T(4,128)S(1)}, f32[4,1024]{1,0:T(4,128)S(1)}, u32[]{:S(2)}, u32[]{:S(2)}) collective-permute-start(f32[4,1024]{1,0:T(4,128)S(1)} %select_n.94), channel_id=1, source_target_pairs={{4,8},{8,4},{12,16},{16,12},{20,24},{24,20},{28,32},{32,28},{36,40... | collective-permute-start | bytes 49160 | tf_op jit(solution)/shard_map/ppermute | solution.py:513
  55.6 1.4 %collective-permute-start.6 = (f32[3,8,1024]{2,1,0:T(8,128)S(1)}, f32[3,8,1024]{2,1,0:T(8,128)S(1)}, u32[]{:S(2)}, u32[]{:S(2)}) collective-permute-start(f32[3,8,1024]{2,1,0:T(8,128)S(1)} %get-tuple-element.44), channel_id=1, source_target_pairs={{0,1},{1,0},{2,3},{3,2},{4,5},{5,4},{6,7},{7,6},{8,9},{9,8},{10,11... | collective-permute-start | bytes 294920 | tf_op jit(solution)/shard_map/ppermute | solution.py:482
  57.0 6.7 %collective-permute-start.7 = (f32[3,8,1024]{2,1,0:T(8,128)S(1)}, f32[3,8,1024]{2,1,0:T(8,128)S(1)}, u32[]{:S(2)}, u32[]{:S(2)}) collective-permute-start(f32[3,8,1024]{2,1,0:T(8,128)S(1)} %add.29), channel_id=1, source_target_pairs={{0,2},{1,3},{2,0},{3,1},{4,6},{5,7},{6,4},{7,5},{8,10},{9,11},{10,... | collective-permute-start | bytes 294920 | tf_op jit(solution)/shard_map/ppermute | solution.py:482
  68.6 5.5 %collective-permute-start.10 = (f32[9,8,512]{2,1,0:T(8,128)S(1)}, f32[9,8,512]{2,1,0:T(8,128)S(1)}, u32[]{:S(2)}, u32[]{:S(2)}) collective-permute-start(f32[9,8,512]{2,1,0:T(8,128)S(1)} %slice_select_fusion), channel_id=1, source_target_pairs={{0,1},{1,0},{2,3},{3,2},{4,5},{5,4},{6,7},{7,6},{8,9},{9,8},{10,11... | collective-permute-start | bytes 442376 | tf_op jit(solution)/shard_map/ppermute | solution.py:482
  73.6 8.1 %collective-permute-start.13 = (f32[2,6,2,8,256]{4,3,2,1,0:T(8,128)S(1)}, f32[2,6,2,8,256]{4,3,2,1,0:T(8,128)S(1)}, u32[]{:S(2)}, u32[]{:S(2)}) collective-permute-start(f32[2,6,2,8,256]{4,3,2,1,0:T(8,128)S(1)} %pad_maximum_fusion), channel_id=1, source_target_pairs={{0,1},{1,0},{2,3},{3,2},{4,5},{5,4},{6,7},{7,6},{8,9},{9,8},{10,11... | collective-permute-start | bytes 589832 | tf_op jit(solution)/shard_map/ppermute | solution.py:482
  74.2 7.4 %collective-permute-start.11 = (f32[9,8,512]{2,1,0:T(8,128)S(1)}, f32[9,8,512]{2,1,0:T(8,128)S(1)}, u32[]{:S(2)}, u32[]{:S(2)}) collective-permute-start(f32[9,8,512]{2,1,0:T(8,128)S(1)} %select_add_fusion), channel_id=1, source_target_pairs={{0,2},{1,3},{2,0},{3,1},{4,6},{5,7},{6,4},{7,5},{8,10},{9,11},{10,... | collective-permute-start | bytes 442376 | tf_op jit(solution)/shard_map/ppermute | solution.py:482
  81.6 1.5 %collective-permute-start.12 = (f32[9,8,512]{2,1,0:T(8,128)S(1)}, f32[9,8,512]{2,1,0:T(8,128)S(1)}, u32[]{:S(2)}, u32[]{:S(2)}) collective-permute-start(f32[9,8,512]{2,1,0:T(8,128)S(1)} %add.32), channel_id=1, source_target_pairs={{0,1},{1,0},{2,3},{3,2},{4,5},{5,4},{6,7},{7,6},{8,9},{9,8},{10,11... | collective-permute-start | bytes 442376 | tf_op jit(solution)/shard_map/ppermute | solution.py:482
  83.1 5.7 %collective-permute-start.14 = (f32[3,2,8,256]{3,2,1,0:T(8,128)S(1)}, f32[3,2,8,256]{3,2,1,0:T(8,128)S(1)}, u32[]{:S(2)}, u32[]{:S(2)}) collective-permute-start(f32[3,2,8,256]{3,2,1,0:T(8,128)S(1)} %select_bitcast_fusion.4), channel_id=1, source_target_pairs={{0,2},{1,3},{2,0},{3,1},{4,6},{5,7},{6,4},{7,5},{8,10},{9,11},{10,... | collective-permute-start | bytes 147464 | tf_op jit(solution)/shard_map/ppermute | solution.py:482
